TPU v7x, 32 devices: a whole 2x2x4 slice. The times are simulated.
32 devices in a mesh: grp: 2 (over x), lon: 16 (over z, y, core).
Axes of the slice: x: 2, y: 2, z: 4, core: 2. Of those that a mesh axis runs over, the one named last changes fastest.
Arguments:
- state: bfloat16 [256, 256, 300], P(None, ('grp', 'lon')), parts along dimension 1, may hold values from -6 to 6
- ocean_mask: int32 [256, 128], P(None, 'lon'), may hold values from 0 to 1, as said below
- fold_map: int32 [128], replicated, may hold values from 0 to 127, as said below
- w_first: bfloat16 [3, 3, 300, 256], replicated, may hold values from -0.125 to 0.125
- b_first: float32 [256], replicated, may hold values from -3 to 3
- w_second: bfloat16 [3, 3, 256, 256], replicated, may hold values from -0.125 to 0.125
- b_second: float32 [256], replicated, may hold values from -3 to 3
Outputs:
- features: bfloat16 [256, 256, 256], P(None, ('grp', 'lon')), parts along dimension 1
There are 2 independent parts, one for each index of `grp`. A program takes and returns all parts, laid end to end along the dimension named above; an argument that names none is the same for every part. Nothing has to cross between parts.
Inputs may be any that keep to these rules, and one draw needn't show every extreme that they name: `ocean_mask`: 1 marks ocean, 0 land; the ocean share varies from column to column. A reflection: (fold_map[i] + i) mod 128 is the same for every i.
All inputs are finite; a program needn't handle non-finite values.
Results may differ from a plain program's by a relative error of at most 0.004.
Values may be sent and summed in bfloat16 or wider, within the bound.
No kernel may reach another device: no remote copies, remote signals or barrier semaphores. Data moves between devices by JAX's collectives and lax.ppermute only.
A program may use at most 64 MiB of HBM per device.

v0:
```python
import jax
import jax.numpy as jnp
from jax import lax
from jax.sharding import PartitionSpec as P


def extended(array, sides, width):
    for axis, dim in sides:
        devices, length = (lax.axis_size(axis), array.shape[dim])
        up = [(i, (i + 1) % devices) for i in range(devices)]
        down = [(j, i) for i, j in up]
        last = lax.slice_in_dim(array, length - width, length, axis=dim)
        first = lax.slice_in_dim(array, 0, width, axis=dim)
        before = lax.ppermute(last, axis, up)
        after = lax.ppermute(first, axis, down)
        array = jnp.concatenate([before, array, after], axis=dim)
    return array


def gelu(value):
    return 0.5 * value * (1.0 + jnp.tanh(0.7978845608 * (value + 0.044715 * value * value * value)))


def conv_taps(padded, weight, rows, cols):
    chans = padded.shape[-1]
    total = jnp.zeros((rows * cols, weight.shape[-1]), jnp.float32)
    for shift_y in range(3):
        for shift_x in range(3):
            tap = padded[shift_y : shift_y + rows, shift_x : shift_x + cols].reshape(
                rows * cols, chans
            )
            total = total + jnp.dot(
                tap, weight[shift_y, shift_x], preferred_element_type=jnp.float32
            )
    return total.reshape(rows, cols, weight.shape[-1])


def fold_ghost(gathered, fold_map, start, depth, width):
    total = fold_map.shape[0]
    columns = (start - depth + jnp.arange(width + 2 * depth, dtype=jnp.int32)) % total
    return jnp.take(gathered, jnp.take(fold_map, columns, axis=0), axis=0)


def stack_rows(wide, ghost):
    zeros = jnp.zeros((1,) + wide.shape[1:], wide.dtype)
    return jnp.concatenate([zeros, wide, ghost[None]], axis=0)


def local(state, ocean_mask, fold_map, w_first, b_first, w_second, b_second):
    rows, width, chans = state.shape
    start = lax.axis_index("lon") * width
    masked = state * ocean_mask.astype(jnp.bfloat16)[:, :, None]
    signs = jnp.where(jnp.arange(chans) < chans // 2, -1.0, 1.0).astype(jnp.bfloat16)
    mask_own = ocean_mask.astype(jnp.float32)[:, :, None]
    top_state = lax.all_gather(masked[rows - 1], "lon", axis=0, tiled=True)
    wide = extended(masked, (("lon", 1),), 1)
    ghost = fold_ghost(top_state, fold_map, start, 1, width) * signs
    first = conv_taps(stack_rows(wide, ghost), w_first, rows, width)
    hidden = (gelu(first + b_first) * mask_own).astype(jnp.bfloat16)
    hidden_wide = extended(hidden, (("lon", 1),), 1)
    top_hidden = lax.all_gather(hidden[rows - 1], "lon", axis=0, tiled=True)
    ghost_hidden = fold_ghost(top_hidden, fold_map, start, 1, width)
    second = conv_taps(stack_rows(hidden_wide, ghost_hidden), w_second, rows, width)
    return ((second + b_second) * mask_own).astype(jnp.bfloat16)


def solution(mesh):
    return jax.shard_map(
        local,
        mesh=mesh,
        in_specs=(P(None, ("grp", "lon"), None), P(None, "lon"), P(), P(), P(), P(), P()),
        out_specs=P(None, ("grp", "lon"), None),
        check_vma=False,
    )
```

profile of v0, /device:TPU:0, one launch (start us, length us, event | category | flops | bytes accessed | tf_op | source)
XLA Modules:
  0.0 118.8 jit_solution(11845723673529406524)
XLA Ops:
  0.9 2.4 %copy.28 = bf16[256,8,300]{2,1,0:T(8,128)(2,1)S(1)} copy(bf16[256,8,300]{0,1,2:T(8,128)(2,1)} %param.9) | data formatting | bytes 2457600 | tf_op args[0]
  3.6 1.3 %fusion.92 = (bf16[256,1,300]{2,1,0:T(2,128)(2,1)S(1)}, bf16[256,1,300]{2,1,0:T(2,128)(2,1)}) fusion(bf16[256,8,300]{2,1,0:T(8,128)(2,1)S(1)} %broadcast_multiply_fusion), kind=kLoop, calls=%fused_computation.138 | loop fusion | bytes 614400 | tf_op jit(solution)/shard_map/slice | solution.py:12
  5.4 5.0 %collective-permute-start.1 = (bf16[256,1,300]{2,1,0:T(2,128)(2,1)}, bf16[256,1,300]{2,1,0:T(2,128)(2,1)}, u32[]{:S(2)}, u32[]{:S(2)}) collective-permute-start(bf16[256,1,300]{2,1,0:T(2,128)(2,1)} %get-tuple-element.17), channel_id=1, source_target_pairs={{1,0},{2,1},{3,2},{4,3},{5,4},{6,5},{7,6},{8,7},{9,8},{10,9},{11,1... | collective-permute-start | bytes 460808 | tf_op jit(solution)/shard_map/ppermute | solution.py:15
  11.5 20.3 %all-gather = bf16[1,128,300]{2,1,0:T(8,128)(2,1)S(1)} all-gather(bf16[1,8,300]{2,1,0:T(8,128)(2,1)S(1)} %slice.187), channel_id=2, replica_groups=mesh['grp'=2,'lon'=16] {'lon'}, dimensions={1}, use_global_device_ids=true | all-gather | bytes 81600 | tf_op jit(solution)/shard_map/all_gather | solution.py:55
  33.2 1.2 %copy.41 = bf16[1,10,300]{0,2,1:T(8,128)(2,1)} copy(bf16[1,10,300]{2,1,0:T(8,128)(2,1)S(1)} %fusion.82) | data formatting | bytes 12000 | tf_op jit(solution)/shard_map/mul | solution.py:57
  34.7 1.2 %copy.29 = bf16[256,1,300]{0,2,1:T(8,128)(2,1)S(1)} copy(bf16[256,1,300]{2,1,0:T(2,128)(2,1)} %collective-permute-done) | data formatting | bytes 307200 | tf_op jit(solution)/shard_map/ppermute | solution.py:14
  35.9 1.2 %copy.31 = bf16[256,1,300]{0,2,1:T(8,128)(2,1)S(1)} copy(bf16[256,1,300]{2,1,0:T(2,128)(2,1)} %collective-permute-done.1) | data formatting | bytes 307200 | tf_op jit(solution)/shard_map/ppermute | solution.py:15
  37.2 1.7 %pad_maximum_fusion.2 = (bf16[256,8,300]{0,2,1:T(8,128)(2,1)}, bf16[256,8,300]{0,2,1:T(8,128)(2,1)}) fusion(bf16[256,1,300]{0,2,1:T(8,128)(2,1)S(1)} %copy.31, bf16[256,8,300]{0,2,1:T(8,128)(2,1)S(1)} %copy.30, bf16[256,1,300]{0,2,1:T(8,128)(2,1)S(1)} %copy.29), kind=kLoop, calls=%fused_computation.61 | loop fusion | flops 1228800 | bytes 3993600 | tf_op jit(solution)/shard_map/concatenate | solution.py:16
  38.9 2.0 %pad_maximum_fusion = (bf16[257,10,300]{0,2,1:T(8,128)(2,1)S(1)}, bf16[257,10,300]{0,2,1:T(8,128)(2,1)S(1)}) fusion(bf16[1,10,300]{0,2,1:T(8,128)(2,1)S(1)} %copy-done.11, bf16[256,1,300]{0,2,1:T(8,128)(2,1)S(1)} %copy.31, bf16[256,8,300]{0,2,1:T(8,128)(2,1)S(1)} %copy.30, bf16[256,1,300]{0,2,1:T(8,128)(2,1)S(1)} %copy.29), kind=kLoop, calls=%fused_computation.31 | loop fusion | flops 13878000 | bytes 4626000 | tf_op jit(solution)/shard_map/concatenate | solution.py:46
  40.9 3.8 %fusion.90 = (bf16[256,8,300]{0,2,1:T(8,128)(2,1)}, bf16[256,8,300]{0,2,1:T(8,128)(2,1)}, bf16[256,8,300]{0,2,1:T(8,128)(2,1)}, bf16[256,8,300]{0,2,1:T(8,128)(2...) fusion(bf16[257,10,300]{0,2,1:T(8,128)(2,1)S(1)} %get-tuple-element.18, ...), kind=kLoop, calls=%fused_computation.136 | loop fusion | bytes 14745600 | tf_op jit(solution)/shard_map/slice | solution.py:29
  44.7 2.9 %copy.32 = bf16[256,8,300]{2,1,0:T(8,128)(2,1)} copy(bf16[256,8,300]{0,2,1:T(8,128)(2,1)} %get-tuple-element.28) | data formatting | bytes 2457600 | tf_op jit(solution)/shard_map/slice | solution.py:29
  47.6 2.9 %copy.33 = bf16[256,8,300]{2,1,0:T(8,128)(2,1)} copy(bf16[256,8,300]{0,2,1:T(8,128)(2,1)} %get-tuple-element.29) | data formatting | bytes 2457600 | tf_op jit(solution)/shard_map/slice | solution.py:29
  50.5 2.0 %copy.34 = bf16[256,8,300]{2,1,0:T(8,128)(2,1)} copy(bf16[256,8,300]{0,2,1:T(8,128)(2,1)S(1)} %get-tuple-element.30) | data formatting | bytes 2457600 | tf_op jit(solution)/shard_map/slice | solution.py:29
  52.5 2.1 %copy.37 = bf16[256,8,300]{2,1,0:T(8,128)(2,1)S(1)} copy(bf16[256,8,300]{0,2,1:T(8,128)(2,1)} %get-tuple-element.21) | data formatting | bytes 2457600 | tf_op jit(solution)/shard_map/slice | solution.py:29
  54.6 2.2 %fusion.34 = f32[2048,256]{1,0:T(8,128)S(1)} fusion(bf16[256,8,300]{2,1,0:T(8,128)(2,1)} %copy.32, bf16[3,3,300,256]{3,2,1,0:T(8,128)(2,1)} %param.12), kind=kOutput, calls=%fused_computation.59 | convolution fusion | flops 314572800 | bytes 3825664 | tf_op jit(solution)/shard_map/dot_general | solution.py:32
  56.9 1.7 %convolution_add_fusion.7 = f32[2048,256]{1,0:T(8,128)S(1)} fusion(f32[2048,256]{1,0:T(8,128)S(1)} %fusion.34, bf16[256,8,300]{2,1,0:T(8,128)(2,1)S(1)} %copy-done.6, bf16[3,3,300,256]{3,2,1,0:T(8,128)(2,1)} %param.12), kind=kOutput, calls=%fused_computation.20 | convolution fusion | flops 315097088 | bytes 5578752 | tf_op jit(solution)/shard_map/dot_general | solution.py:32
  58.6 1.6 %convolution_add_fusion.6 = f32[2048,256]{1,0:T(8,128)S(1)} fusion(f32[2048,256]{1,0:T(8,128)S(1)} %convolution_add_fusion.7, bf16[256,8,300]{2,1,0:T(8,128)(2,1)S(1)} %copy-done.5, bf16[3,3,300,256]{3,2,1,0:T(8,128)(2,1)} %param.12), kind=kOutput, calls=%fused_computation.19 | convolution fusion | flops 315097088 | bytes 5578752 | tf_op jit(solution)/shard_map/dot_general | solution.py:32
  60.2 1.6 %convolution_add_fusion.5 = f32[2048,256]{1,0:T(8,128)S(1)} fusion(f32[2048,256]{1,0:T(8,128)S(1)} %convolution_add_fusion.6, bf16[256,8,300]{2,1,0:T(8,128)(2,1)S(1)} %copy.37, bf16[3,3,300,256]{3,2,1,0:T(8,128)(2,1)} %param.12), kind=kOutput, calls=%fused_computation.18 | convolution fusion | flops 315097088 | bytes 5578752 | tf_op jit(solution)/shard_map/dot_general | solution.py:32
  61.9 3.1 %convolution_add_fusion.4 = f32[2048,256]{1,0:T(8,128)} fusion(f32[2048,256]{1,0:T(8,128)S(1)} %convolution_add_fusion.5, bf16[256,8,300]{2,1,0:T(8,128)(2,1)S(1)} %broadcast_multiply_fusion, bf16[3,3,300,256]{3,2,1,0:T(8,128)(2,1)} %param.12), kind=kOutput, calls=%fused_computation.17 | convolution fusion | flops 315097088 | bytes 5578752 | tf_op jit(solution)/shard_map/dot_general | solution.py:32
  65.0 2.0 %copy.40 = bf16[256,8,300]{2,1,0:T(8,128)(2,1)} copy(bf16[256,8,300]{0,2,1:T(8,128)(2,1)S(1)} %copy-done.10) | data formatting | bytes 2457600 | tf_op jit(solution)/shard_map/slice | solution.py:29
  67.0 2.1 %copy.42 = bf16[256,8,300]{2,1,0:T(8,128)(2,1)} copy(bf16[256,8,300]{0,2,1:T(8,128)(2,1)S(1)} %copy-done.9) | data formatting | bytes 2457600 | tf_op jit(solution)/shard_map/slice | solution.py:29
  69.1 2.0 %copy.43 = bf16[256,8,300]{2,1,0:T(8,128)(2,1)} copy(bf16[256,8,300]{0,2,1:T(8,128)(2,1)S(1)} %copy-done.8) | data formatting | bytes 2457600 | tf_op jit(solution)/shard_map/slice | solution.py:29
  71.1 2.1 %copy.44 = bf16[256,8,300]{2,1,0:T(8,128)(2,1)} copy(bf16[256,8,300]{0,2,1:T(8,128)(2,1)S(1)} %copy-done.7) | data formatting | bytes 2457600 | tf_op jit(solution)/shard_map/slice | solution.py:29
  73.2 2.2 %convolution_add_fusion.3 = f32[2048,256]{1,0:T(8,128)S(1)} fusion(f32[2048,256]{1,0:T(8,128)S(1)} %copy-done.2, bf16[256,8,300]{2,1,0:T(8,128)(2,1)} %copy.40, bf16[3,3,300,256]{3,2,1,0:T(8,128)(2,1)} %param.12), kind=kOutput, calls=%fused_computation.16 | convolution fusion | flops 315097088 | bytes 5922816 | tf_op jit(solution)/shard_map/dot_general | solution.py:32
  75.5 1.7 %convolution_add_fusion.2 = f32[2048,256]{1,0:T(8,128)S(1)} fusion(f32[2048,256]{1,0:T(8,128)S(1)} %convolution_add_fusion.3, bf16[256,8,300]{2,1,0:T(8,128)(2,1)S(1)} %copy-done.4, bf16[3,3,300,256]{3,2,1,0:T(8,128)(2,1)} %param.12), kind=kOutput, calls=%fused_computation.15 | convolution fusion | flops 315097088 | bytes 5578752 | tf_op jit(solution)/shard_map/dot_general | solution.py:32
  77.3 1.7 %convolution_add_fusion.1 = f32[2048,256]{1,0:T(8,128)S(1)} fusion(f32[2048,256]{1,0:T(8,128)S(1)} %convolution_add_fusion.2, bf16[256,8,300]{2,1,0:T(8,128)(2,1)S(1)} %copy-done.3, bf16[3,3,300,256]{3,2,1,0:T(8,128)(2,1)} %param.12), kind=kOutput, calls=%fused_computation.14 | convolution fusion | flops 315097088 | bytes 5578752 | tf_op jit(solution)/shard_map/dot_general | solution.py:32
  79.1 3.5 %fusion.17 = (bf16[256,8,256]{2,1,0:T(8,128)(2,1)S(1)}, f32[2048,256]{1,0:T(8,128)}) fusion(f32[256,8]{1,0:T(8,128)S(1)} %copy.45, f32[256]{0:T(256)S(1)} %copy-done.14, f32[2048,256]{1,0:T(8,128)S(1)} %convolution_add_fusion.1, bf16[3,3,300,256]{3,2,1,0:T(8,128)(2,1)} %param.12, bf16[256,8,300]{2,1,0:T(8,128)(2,1)S(1)} %copy-done.12), kind=kOutput, calls=%fused_computation.40 | convolution fusion | flops 320864256 | bytes 6636544 | tf_op jit(solution)/shard_map/dot_general | solution.py:32
  83.3 4.1 %collective-permute-start.3 = (bf16[256,1,256]{2,1,0:T(2,128)(2,1)S(1)}, bf16[256,1,256]{2,1,0:T(2,128)(2,1)S(1)}, u32[]{:S(2)}, u32[]{:S(2)}) collective-permute-start(bf16[256,1,256]{2,1,0:T(2,128)(2,1)S(1)} %get-tuple-element.23), channel_id=1, source_target_pairs={{1,0},{2,1},{3,2},{4,3},{5,4},{6,5},{7,6},{8,7},{9,8},{10,9},{11,1... | collective-permute-start | bytes 393224 | tf_op jit(solution)/shard_map/ppermute | solution.py:15
  87.4 19.5 %all-gather.1 = bf16[1,128,256]{2,1,0:T(8,128)(2,1)S(1)} all-gather(bf16[1,8,256]{2,1,0:T(8,128)(2,1)S(1)} %slice.196), channel_id=3, replica_groups=mesh['grp'=2,'lon'=16] {'lon'}, dimensions={1}, use_global_device_ids=true | all-gather | bytes 69632 | tf_op jit(solution)/shard_map/all_gather | solution.py:61
  107.4 2.5 %fusion.44 = f32[2048,256]{1,0:T(8,128)S(1)} fusion(f32[2048,256]{1,0:T(8,128)} %get-tuple-element.27, f32[2048]{0:T(1024)S(1)} %mul.123, f32[256]{0:T(256)S(1)} %copy-done.14, bf16[3,3,256,256]{3,2,1,0:T(8,128)(2,1)S(1)} %copy-done.13), kind=kOutput, calls=%fused_computation.77 | convolution fusion | flops 274202624 | bytes 4334592 | tf_op jit(solution)/shard_map/dot_general | solution.py:32
  110.0 2.8 %fusion.11 = (bf16[257,10,256]{2,1,0:T(8,128)(2,1)S(1)}, bf16[257,10,256]{2,1,0:T(8,128)(2,1)S(1)}) fusion(bf16[256,1,256]{2,1,0:T(2,128)(2,1)S(1)} %collective-permute-done.3, bf16[256,8,256]{2,1,0:T(8,128)(2,1)S(1)} %get-tuple-element.26, bf16[256,1,256]{2,1,0:T(2,128)(2,1)S(1)} %collective-permute-done.2, bf16[1,10,256]{2,1,0:T(8,128)(2,1)S(1)} %bitcast_select_fusion.1), kind=kLoop, calls=%fused_computation.33 | loop fusion | flops 11842560 | bytes 3947520 | tf_op jit(solution)/shard_map/concatenate | solution.py:16
  117.2 1.7 %fusion.25 = bf16[256,8,256]{2,1,0:T(8,128)(2,1)} fusion(f32[2048,256]{1,0:T(8,128)S(1)} %convolution_add_fusion.9, bf16[257,10,256]{2,1,0:T(8,128)(2,1)S(1)} %get-tuple-element.15, f32[256]{0:T(256)S(1)} %copy-done.15, f32[256,8]{1,0:T(8,128)S(1)} %copy.45, bf16[3,3,256,256]{3,2,1,0:T(8,128)(2,1)S(1)} %copy-done.13), kind=kOutput, calls=%fused_computation.49 | convolution fusion | flops 270532608 | bytes 4457472 | tf_op jit(solution)/shard_map/dot_general | solution.py:32
  (64 shorter events, 10.2 us)
Async XLA Ops:
  0.0 31.8 %copy-start = (s32[128]{0:T(128)S(1)}, s32[128]{0:T(128)}, u32[]{:S(2)}) copy-start(s32[128]{0:T(128)} %param.11) | copy-start | bytes 1540
  4.9 29.8 %collective-permute-start = (bf16[256,1,300]{2,1,0:T(2,128)(2,1)S(1)}, bf16[256,1,300]{2,1,0:T(2,128)(2,1)}, u32[]{:S(2)}, u32[]{:S(2)}) collective-permute-start(bf16[256,1,300]{2,1,0:T(2,128)(2,1)S(1)} %get-tuple-element.16), channel_id=1, source_target_pairs={{0,1},{1,2},{2,3},{3,4},{4,5},{5,6},{6,7},{7,8},{8,9},{9,10},{10,1... | collective-permute-start | bytes 460808 | tf_op jit(solution)/shard_map/ppermute | solution.py:14
  5.4 30.5 %collective-permute-start.1 = (bf16[256,1,300]{2,1,0:T(2,128)(2,1)}, bf16[256,1,300]{2,1,0:T(2,128)(2,1)}, u32[]{:S(2)}, u32[]{:S(2)}) collective-permute-start(bf16[256,1,300]{2,1,0:T(2,128)(2,1)} %get-tuple-element.17), channel_id=1, source_target_pairs={{1,0},{2,1},{3,2},{4,3},{5,4},{6,5},{7,6},{8,7},{9,8},{10,9},{11,1... | collective-permute-start | bytes 460808 | tf_op jit(solution)/shard_map/ppermute | solution.py:15
  37.1 1.7 %copy-start.11 = (bf16[1,10,300]{0,2,1:T(8,128)(2,1)S(1)}, bf16[1,10,300]{0,2,1:T(8,128)(2,1)}, u32[]{:S(2)}) copy-start(bf16[1,10,300]{0,2,1:T(8,128)(2,1)} %copy.41) | copy-start | bytes 18004
  54.6 2.2 %copy-start.6 = (bf16[256,8,300]{2,1,0:T(8,128)(2,1)S(1)}, bf16[256,8,300]{2,1,0:T(8,128)(2,1)}, u32[]{:S(2)}) copy-start(bf16[256,8,300]{2,1,0:T(8,128)(2,1)} %copy.33) | copy-start | bytes 3686404
  56.9 1.8 %copy-start.5 = (bf16[256,8,300]{2,1,0:T(8,128)(2,1)S(1)}, bf16[256,8,300]{2,1,0:T(8,128)(2,1)}, u32[]{:S(2)}) copy-start(bf16[256,8,300]{2,1,0:T(8,128)(2,1)} %copy.34) | copy-start | bytes 3686404
  61.9 3.1 %copy-start.10 = (bf16[256,8,300]{0,2,1:T(8,128)(2,1)S(1)}, bf16[256,8,300]{0,2,1:T(8,128)(2,1)}, u32[]{:S(2)}) copy-start(bf16[256,8,300]{0,2,1:T(8,128)(2,1)} %get-tuple-element.20) | copy-start | bytes 3686404
  65.0 2.0 %copy-start.9 = (bf16[256,8,300]{0,2,1:T(8,128)(2,1)S(1)}, bf16[256,8,300]{0,2,1:T(8,128)(2,1)}, u32[]{:S(2)}) copy-start(bf16[256,8,300]{0,2,1:T(8,128)(2,1)} %get-tuple-element.10) | copy-start | bytes 3686404
  67.0 2.1 %copy-start.8 = (bf16[256,8,300]{0,2,1:T(8,128)(2,1)S(1)}, bf16[256,8,300]{0,2,1:T(8,128)(2,1)}, u32[]{:S(2)}) copy-start(bf16[256,8,300]{0,2,1:T(8,128)(2,1)} %get-tuple-element.9) | copy-start | bytes 3686404
  69.1 2.0 %copy-start.7 = (bf16[256,8,300]{0,2,1:T(8,128)(2,1)S(1)}, bf16[256,8,300]{0,2,1:T(8,128)(2,1)}, u32[]{:S(2)}) copy-start(bf16[256,8,300]{0,2,1:T(8,128)(2,1)} %get-tuple-element.8) | copy-start | bytes 3686404
  71.1 2.1 %copy-start.2 = (f32[2048,256]{1,0:T(8,128)S(1)}, f32[2048,256]{1,0:T(8,128)}, u32[]{:S(2)}) copy-start(f32[2048,256]{1,0:T(8,128)} %convolution_add_fusion.4) | copy-start | bytes 6291460
  73.2 2.2 %copy-start.4 = (bf16[256,8,300]{2,1,0:T(8,128)(2,1)S(1)}, bf16[256,8,300]{2,1,0:T(8,128)(2,1)}, u32[]{:S(2)}) copy-start(bf16[256,8,300]{2,1,0:T(8,128)(2,1)} %copy.42) | copy-start | bytes 3686404
  75.5 1.7 %copy-start.3 = (bf16[256,8,300]{2,1,0:T(8,128)(2,1)S(1)}, bf16[256,8,300]{2,1,0:T(8,128)(2,1)}, u32[]{:S(2)}) copy-start(bf16[256,8,300]{2,1,0:T(8,128)(2,1)} %copy.43) | copy-start | bytes 3686404
  77.3 1.8 %copy-start.12 = (bf16[256,8,300]{2,1,0:T(8,128)(2,1)S(1)}, bf16[256,8,300]{2,1,0:T(8,128)(2,1)}, u32[]{:S(2)}) copy-start(bf16[256,8,300]{2,1,0:T(8,128)(2,1)} %copy.44) | copy-start | bytes 3686404
  77.3 1.8 %copy-start.14 = (f32[256]{0:T(256)S(1)}, f32[256]{0:T(256)}, u32[]{:S(2)}) copy-start(f32[256]{0:T(256)} %param.13) | copy-start | bytes 3076
  79.0 28.4 %copy-start.13 = (bf16[3,3,256,256]{3,2,1,0:T(8,128)(2,1)S(1)}, bf16[3,3,256,256]{3,2,1,0:T(8,128)(2,1)}, u32[]{:S(2)}) copy-start(bf16[3,3,256,256]{3,2,1,0:T(8,128)(2,1)} %param.14) | copy-start | bytes 3538948
  82.9 27.1 %collective-permute-start.2 = (bf16[256,1,256]{2,1,0:T(2,128)(2,1)S(1)}, bf16[256,1,256]{2,1,0:T(2,128)(2,1)S(1)}, u32[]{:S(2)}, u32[]{:S(2)}) collective-permute-start(bf16[256,1,256]{2,1,0:T(2,128)(2,1)S(1)} %get-tuple-element.22), channel_id=1, source_target_pairs={{0,1},{1,2},{2,3},{3,4},{4,5},{5,6},{6,7},{7,8},{8,9},{9,10},{10,1... | collective-permute-start | bytes 393224 | tf_op jit(solution)/shard_map/ppermute | solution.py:14
  83.3 26.7 %collective-permute-start.3 = (bf16[256,1,256]{2,1,0:T(2,128)(2,1)S(1)}, bf16[256,1,256]{2,1,0:T(2,128)(2,1)S(1)}, u32[]{:S(2)}, u32[]{:S(2)}) collective-permute-start(bf16[256,1,256]{2,1,0:T(2,128)(2,1)S(1)} %get-tuple-element.23), channel_id=1, source_target_pairs={{1,0},{2,1},{3,2},{4,3},{5,4},{6,5},{7,6},{8,7},{9,8},{10,9},{11,1... | collective-permute-start | bytes 393224 | tf_op jit(solution)/shard_map/ppermute | solution.py:15
  116.5 0.7 copy-start.15
  116.5 2.3 %copy-start.1 = (s32[128]{0:T(128)S(1)}, s32[128]{0:T(128)}, u32[]{:S(2)}) copy-start(s32[128]{0:T(128)} %param.11) | copy-start | bytes 1540
where the time goes:
time: 119 us
  blocking collectives  39.7 us (33%)
  local copies, waits for them, and re-layouts  33.1 us (28%)
  matrix products  27.8 us (23%)
  starting transfers between devices  9.97 us (8%)
  other arithmetic  7.89 us (7%)
    dot_general x18, matrix products, conv_taps(): jnp.dot(tap, weight[shift_y, shift_x], preferred_element_type=jnp.float32)  27.8 us
    slice x9, local copies, waits for them, and re-layouts, conv_taps(): padded[shift_y:shift_y + rows, shift_x:shift_x + cols]  21.9 us
    all_gather x1, blocking collectives, local(): top_state = lax.all_gather(masked[rows - 1], 'lon', axis=0, tiled=True)  20.3 us
    all_gather x1, blocking collectives, local(): top_hidden = lax.all_gather(hidden[rows - 1], 'lon', axis=0, tiled=True)  19.5 us
    ppermute x2, starting transfers between devices, extended(): after = lax.ppermute(first, axis, down)  9.08 us
    concatenate x2, other arithmetic, extended(): array = jnp.concatenate([before, array, after], axis=dim)  4.51 us
    unnamed x33, local copies, waits for them, and re-layouts  2.55 us
  transfers between devices with their start and end apart: 4, of which 0 were waited for; matrix products, arithmetic and copies ran while one was open for 7% of the time, Pallas kernels for 0%

commit v1 on v0

v1 whole, which is shorter than its diff:
```python
import functools

import jax
import jax.numpy as jnp
from jax import lax
from jax.experimental import pallas as pl
from jax.experimental.pallas import tpu as pltpu
from jax.sharding import PartitionSpec as P

BF, F32 = jnp.bfloat16, jnp.float32
LANES, MAIN, SLOT = 128, 256, 64
WIDE = MAIN + 2 * SLOT


def gelu(value):
    return 0.5 * value * (1.0 + jnp.tanh(0.7978845608 * (value + 0.044715 * value * value * value)))


def turned(block, chans):
    rows = block.shape[-1]
    tail = block[MAIN : MAIN + SLOT]
    tail = jnp.concatenate([tail, jnp.zeros((SLOT - tail.shape[0], rows), BF)], axis=0)
    full = jnp.concatenate([block[:MAIN], tail, tail], axis=0)
    eye = (
        lax.broadcasted_iota(jnp.int32, (rows, rows), 0) == lax.broadcasted_iota(jnp.int32, (rows, rows), 1)
    ).astype(F32).astype(BF)
    return lax.dot_general(eye, full, (((1,), (1,)), ((), ())), preferred_element_type=F32)


def prepare(me_ref, x_ref, mask_ref, outer_ref, inner_ref, cols_ref, top_ref, field, topf):
    chans, width, rows = x_ref.shape
    held = outer_ref.shape[1]
    odd = lax.rem(me_ref[0], 2) == 1
    mask = mask_ref[...].astype(F32)
    for i in range(rows // LANES):
        at = slice(i * LANES, (i + 1) * LANES)
        field[i, : chans * width, :] = (x_ref[:, :, at].astype(F32) * mask[None, :, at]).reshape(chans * width, LANES)
        field[i, chans * width : (chans + 1) * width, :] = mask[:, at]
        field[i, (chans + 1) * width :, :] = jnp.zeros(((held - chans - 1) * width, LANES), F32)

    def column(c):
        parts = [field[i, pl.ds(c, held, stride=width), :] for i in range(rows // LANES)]
        return jnp.concatenate(parts, axis=1).astype(BF)

    for c in range(2):
        low, high = column(c), column(width - 2 + c)
        outer_ref[c] = jnp.where(odd, high, low)
        inner_ref[c] = jnp.where(odd, low, high)
    for c in range(width):
        out = turned(column(c), chans)
        cols_ref[c] = out.astype(BF)
        for i in range(2):
            topf[i, c : c + 1, :] = out[rows - 2 + i : rows - 1 + i]
    top_ref[...] = topf[...].astype(BF)


def tails(parts):
    lanes = lax.broadcasted_iota(jnp.int32, parts[0].shape, 1)
    return [jnp.where(lanes < SLOT, parts[0], parts[1]), parts[2]]


def conv_block(
    me_ref, fold_ref, cols_ref, outer_ref, inner_ref, top_ref, w1_ref, b1_ref, w2_ref, b2_ref, out_ref,
    xs, wa, wb, hid, gf, m0, m1, r2, gs, hg, ghost1, ghost2, outf,
):
    chans = w1_ref.shape[2]
    width, rows, _ = cols_ref.shape
    hidden = w1_ref.shape[3]
    total = fold_ref.shape[0]
    me = me_ref[0]
    odd = lax.rem(me, 2) == 1
    for dy in range(3):
        for dx in range(3):
            wa[dx * MAIN : (dx + 1) * MAIN, dy * hidden : (dy + 1) * hidden] = w1_ref[dy, dx, :MAIN, :]
            rest = jnp.concatenate(
                [w1_ref[dy, dx, MAIN:, :], jnp.zeros((SLOT - chans + MAIN, hidden), BF)], axis=0
            )
            wa[3 * MAIN + dx * SLOT : 3 * MAIN + (dx + 1) * SLOT, dy * hidden : (dy + 1) * hidden] = rest
            wb[dx * hidden : (dx + 1) * hidden, dy * hidden : (dy + 1) * hidden] = w2_ref[dy, dx]
    wa[3 * MAIN + 3 * SLOT :, :] = jnp.zeros((SLOT, 3 * hidden), BF)

    xs[2 : 2 + width] = cols_ref[...]
    for c in range(2):
        left = jnp.where(odd, inner_ref[c], outer_ref[c])
        right = jnp.where(odd, outer_ref[c], inner_ref[c])
        xs[c] = turned(left, chans).astype(BF)
        xs[2 + width + c] = turned(right, chans).astype(BF)

    bias1, bias2 = b1_ref[...], b2_ref[...]
    mask_lane = chans
    blocks = top_ref.shape[0]
    gf[...] = top_ref[...].astype(F32).reshape(blocks * 2 * width, WIDE)
    for ref in (m0, m1, r2, gs):
        ref[...] = jnp.zeros_like(ref)
    lane = lax.broadcasted_iota(jnp.int32, (1, WIDE), 1)
    sign = jnp.where(lane < chans // 2, -1.0, 1.0).astype(F32)
    for j in range(width + 4):
        col = lax.rem(me * width + (j - 2) + total, total)
        src = fold_ref[col]
        at = (lax.bitwise_xor(src // width, me) * 2) * width + lax.rem(src, width)
        m0[j : j + 1, :] = gf[pl.ds(at, 1), :]
        north = gf[pl.ds(at + width, 1), :]
        m1[j : j + 1, :] = north
        gs[j : j + 1, :] = north * sign
        r2[j : j + 1, :] = xs[j, rows - 16 :, :].astype(F32)[15:16] * sign

    def taps(ref, offsets):
        parts = [ref[o : o + 16, :].astype(BF) for o in offsets]
        return jnp.concatenate([p[:, :MAIN] for p in parts] + tails([p[:, MAIN:] for p in parts]), axis=1)

    def mm(a, b):
        return jnp.dot(a, b, preferred_element_type=F32)

    ghost1[...] = mm(taps(gs, (0, 1, 2)), wa[:, 2 * hidden :])
    pre = mm(taps(m0, (2, 1, 0)), wa[:, :hidden])
    pre += mm(taps(m1, (2, 1, 0)), wa[:, hidden : 2 * hidden])
    pre += mm(taps(r2, (2, 1, 0)), wa[:, 2 * hidden :])
    hg[...] = jnp.zeros_like(hg)
    hg[:16, :] = gelu(pre + bias1) * m1[1:17, mask_lane : mask_lane + 1]
    ghost2[...] = mm(
        jnp.concatenate([hg[o : o + 16, :].astype(BF) for o in range(3)], axis=1), wb[:, 2 * hidden :]
    )

    row = lax.broadcasted_iota(jnp.int32, (rows, hidden), 0)

    def summed(p, ghost):
        south = jnp.where(row == 0, 0.0, pltpu.roll(p[:, :hidden], 1, 0))
        north = jnp.where(row == rows - 1, ghost, pltpu.roll(p[:, 2 * hidden :], rows - 1, 0))
        return p[:, hidden : 2 * hidden] + south + north

    for h in range(width + 2):
        parts = [xs[h + dx, :, MAIN:] for dx in range(3)]
        lhs = jnp.concatenate([xs[h + dx, :, :MAIN] for dx in range(3)] + tails(parts), axis=1)
        value = summed(mm(lhs, wa[...]), ghost1[h : h + 1, :])
        mask = xs[h + 1, :, MAIN:].astype(F32)[:, mask_lane - MAIN : mask_lane - MAIN + 1]
        hid[h] = (gelu(value + bias1) * mask).astype(BF)
    for o in range(width):
        lhs = jnp.concatenate([hid[o + dx] for dx in range(3)], axis=1)
        value = summed(mm(lhs, wb[...]), ghost2[o : o + 1, :])
        mask = xs[o + 2, :, MAIN:].astype(F32)[:, mask_lane - MAIN : mask_lane - MAIN + 1]
        value = (value + bias2) * mask
        for i in range(hidden // LANES):
            outf[i, pl.ds(o, rows, stride=width), :] = value[:, i * LANES : (i + 1) * LANES]
    for i in range(hidden // LANES):
        out_ref[:, :, i * LANES : (i + 1) * LANES] = outf[i].reshape(rows, width, LANES).astype(BF)


def local(state, ocean_mask, fold_map, w_first, b_first, w_second, b_second):
    rows, width, chans = state.shape
    hidden = w_first.shape[-1]
    n = lax.axis_size("lon")
    me = lax.axis_index("lon")
    assert n & (n - 1) == 0 and MAIN <= chans < MAIN + SLOT and chans // 2 <= MAIN
    held = -(-(chans + 1) // 16) * 16
    smem = pl.BlockSpec(memory_space=pltpu.SMEM)
    vmem = pl.BlockSpec(memory_space=pltpu.VMEM)
    place = jnp.full((1,), me, jnp.int32)
    outer, inner, cols, top = pl.pallas_call(
        prepare,
        out_shape=(
            jax.ShapeDtypeStruct((2, held, rows), BF),
            jax.ShapeDtypeStruct((2, held, rows), BF),
            jax.ShapeDtypeStruct((width, rows, WIDE), BF),
            jax.ShapeDtypeStruct((2, width, WIDE), BF),
        ),
        in_specs=[smem, vmem, vmem],
        out_specs=(vmem,) * 4,
        scratch_shapes=[pltpu.VMEM((rows // LANES, held * width, LANES), F32), pltpu.VMEM((2, width, WIDE), F32)],
        name="prepare",
    )(place, state.transpose(2, 1, 0), ocean_mask.T)

    def swap(value, pairs):
        return lax.ppermute(value, "lon", pairs)

    outer = swap(outer, [(i, (i + 1 if i % 2 else i - 1) % n) for i in range(n)])
    inner = swap(inner, [(i, i ^ 1) for i in range(n)])
    tops, step = top[None], 1
    while step < n:
        tops = jnp.concatenate([tops, swap(tops, [(i, i ^ step) for i in range(n)])], axis=0)
        step *= 2
    blocks = width + 2
    return pl.pallas_call(
        conv_block,
        out_shape=jax.ShapeDtypeStruct((rows, width, hidden), BF),
        in_specs=[smem, smem] + [vmem] * 8,
        out_specs=vmem,
        scratch_shapes=[
            pltpu.VMEM((width + 4, rows, WIDE), BF),
            pltpu.VMEM((3 * MAIN + 4 * SLOT, 3 * hidden), BF),
            pltpu.VMEM((3 * hidden, 3 * hidden), BF),
            pltpu.VMEM((blocks, rows, hidden), BF),
            pltpu.VMEM((n * 2 * width, WIDE), F32),
            pltpu.VMEM((24, WIDE), F32),
            pltpu.VMEM((24, WIDE), F32),
            pltpu.VMEM((24, WIDE), F32),
            pltpu.VMEM((24, WIDE), F32),
            pltpu.VMEM((24, hidden), F32),
            pltpu.VMEM((16, hidden), F32),
            pltpu.VMEM((16, hidden), F32),
            pltpu.VMEM((hidden // LANES, rows * width, LANES), F32),
        ],
        compiler_params=pltpu.CompilerParams(vmem_limit_bytes=48 << 20),
        name="conv_block",
    )(place, fold_map, cols, outer, inner, tops, w_first, b_first[None], w_second, b_second[None])


def solution(mesh):
    return jax.shard_map(
        local,
        mesh=mesh,
        in_specs=(P(None, ("grp", "lon"), None), P(None, "lon"), P(), P(), P(), P(), P()),
        out_specs=P(None, ("grp", "lon"), None),
        check_vma=False,
    )
```

time: 119 us -> 40.6 us (0.34)
  blocking collectives: 39.7 us -> 0 us
  local copies, waits for them, and re-layouts: 33.1 us -> 3.44 us
  matrix products: 27.8 us -> 0 us
  Pallas kernels: 0 us -> 14 us
  waiting for transfers between devices: 0.01 us -> 9.01 us
  other arithmetic: 7.89 us -> 2.15 us
  starting transfers between devices: 9.97 us -> 11.5 us
    all_gather x2 -> x0, blocking collectives: 39.7 us -> none  [the longest x1 20.3 us: local(): top_state = lax.all_gather(masked[rows - 1], 'lon', axis=0, tiled=True)]
    dot_general x18 -> x0, matrix products: 27.8 us -> none  [conv_taps(): jnp.dot(tap, weight[shift_y, shift_x], preferred_element_type=jnp.float32)]
    slice x13 -> x0, local copies, waits for them, and re-layouts: 23.5 us -> none  [the longest x9 21.9 us: conv_taps(): padded[shift_y:shift_y + rows, shift_x:shift_x + cols]]
    pallas_call x0 -> x2, Pallas kernels: none -> 14 us  [the longest x1 10.3 us: local(): pl.pallas_call(conv_block, out_shape=jax.ShapeDtypeStruct((rows, width, h...]
    ppermute x4 -> x6, waiting for transfers between devices: 0.01 us -> 9.01 us  [swap(): return lax.ppermute(value, 'lon', pairs)]
    concatenate x3, other arithmetic: 6.56 us -> 2.15 us  [local(): jnp.concatenate([tops, swap(tops, [(i, i ^ step) for i in range(n)])], ax...]
    mul x3 -> x0, local copies, waits for them, and re-layouts: 2.48 us -> none  [the longest x1 1.24 us: local(): ghost = fold_ghost(top_state, fold_map, start, 1, width) * signs]
    ppermute x2 -> x0, local copies, waits for them, and re-layouts: 2.44 us -> none  [the longest x1 1.22 us: extended(): before = lax.ppermute(last, axis, up)]
  transfers between devices with their start and end apart: 4 -> 6, of which waited for: 0 -> 3; matrix products, arithmetic and copies ran while one was open for 7% -> 7% of each run, Pallas kernels for 0% -> 0%
where the time goes in v1:
time: 40.6 us; the launch traced here: 40.2 us
  Pallas kernels  14 us (34%)
  starting transfers between devices  11.5 us (28%)
  waiting for transfers between devices  9.01 us (22%)
  local copies, waits for them, and re-layouts  3.44 us (8%)
  other arithmetic  2.15 us (5%)
    ppermute x6, starting transfers between devices, swap(): return lax.ppermute(value, 'lon', pairs)  11.5 us
    pallas_call x1, Pallas kernels, local(): pl.pallas_call(conv_block, out_shape=jax.ShapeDtypeStruct((rows, width, h...  10.3 us
    ppermute x6, waiting for transfers between devices, swap(): return lax.ppermute(value, 'lon', pairs)  9.01 us
    pallas_call x1, Pallas kernels, local(): pl.pallas_call(prepare, out_shape=(jax.ShapeDtypeStruct((2, held, rows),...  3.69 us
    unnamed x16, local copies, waits for them, and re-layouts  3.42 us
    concatenate x3, other arithmetic, local(): jnp.concatenate([tops, swap(tops, [(i, i ^ step) for i in range(n)])], ax...  2.15 us
  transfers between devices with their start and end apart: 6, of which 3 were waited for; matrix products, arithmetic and copies ran while one was open for 7% of the time, Pallas kernels for 0%

profile of v1, /device:TPU:0, one launch (start us, length us, event | category | flops | bytes accessed | tf_op | source)
XLA Modules:
  0.0 40.2 jit_solution(16447534440216151330)
XLA Ops:
  0.0 0.0 copy-start.4
  0.0 0.0 copy-start.3
  0.0 0.0 copy-start.1
  0.0 0.0 copy-start.5
  0.0 3.7 %prepare.1 = (bf16[2,304,256]{2,1,0:T(8,128)(2,1)}, bf16[2,304,256]{2,1,0:T(8,128)(2,1)}, bf16[8,256,384]{2,1,0:T(8,128)(2,1)}, bf16[2,8,384]{2,1,0:T(8,128)(2,1)}) custom-call(s32[1]{0:T(128)} %bitcast.me_ref, bf16[300,8,256]{2,1,0:T(8,128)(2,1)} %bitcast.9, s32[8,256]{1,0:T(8,128)} %bitcast.14), custom_call_target="tpu_custom_call" | custom-call | tf_op jit(solution)/shard_map/prepare/pallas_call | solution.py:158
  3.7 0.5 %collective-permute-start.2 = (bf16[1,2,8,384]{3,2,1,0:T(8,128)(2,1)}, bf16[1,2,8,384]{3,2,1,0:T(8,128)(2,1)S(1)}, u32[]{:S(2)}, u32[]{:S(2)}) collective-permute-start(bf16[1,2,8,384]{3,2,1,0:T(8,128)(2,1)} %bitcast.10), channel_id=1, source_target_pairs={{0,1},{1,0},{2,3},{3,2},{4,5},{5,4},{6,7},{7,6},{8,9},{9,8},{10,11... | collective-permute-start | bytes 36872 | tf_op jit(solution)/shard_map/ppermute | solution.py:173
  4.2 5.7 %collective-permute-start = (bf16[2,304,256]{2,1,0:T(8,128)(2,1)}, bf16[2,304,256]{2,1,0:T(8,128)(2,1)S(1)}, u32[]{:S(2)}, u32[]{:S(2)}) collective-permute-start(bf16[2,304,256]{2,1,0:T(8,128)(2,1)} %get-tuple-element.10), channel_id=1, source_target_pairs={{0,15},{1,2},{2,1},{3,4},{4,3},{5,6},{6,5},{7,8},{8,7},{9,10},{10,... | collective-permute-start | bytes 933896 | tf_op jit(solution)/shard_map/ppermute | solution.py:173
  9.9 0.0 collective-permute-start.1
  9.9 0.7 %constant_dynamic-update-slice_fusion.4 = bf16[16,2,8,384]{3,2,1,0:T(8,128)(2,1)S(1)} fusion(bf16[2,8,384]{2,1,0:T(8,128)(2,1)} %get-tuple-element.12), kind=kLoop, calls=%fused_computation.7 | loop fusion | bytes 24576
  10.6 0.0 collective-permute-done.2
  10.6 0.7 %pad_maximum_fusion.2 = bf16[2,2,8,384]{3,2,1,0:T(8,128)(2,1)S(1)} fusion(bf16[1,2,8,384]{3,2,1,0:T(8,128)(2,1)S(1)} %collective-permute-done.2, bf16[1,2,8,384]{3,2,1,0:T(8,128)(2,1)} %bitcast.11), kind=kLoop, calls=%fused_computation.2 | loop fusion | flops 12288 | bytes 49152 | tf_op jit(solution)/shard_map/concatenate | solution.py:179
  11.3 0.0 collective-permute-start.3
  11.3 4.4 %collective-permute-done.3 = bf16[2,2,8,384]{3,2,1,0:T(8,128)(2,1)S(1)} collective-permute-done((bf16[2,2,8,384]{3,2,1,0:T(8,128)(2,1)S(1)}, bf16[2,2,8,384]{3,2,1,0:T(8,128)(2,1)S(1)}, u32[]{:S(2)}, u32[]{:S(2)}) %collective-permute-start.3) | collective-permute-done | bytes 24608 | tf_op jit(solution)/shard_map/ppermute | solution.py:173
  15.7 0.7 %pad_maximum_fusion.1 = bf16[4,2,8,384]{3,2,1,0:T(8,128)(2,1)S(1)} fusion(bf16[2,2,8,384]{3,2,1,0:T(8,128)(2,1)S(1)} %collective-permute-done.3, bf16[1,2,8,384]{3,2,1,0:T(8,128)(2,1)S(1)} %collective-permute-done.2, bf16[1,2,8,384]{3,2,1,0:T(8,128)(2,1)} %bitcast.12), kind=kLoop, calls=%fused_computation.1 | loop fusion | flops 49152 | bytes 98304 | tf_op jit(solution)/shard_map/concatenate | solution.py:179
  16.4 2.3 %collective-permute-start.4 = (bf16[4,2,8,384]{3,2,1,0:T(8,128)(2,1)S(1)}, bf16[4,2,8,384]{3,2,1,0:T(8,128)(2,1)S(1)}, u32[]{:S(2)}, u32[]{:S(2)}) collective-permute-start(bf16[4,2,8,384]{3,2,1,0:T(8,128)(2,1)S(1)} %pad_maximum_fusion.1), channel_id=1, source_target_pairs={{0,4},{1,5},{2,6},{3,7},{4,0},{5,1},{6,2},{7,3},{8,12},{9,13},{10,... | collective-permute-start | bytes 147464 | tf_op jit(solution)/shard_map/ppermute | solution.py:173
  18.7 2.1 %collective-permute-done.4 = bf16[4,2,8,384]{3,2,1,0:T(8,128)(2,1)S(1)} collective-permute-done((bf16[4,2,8,384]{3,2,1,0:T(8,128)(2,1)S(1)}, bf16[4,2,8,384]{3,2,1,0:T(8,128)(2,1)S(1)}, u32[]{:S(2)}, u32[]{:S(2)}) %collective-permute-start.4) | collective-permute-done | bytes 49184 | tf_op jit(solution)/shard_map/ppermute | solution.py:173
  20.7 0.7 %pad_maximum_fusion = bf16[8,2,8,384]{3,2,1,0:T(8,128)(2,1)S(1)} fusion(bf16[4,2,8,384]{3,2,1,0:T(8,128)(2,1)S(1)} %collective-permute-done.4, bf16[2,2,8,384]{3,2,1,0:T(8,128)(2,1)S(1)} %collective-permute-done.3, bf16[1,2,8,384]{3,2,1,0:T(8,128)(2,1)S(1)} %collective-permute-done.2, bf16[1,2,8,384]{3,2,1,0:T(8,128)(2,1)} %bitcast.13), kind=kLoop, calls=%fused_computation | loop fusion | flops 147456 | bytes 196608 | tf_op jit(solution)/shard_map/concatenate | solution.py:179
  21.4 3.1 %collective-permute-start.5 = (bf16[8,2,8,384]{3,2,1,0:T(8,128)(2,1)S(1)}, bf16[8,2,8,384]{3,2,1,0:T(8,128)(2,1)S(1)}, u32[]{:S(2)}, u32[]{:S(2)}) collective-permute-start(bf16[8,2,8,384]{3,2,1,0:T(8,128)(2,1)S(1)} %pad_maximum_fusion), channel_id=1, source_target_pairs={{0,8},{1,9},{2,10},{3,11},{4,12},{5,13},{6,14},{7,15},{8,0},{9,1},... | collective-permute-start | bytes 294920 | tf_op jit(solution)/shard_map/ppermute | solution.py:173
  24.5 2.6 %collective-permute-done.5 = bf16[8,2,8,384]{3,2,1,0:T(8,128)(2,1)S(1)} collective-permute-done((bf16[8,2,8,384]{3,2,1,0:T(8,128)(2,1)S(1)}, bf16[8,2,8,384]{3,2,1,0:T(8,128)(2,1)S(1)}, u32[]{:S(2)}, u32[]{:S(2)}) %collective-permute-start.5) | collective-permute-done | bytes 98336 | tf_op jit(solution)/shard_map/ppermute | solution.py:173
  27.1 0.0 collective-permute-done.outer_ref
  27.2 0.0 collective-permute-done.1.inner_ref
  27.2 0.0 copy-done.4
  27.2 0.0 copy-done.3
  27.2 0.0 copy-done.1
  27.2 0.0 copy-done.5
  27.2 0.0 copy-start
  27.2 1.4 %copy-done = bf16[8,256,384]{2,1,0:T(8,128)(2,1)S(1)} copy-done((bf16[8,256,384]{2,1,0:T(8,128)(2,1)S(1)}, bf16[8,256,384]{2,1,0:T(8,128)(2,1)}, u32[]{:S(2)}) %copy-start) | copy-done | bytes 1572888
  28.6 0.0 copy-start.2
  28.6 1.3 %copy-done.2 = bf16[3,3,256,256]{3,2,1,0:T(8,128)(2,1)S(1)} copy-done((bf16[3,3,256,256]{3,2,1,0:T(8,128)(2,1)S(1)}, bf16[3,3,256,256]{3,2,1,0:T(8,128)(2,1)}, u32[]{:S(2)}) %copy-start.2) | copy-done | bytes 1179672
  29.9 10.3 %conv_block.1 = bf16[256,8,256]{2,1,0:T(8,128)(2,1)} custom-call(s32[1]{0:T(128)} %bitcast.me_ref, s32[128]{0:T(128)S(1)} %copy-done.5, bf16[8,256,384]{2,1,0:T(8,128)(2,1)S(1)} %copy-done, bf16[2,304,256]{2,1,0:T(8,128)(2,1)S(1)} %collective-permute-done.outer_ref, bf16[2,304,256]{2,1,0:T(8,128)(2,1)S(1)} %collective-permute-done.1.inner_ref, ...), custom_call_target="tpu_custom_call" | custom-call | tf_op jit(solution)/shard_map/conv_block/pallas_call | solution.py:182
  (4 shorter events, 0.0 us)
Async XLA Ops:
  0.0 27.2 %copy-start.4 = (f32[256]{0:T(256)S(1)}, f32[256]{0:T(256)}, u32[]{:S(2)}) copy-start(f32[256]{0:T(256)} %param.13) | copy-start | bytes 3076
  0.0 27.2 %copy-start.3 = (f32[256]{0:T(256)S(1)}, f32[256]{0:T(256)}, u32[]{:S(2)}) copy-start(f32[256]{0:T(256)} %param.11) | copy-start | bytes 3076
  0.0 27.2 %copy-start.1 = (bf16[3,3,300,256]{3,2,1,0:T(8,128)(2,1)S(1)}, bf16[3,3,300,256]{3,2,1,0:T(8,128)(2,1)}, u32[]{:S(2)}) copy-start(bf16[3,3,300,256]{3,2,1,0:T(8,128)(2,1)} %w1_ref.1) | copy-start | bytes 4147204
  0.0 27.2 %copy-start.5 = (s32[128]{0:T(128)S(1)}, s32[128]{0:T(128)}, u32[]{:S(2)}) copy-start(s32[128]{0:T(128)} %fold_ref.1) | copy-start | bytes 1540
  3.7 6.9 %collective-permute-start.2 = (bf16[1,2,8,384]{3,2,1,0:T(8,128)(2,1)}, bf16[1,2,8,384]{3,2,1,0:T(8,128)(2,1)S(1)}, u32[]{:S(2)}, u32[]{:S(2)}) collective-permute-start(bf16[1,2,8,384]{3,2,1,0:T(8,128)(2,1)} %bitcast.10), channel_id=1, source_target_pairs={{0,1},{1,0},{2,3},{3,2},{4,5},{5,4},{6,7},{7,6},{8,9},{9,8},{10,11... | collective-permute-start | bytes 36872 | tf_op jit(solution)/shard_map/ppermute | solution.py:173
  4.2 22.9 %collective-permute-start = (bf16[2,304,256]{2,1,0:T(8,128)(2,1)}, bf16[2,304,256]{2,1,0:T(8,128)(2,1)S(1)}, u32[]{:S(2)}, u32[]{:S(2)}) collective-permute-start(bf16[2,304,256]{2,1,0:T(8,128)(2,1)} %get-tuple-element.10), channel_id=1, source_target_pairs={{0,15},{1,2},{2,1},{3,4},{4,3},{5,6},{6,5},{7,8},{8,7},{9,10},{10,... | collective-permute-start | bytes 933896 | tf_op jit(solution)/shard_map/ppermute | solution.py:173
  9.9 17.3 %collective-permute-start.1 = (bf16[2,304,256]{2,1,0:T(8,128)(2,1)}, bf16[2,304,256]{2,1,0:T(8,128)(2,1)S(1)}, u32[]{:S(2)}, u32[]{:S(2)}) collective-permute-start(bf16[2,304,256]{2,1,0:T(8,128)(2,1)} %get-tuple-element.11), channel_id=1, source_target_pairs={{0,1},{1,0},{2,3},{3,2},{4,5},{5,4},{6,7},{7,6},{8,9},{9,8},{10,11... | collective-permute-start | bytes 933896 | tf_op jit(solution)/shard_map/ppermute | solution.py:173
  11.3 4.4 %collective-permute-start.3 = (bf16[2,2,8,384]{3,2,1,0:T(8,128)(2,1)S(1)}, bf16[2,2,8,384]{3,2,1,0:T(8,128)(2,1)S(1)}, u32[]{:S(2)}, u32[]{:S(2)}) collective-permute-start(bf16[2,2,8,384]{3,2,1,0:T(8,128)(2,1)S(1)} %pad_maximum_fusion.2), channel_id=1, source_target_pairs={{0,2},{1,3},{2,0},{3,1},{4,6},{5,7},{6,4},{7,5},{8,10},{9,11},{10,... | collective-permute-start | bytes 73736 | tf_op jit(solution)/shard_map/ppermute | solution.py:173
  16.4 4.3 %collective-permute-start.4 = (bf16[4,2,8,384]{3,2,1,0:T(8,128)(2,1)S(1)}, bf16[4,2,8,384]{3,2,1,0:T(8,128)(2,1)S(1)}, u32[]{:S(2)}, u32[]{:S(2)}) collective-permute-start(bf16[4,2,8,384]{3,2,1,0:T(8,128)(2,1)S(1)} %pad_maximum_fusion.1), channel_id=1, source_target_pairs={{0,4},{1,5},{2,6},{3,7},{4,0},{5,1},{6,2},{7,3},{8,12},{9,13},{10,... | collective-permute-start | bytes 147464 | tf_op jit(solution)/shard_map/ppermute | solution.py:173
  21.4 5.7 %collective-permute-start.5 = (bf16[8,2,8,384]{3,2,1,0:T(8,128)(2,1)S(1)}, bf16[8,2,8,384]{3,2,1,0:T(8,128)(2,1)S(1)}, u32[]{:S(2)}, u32[]{:S(2)}) collective-permute-start(bf16[8,2,8,384]{3,2,1,0:T(8,128)(2,1)S(1)} %pad_maximum_fusion), channel_id=1, source_target_pairs={{0,8},{1,9},{2,10},{3,11},{4,12},{5,13},{6,14},{7,15},{8,0},{9,1},... | collective-permute-start | bytes 294920 | tf_op jit(solution)/shard_map/ppermute | solution.py:173
  27.2 1.4 %copy-start = (bf16[8,256,384]{2,1,0:T(8,128)(2,1)S(1)}, bf16[8,256,384]{2,1,0:T(8,128)(2,1)}, u32[]{:S(2)}) copy-start(bf16[8,256,384]{2,1,0:T(8,128)(2,1)} %get-tuple-element.9.cols_ref) | copy-start | bytes 4718596
  28.6 1.3 %copy-start.2 = (bf16[3,3,256,256]{3,2,1,0:T(8,128)(2,1)S(1)}, bf16[3,3,256,256]{3,2,1,0:T(8,128)(2,1)}, u32[]{:S(2)}) copy-start(bf16[3,3,256,256]{3,2,1,0:T(8,128)(2,1)} %w2_ref.1) | copy-start | bytes 3538948

commit v2 on v0

v2 whole, which is shorter than its diff:
```python
import functools

import jax
import jax.numpy as jnp
from jax import lax
from jax.experimental import pallas as pl
from jax.experimental.pallas import tpu as pltpu
from jax.sharding import PartitionSpec as P

BF, F32 = jnp.bfloat16, jnp.float32
LANES, MAIN, SLOT, PIECES = 128, 256, 64, 4
WIDE = MAIN + 2 * SLOT


def gelu(value):
    return 0.5 * value * (1.0 + jnp.tanh(0.7978845608 * (value + 0.044715 * value * value * value)))


def turned(block, chans):
    rows = block.shape[-1]
    tail = block[MAIN : MAIN + SLOT]
    tail = jnp.concatenate([tail, jnp.zeros((SLOT - tail.shape[0], rows), BF)], axis=0)
    full = jnp.concatenate([block[:MAIN], tail, tail], axis=0)
    eye = (
        lax.broadcasted_iota(jnp.int32, (rows, rows), 0) == lax.broadcasted_iota(jnp.int32, (rows, rows), 1)
    ).astype(F32).astype(BF)
    return lax.dot_general(eye, full, (((1,), (1,)), ((), ())), preferred_element_type=F32)


def prepare(
    me_ref, fold_hbm, x_hbm, mask_hbm, b1_hbm, b2_hbm, outer_ref, inner_ref, cols_ref, top_ref, bias_ref, at_ref,
    x_ref, mask_ref, fold_ref, field, sem,
):
    chans, width, rows = x_ref.shape
    held = outer_ref.shape[1]
    me = me_ref[0]
    cuts = [chans * i // PIECES for i in range(PIECES + 1)]
    pairs = [(mask_hbm, mask_ref)]
    pairs += [(x_hbm.at[lo:hi], x_ref.at[lo:hi]) for lo, hi in zip(cuts, cuts[1:])]
    pairs += [(b1_hbm, bias_ref.at[0:1]), (b2_hbm, bias_ref.at[1:2]), (fold_hbm, fold_ref)]
    copies = [pltpu.make_async_copy(src, dst, sem.at[i]) for i, (src, dst) in enumerate(pairs)]
    for copy in copies:
        copy.start()
    odd = lax.rem(me, 2) == 1
    copies[0].wait()
    mask = mask_ref[...].astype(F32)
    halves = [slice(i * LANES, (i + 1) * LANES) for i in range(rows // LANES)]
    for i, at in enumerate(halves):
        field[i, chans * width : (chans + 1) * width, :] = mask[:, at]
        field[i, (chans + 1) * width :, :] = jnp.zeros(((held - chans - 1) * width, LANES), F32)
    for lo, hi, copy in zip(cuts, cuts[1:], copies[1:]):
        copy.wait()
        for i, at in enumerate(halves):
            block = x_ref[lo:hi, :, at].astype(F32) * mask[None, :, at]
            field[i, lo * width : hi * width, :] = block.reshape((hi - lo) * width, LANES)

    def column(c):
        parts = [field[i, pl.ds(c, held, stride=width), :] for i in range(rows // LANES)]
        return jnp.concatenate(parts, axis=1).astype(BF)

    for c in range(2):
        low, high = column(c), column(width - 2 + c)
        outer_ref[c] = jnp.where(odd, high, low)
        inner_ref[c, :held] = jnp.where(odd, low, high)
    last = []
    for c in range(width):
        out = turned(column(c), chans)
        cols_ref[c] = out.astype(BF)
        last.append(out[rows - 2 :])
    top = jnp.concatenate([v[i : i + 1] for i in range(2) for v in last], axis=0).astype(BF)
    top_ref[0] = top
    inner_ref[0, held:] = top[:, :rows]
    pad = jnp.zeros((2 * width, 2 * rows - WIDE), BF)
    inner_ref[1, held:] = jnp.concatenate([top[:, rows:], pad], axis=1)
    for copy in copies[1 + PIECES :]:
        copy.wait()
    total = fold_ref.shape[0]
    for j in range(16):
        src = fold_ref[lax.rem(me * width + (j - 2) + total, total)]
        at_ref[j] = lax.bitwise_xor(src // width, me) * (2 * width) + lax.rem(src, width)


def top_rows(block):
    return jnp.concatenate([block[0], block[1][:, : WIDE - MAIN]], axis=1)


def join(mine_ref, got_ref, after_ref, out_ref):
    count = mine_ref.shape[0]
    out_ref[:count] = mine_ref[...]
    if got_ref.shape == mine_ref.shape:
        out_ref[count:] = got_ref[...]
    else:
        out_ref[count] = top_rows(got_ref[:, got_ref.shape[1] - mine_ref.shape[1] :])


def mm(a, b):
    return jnp.dot(a, b, preferred_element_type=F32)


def mask_of(column, chans):
    return column[:, MAIN:].astype(F32)[:, chans - MAIN : chans - MAIN + 1]


def tail_weights(w1_ref, wt):
    chans, hidden = w1_ref.shape[2:]
    for dy in range(3):
        for dx in range(3):
            rest = jnp.concatenate(
                [w1_ref[dy, dx, MAIN:, :], jnp.zeros((SLOT - chans + MAIN, hidden), BF)], axis=0
            )
            wt[dx * SLOT : (dx + 1) * SLOT, dy * hidden : (dy + 1) * hidden] = rest
    wt[3 * SLOT :, :] = jnp.zeros((SLOT, 3 * hidden), BF)


def first_taps(columns):
    some = next(c for c in columns if c is not None)
    lanes = lax.broadcasted_iota(jnp.int32, (some.shape[0], LANES), 1)
    zero = jnp.zeros((some.shape[0], LANES), BF)
    tail = [zero if c is None else c[:, MAIN:] for c in columns]
    parts = [c[:, :MAIN] for c in columns if c is not None]
    if columns[0] is not None or columns[1] is not None:
        parts.append(jnp.where(lanes < SLOT, tail[0], tail[1]))
    if columns[2] is not None:
        parts.append(tail[2])
    return jnp.concatenate(parts, axis=1)


def first_weights(w1_ref, wt, columns, dys=(0, 1, 2)):
    hidden = w1_ref.shape[3]
    out = []
    for dy in dys:
        at = slice(dy * hidden, (dy + 1) * hidden)
        parts = [w1_ref[dy, dx, :MAIN, :] for dx in range(3) if columns[dx] is not None]
        if columns[0] is not None or columns[1] is not None:
            parts.append(wt[: 2 * SLOT, at])
        if columns[2] is not None:
            parts.append(wt[2 * SLOT :, at])
        out.append(jnp.concatenate(parts, axis=0))
    return jnp.concatenate(out, axis=1)


def second_weights(w2_ref, columns, dys=(0, 1, 2)):
    return jnp.concatenate(
        [
            jnp.concatenate([w2_ref[dy, dx] for dx in range(3) if columns[dx] is not None], axis=0)
            for dy in dys
        ],
        axis=1,
    )


def summed(p):
    rows, hidden = p.shape[0], p.shape[1] // 3
    row = lax.broadcasted_iota(jnp.int32, (rows, hidden), 0)
    south = jnp.where(row == 0, 0.0, pltpu.roll(p[:, :hidden], 1, 0))
    north = jnp.where(row == rows - 1, 0.0, pltpu.roll(p[:, 2 * hidden :], rows - 1, 0))
    return p[:, hidden : 2 * hidden] + south + north


def edges(width):
    return (0, 1, width, width + 1)


def own_column(cols_ref, j):
    return cols_ref[j - 2] if 2 <= j < 2 + cols_ref.shape[0] else None


def hidden_columns(cols_ref, w1_ref, bias_ref, wt, hid_ref, last_ref, first):
    chans, hidden = w1_ref.shape[2:]
    rows = cols_ref.shape[1]
    row = lax.broadcasted_iota(jnp.int32, (rows, hidden), 0)
    last_ref[...] = jnp.zeros_like(last_ref)
    for i in range(hid_ref.shape[0]):
        columns = [own_column(cols_ref, first + i + dx) for dx in range(3)]
        value = summed(mm(first_taps(columns), first_weights(w1_ref, wt, columns)))
        last_ref[i : i + 1, :] = value[rows - 1 :]
        value = gelu(value + bias_ref[0:1]) * mask_of(columns[1], chans)
        hid_ref[i] = jnp.where(row == rows - 1, 0.0, value).astype(BF)


def inside_a(cols_ref, w1_ref, bias_ref, hid_ref, last_ref, wt_ref):
    tail_weights(w1_ref, wt_ref)
    hidden_columns(cols_ref, w1_ref, bias_ref, wt_ref, hid_ref, last_ref, 2)


def inside_b(before, cols_ref, w1_ref, bias_ref, wt_ref, after_ref, hid_ref, last_ref, part_ref):
    hidden_columns(cols_ref, w1_ref, bias_ref, wt_ref, hid_ref, last_ref, 2 + before)
    for i, h in enumerate(edges(cols_ref.shape[0])):
        columns = [own_column(cols_ref, h + dx) for dx in range(3)]
        part_ref[i] = summed(mm(first_taps(columns), first_weights(w1_ref, wt_ref, columns)))


def inside_c(chans, hid_a, hid_b, cols_ref, w2_ref, bias_ref, after_ref, out_ref):
    width, rows, _ = cols_ref.shape
    hidden = w2_ref.shape[3]
    before = hid_a.shape[0]
    for o in range(width):
        columns = []
        for h in range(o, o + 3):
            inside = 2 <= h < width
            columns.append((hid_a[h - 2] if h - 2 < before else hid_b[h - 2 - before]) if inside else None)
        have = [c for c in columns if c is not None]
        if have:
            value = summed(mm(jnp.concatenate(have, axis=1), second_weights(w2_ref, columns)))
        else:
            value = jnp.zeros((rows, hidden), F32)
        value = value + bias_ref[1:2]
        if len(have) == 3:
            value = value * mask_of(cols_ref[o], chans)
        for i in range(hidden // LANES):
            out_ref[i, pl.ds(o, rows, stride=width), :] = value[:, i * LANES : (i + 1) * LANES]


def border(
    me_ref, cols_ref, top_ref, outer_ref, inner_ref, part_ref, last_a, last_b, outp_ref, wt, w1_ref, bias_ref, w2_ref,
    after_ref, out_hbm, slab_ref, sea_ref, line_ref, own_ref, hx, hid, outf, outb, sem,
):
    chans, hidden = w1_ref.shape[2:]
    width, rows, _ = cols_ref.shape
    held = outer_ref.shape[1]
    odd = lax.rem(me_ref[0], 2) == 1
    for c in range(2):
        hx[c] = turned(jnp.where(odd, inner_ref[c, :held], outer_ref[c]), chans).astype(BF)
        hx[2 + c] = turned(jnp.where(odd, outer_ref[c], inner_ref[c, :held]), chans).astype(BF)

    def column(j):
        return hx[j] if j < 2 else cols_ref[j - 2] if j < 2 + width else hx[j - width]

    own_ref[...] = jnp.zeros_like(own_ref)
    for j in range(width + 4):
        own_ref[j : j + 1, :] = column(j)[rows - 16 :].astype(F32)[15:16]
    bias1 = bias_ref[0:1]
    row = lax.broadcasted_iota(jnp.int32, (rows, hidden), 0)
    line_ref[...] = jnp.zeros_like(line_ref)
    line_ref[2:6] = last_a[:4]
    line_ref[6:width] = last_b[: width - 6]
    for i, h in enumerate(edges(width)):
        columns = [column(h + dx) if not 2 <= h + dx < 2 + width else None for dx in range(3)]
        value = part_ref[i] + summed(mm(first_taps(columns), first_weights(w1_ref, wt, columns)))
        line_ref[h : h + 1, :] = value[rows - 1 :]
        value = gelu(value + bias1) * mask_of(column(h + 1), chans)
        hid[i] = jnp.where(row == rows - 1, 0.0, value).astype(BF)
    for o in (0, 1, width - 2, width - 1):
        columns = [hid[edges(width).index(o + dx)] if o + dx in edges(width) else None for dx in range(3)]
        have = [c for c in columns if c is not None]
        value = summed(mm(jnp.concatenate(have, axis=1), second_weights(w2_ref, columns)))
        mask = mask_of(cols_ref[o], chans)
        for i in range(hidden // LANES):
            at = (i, pl.ds(o, rows, stride=width), slice(None))
            outf[at] = (outp_ref[at] + value[:, i * LANES : (i + 1) * LANES]) * mask
    step = rows // PIECES
    place = lax.rem(lax.broadcasted_iota(jnp.int32, (step * width, LANES), 0), width)
    edge = (place < 2) | (place >= width - 2)
    copies = []
    for p in range(PIECES):
        at = slice(p * step * width, (p + 1) * step * width)
        for i in range(hidden // LANES):
            lanes = slice(i * LANES, (i + 1) * LANES)
            value = jnp.where(edge, outf[i, at], outp_ref[i, at])
            outb[p * step : (p + 1) * step, :, lanes] = value.reshape(step, width, LANES).astype(BF)
            if p == PIECES - 1:
                slab_ref[:, lanes] = value[(step - 2) * width :]
        here = slice(p * step, (p + 1) * step)
        copies.append(pltpu.make_async_copy(outb.at[here], out_hbm.at[here], sem.at[p]))
        copies[-1].start()
    sea = mask_of(top_ref[0], chans)
    sea_ref[...] = jnp.broadcast_to(sea, sea_ref.shape)
    for copy in copies:
        copy.wait()


def fold(
    at_ref, tops_ref, slab_ref, sea_ref, line_ref, own_ref, wt, w1_ref, bias_ref, w2_ref, old_hbm,
    out_hbm, gf, m0, m1, r2, gs, hg, hz, outb, sem,
):
    chans, hidden = w1_ref.shape[2:]
    rows, width, _ = out_hbm.shape
    bias1 = bias_ref[0:1]
    gf[...] = tops_ref[...].astype(F32).reshape(gf.shape)
    for ref in (m0, m1, r2, gs):
        ref[...] = jnp.zeros_like(ref)
    lane = lax.broadcasted_iota(jnp.int32, (1, WIDE), 1)
    sign = jnp.where(lane < chans // 2, -1.0, 1.0).astype(F32)
    for j in range(width + 4):
        at = at_ref[j]
        m0[j : j + 1, :] = gf[pl.ds(at, 1), :]
        north = gf[pl.ds(at + width, 1), :]
        m1[j : j + 1, :] = north
        gs[j : j + 1, :] = north * sign
    r2[...] = own_ref[...] * sign

    def taps(ref, offsets):
        return first_taps([ref[o : o + 16, :].astype(BF) for o in offsets])

    every = (0, 0, 0)
    mixed = mm(
        jnp.concatenate([taps(gs, (0, 1, 2)), taps(r2, (2, 1, 0))], axis=0), first_weights(w1_ref, wt, every, (2,))
    )
    pre = mixed[16:]
    pre += mm(taps(m0, (2, 1, 0)), first_weights(w1_ref, wt, every, (0,)))
    pre += mm(taps(m1, (2, 1, 0)), first_weights(w1_ref, wt, every, (1,)))
    hg[...] = jnp.zeros_like(hg)
    hg[:16, :] = gelu(pre + bias1) * m1[1:17, chans : chans + 1]
    hz[...] = jnp.zeros_like(hz)
    hz[:16, :] = gelu(line_ref[...] + mixed[:16] + bias1) * own_ref[1:17, chans : chans + 1]
    wide = [jnp.concatenate([ref[o : o + 16, :].astype(BF) for o in range(3)], axis=1) for ref in (hz, hg)]
    more = mm(jnp.concatenate(wide, axis=0), second_weights(w2_ref, every, (1, 2)))
    below = more[:width, hidden:]
    level = more[:width, :hidden] + more[16 : 16 + width, hidden:]
    value = slab_ref[...] + jnp.concatenate([below, level], axis=0) * sea_ref[...]
    outb[...] = value.reshape(2, width, hidden).astype(BF)
    copy = pltpu.make_async_copy(outb, out_hbm.at[rows - 2 : rows], sem)
    copy.start()
    copy.wait()


def local(state, ocean_mask, fold_map, w_first, b_first, w_second, b_second):
    rows, width, chans = state.shape
    hidden = w_first.shape[-1]
    n = lax.axis_size("lon")
    me = lax.axis_index("lon")
    assert n & (n - 1) == 0 and MAIN <= chans < MAIN + SLOT and chans // 2 <= MAIN and width == 8 and rows == MAIN
    held = -(-(chans + 1) // 16) * 16
    smem = pl.BlockSpec(memory_space=pltpu.SMEM)
    vmem = pl.BlockSpec(memory_space=pltpu.VMEM)
    hbm = pl.BlockSpec(memory_space=pltpu.MemorySpace.HBM)
    shape = jax.ShapeDtypeStruct
    scratch = pltpu.VMEM
    dma = pltpu.SemaphoreType.DMA
    place = jnp.full((1,), me, jnp.int32)

    def limit(mib):
        return pltpu.CompilerParams(vmem_limit_bytes=mib << 20)

    def far(value):
        return pltpu.with_memory_space_constraint(value, pltpu.MemorySpace.HBM)

    sent, inner, cols, top, bias, at = pl.pallas_call(
        prepare,
        out_shape=(
            shape((2, held, rows), BF),
            shape((2, held + 2 * width, rows), BF),
            shape((width, rows, WIDE), BF),
            shape((1, 2 * width, WIDE), BF),
            shape((2, hidden), F32),
            shape((16,), jnp.int32),
        ),
        in_specs=[smem] + [hbm] * 5,
        out_specs=(vmem,) * 5 + (smem,),
        scratch_shapes=[
            scratch((chans, width, rows), BF),
            scratch((width, rows), jnp.int32),
            pltpu.SMEM(fold_map.shape, jnp.int32),
            scratch((rows // LANES, held * width, LANES), F32),
            dma((PIECES + 4,)),
        ],
        compiler_params=limit(14),
        name="prepare",
    )(
        place, far(fold_map), far(state.transpose(2, 1, 0)), far(ocean_mask.T),
        far(b_first[None]), far(b_second[None]),
    )
    outer = lax.ppermute(sent, "lon", [(i, (i + 1 if i % 2 else i - 1) % n) for i in range(n)])
    inner = lax.ppermute(inner, "lon", [(i, i ^ 1) for i in range(n)])

    def joined(mine, got, after):
        return pl.pallas_call(
            join,
            out_shape=shape((2 * mine.shape[0],) + mine.shape[1:], BF),
            in_specs=[vmem] * 3,
            out_specs=vmem,
            compiler_params=limit(4),
            name="join",
        )(mine, got, after)

    before = 4
    hid_a, last_a, wt = pl.pallas_call(
        inside_a,
        out_shape=(
            shape((before, rows, hidden), BF),
            shape((8, hidden), F32),
            shape((4 * SLOT, 3 * hidden), BF),
        ),
        in_specs=[vmem] * 3,
        out_specs=(vmem,) * 3,
        compiler_params=limit(12),
        name="inside_a",
    )(cols, w_first, bias)

    def stage_b(after):
        return pl.pallas_call(
            functools.partial(inside_b, before),
            out_shape=(
                shape((width - 2 - before, rows, hidden), BF),
                shape((8, hidden), F32),
                shape((4, rows, hidden), F32),
            ),
            in_specs=[vmem] * 5,
            out_specs=(vmem,) * 3,
            compiler_params=limit(12),
            name="inside_b",
        )(cols, w_first, bias, wt, after)

    def stage_c(hid_b, after):
        return pl.pallas_call(
            functools.partial(inside_c, chans),
            out_shape=shape((hidden // LANES, rows * width, LANES), F32),
            in_specs=[vmem] * 6,
            out_specs=vmem,
            compiler_params=limit(12),
            name="inside_c",
        )(hid_a, hid_b, cols, w_second, bias, after)

    tops = joined(top, inner, last_a)
    step, stage, after = 2, 0, tops
    while step < n:
        got = lax.ppermute(tops, "lon", [(i, i ^ step) for i in range(n)])
        if stage == 0:
            hid_b, last_b, part = stage_b(tops)
            after = last_b
        elif stage == 1:
            outp = stage_c(hid_b, tops)
            after = outp
        else:
            after = tops
        if stage < 2:
            tops = joined(tops, got, after)
        else:
            late, final = tops, got
            tops = None
        step, stage = 2 * step, stage + 1
        if tops is None:
            if step < n:
                tops = joined(late, final, late)
    out, slab, sea, line, own = pl.pallas_call(
        border,
        out_shape=(
            shape((rows, width, hidden), BF),
            shape((2 * width, hidden), F32),
            shape((2 * width, hidden), F32),
            shape((16, hidden), F32),
            shape((24, WIDE), F32),
        ),
        in_specs=[smem] + [vmem] * 13,
        out_specs=(hbm,) + (vmem,) * 4,
        scratch_shapes=[
            scratch((4, rows, WIDE), BF),
            scratch((4, rows, hidden), BF),
            scratch((hidden // LANES, rows * width, LANES), F32),
            scratch((rows, width, hidden), BF),
            dma((PIECES,)),
        ],
        compiler_params=limit(16),
        name="border",
    )(place, cols, top, outer, inner, part, last_a, last_b, outp, wt, w_first, bias, w_second, late)
    tops = joined(late, final, line)
    return pl.pallas_call(
        fold,
        out_shape=shape((rows, width, hidden), BF),
        in_specs=[smem] + [vmem] * 9 + [hbm],
        out_specs=hbm,
        scratch_shapes=[scratch((n * 2 * width, WIDE), F32)]
        + [scratch((24, WIDE), F32)] * 4
        + [scratch((24, hidden), F32)] * 2
        + [scratch((2, width, hidden), BF), dma],
        input_output_aliases={10: 0},
        compiler_params=limit(10),
        name="fold",
    )(at, tops, slab, sea, line, own, wt, w_first, bias, w_second, out)


def solution(mesh):
    return jax.shard_map(
        local,
        mesh=mesh,
        in_specs=(P(None, ("grp", "lon"), None), P(None, "lon"), P(), P(), P(), P(), P()),
        out_specs=P(None, ("grp", "lon"), None),
        check_vma=False,
    )
```

time: 119 us -> 29.4 us (0.25)
  blocking collectives: 39.7 us -> 0 us
  local copies, waits for them, and re-layouts: 33.1 us -> 1.36 us
  matrix products: 27.8 us -> 0 us
  Pallas kernels: 0 us -> 15 us
  other arithmetic: 7.89 us -> 0 us
  waiting for transfers between devices: 0.01 us -> 4.28 us
  starting transfers between devices: 9.97 us -> 8.45 us
    all_gather x2 -> x0, blocking collectives: 39.7 us -> none  [the longest x1 20.3 us: local(): top_state = lax.all_gather(masked[rows - 1], 'lon', axis=0, tiled=True)]
    dot_general x18 -> x0, matrix products: 27.8 us -> none  [conv_taps(): jnp.dot(tap, weight[shift_y, shift_x], preferred_element_type=jnp.float32)]
    slice x13 -> x0, local copies, waits for them, and re-layouts: 23.5 us -> none  [the longest x9 21.9 us: conv_taps(): padded[shift_y:shift_y + rows, shift_x:shift_x + cols]]
    pallas_call x0 -> x10, Pallas kernels: none -> 15 us  [the longest x1 3.67 us: local(): pl.pallas_call(border, out_shape=(shape((rows, width, hidden), BF), shape...]
    concatenate x3 -> x0, other arithmetic: 6.56 us -> none  [the longest x2 4.51 us: extended(): array = jnp.concatenate([before, array, after], axis=dim)]
    ppermute x4 -> x5, waiting for transfers between devices: 0.01 us -> 4.28 us  [the longest x3 4.27 us: local(): got = lax.ppermute(tops, 'lon', [(i, i ^ step) for i in range(n)])]
    mul x3 -> x0, local copies, waits for them, and re-layouts: 2.48 us -> none  [the longest x1 1.24 us: local(): ghost = fold_ghost(top_state, fold_map, start, 1, width) * signs]
    ppermute x2 -> x0, local copies, waits for them, and re-layouts: 2.44 us -> none  [the longest x1 1.22 us: extended(): before = lax.ppermute(last, axis, up)]
  transfers between devices with their start and end apart: 4 -> 5, of which waited for: 0 -> 3; matrix products, arithmetic and copies ran while one was open for 7% -> 0% of each run, Pallas kernels for 0% -> 34%
where the time goes in v2:
time: 29.4 us; the launch traced here: 29.2 us
  Pallas kernels  15 us (51%)
  starting transfers between devices  8.45 us (29%)
  waiting for transfers between devices  4.28 us (15%)
  local copies, waits for them, and re-layouts  1.36 us (5%)
    ppermute x1, starting transfers between devices, local(): lax.ppermute(sent, 'lon', [(i, (i + 1 if i % 2 else i - 1) % n) for i in...  5.66 us
    ppermute x3, waiting for transfers between devices, local(): got = lax.ppermute(tops, 'lon', [(i, i ^ step) for i in range(n)])  4.27 us
    pallas_call x1, Pallas kernels, local(): pl.pallas_call(border, out_shape=(shape((rows, width, hidden), BF), shape...  3.67 us
    pallas_call x1, Pallas kernels, local(): pl.pallas_call(prepare, out_shape=(shape((2, held, rows), BF), shape((2,...  3.12 us
    ppermute x3, starting transfers between devices, local(): got = lax.ppermute(tops, 'lon', [(i, i ^ step) for i in range(n)])  2.24 us
    pallas_call x1, Pallas kernels, stage_c(): pl.pallas_call(functools.partial(inside_c, chans), out_shape=shape((hidde...  2.22 us
    pallas_call x1, Pallas kernels, stage_b(): pl.pallas_call(functools.partial(inside_b, before), out_shape=(shape((wid...  2.11 us
    pallas_call x1, Pallas kernels, local(): pl.pallas_call(inside_a, out_shape=(shape((before, rows, hidden), BF), sh...  1.99 us
  transfers between devices with their start and end apart: 5, of which 3 were waited for; matrix products, arithmetic and copies ran while one was open for 0% of the time, Pallas kernels for 34%

profile of v2, /device:TPU:0, one launch (start us, length us, event | category | flops | bytes accessed | tf_op | source)
XLA Modules:
  0.0 29.2 jit_solution(4031282238152044095)
XLA Ops:
  0.0 3.1 %prepare.1 = (bf16[2,304,256]{2,1,0:T(8,128)(2,1)S(1)}, bf16[2,320,256]{2,1,0:T(8,128)(2,1)S(1)}, bf16[8,256,384]{2,1,0:T(8,128)(2,1)S(1)}, bf16[1,16,384]{2,1,0...) custom-call(s32[1]{0:T(128)} %bitcast.me_ref, s32[128]{0:T(128)} %fold_hbm.1, bf16[300,8,256]{2,1,0:T(8,128)(2,1)} %bitcast.5, ...), custom_call_target="tpu_custom_call" | custom-call | tf_op jit(solution)/shard_map/prepare/pallas_call | solution.py:338
  3.1 0.6 %collective-permute-start = (bf16[2,320,256]{2,1,0:T(8,128)(2,1)S(1)}, bf16[2,320,256]{2,1,0:T(8,128)(2,1)S(1)}, u32[]{:S(2)}, u32[]{:S(2)}) collective-permute-start(bf16[2,320,256]{2,1,0:T(8,128)(2,1)S(1)} %get-tuple-element.24), channel_id=1, source_target_pairs={{0,1},{1,0},{2,3},{3,2},{4,5},{5,4},{6,7},{7,6},{8,9},{9,8},{10,11... | collective-permute-start | bytes 983048 | tf_op jit(solution)/shard_map/ppermute | solution.py:364
  3.7 5.7 %collective-permute-start.4 = (bf16[2,304,256]{2,1,0:T(8,128)(2,1)S(1)}, bf16[2,304,256]{2,1,0:T(8,128)(2,1)S(1)}, u32[]{:S(2)}, u32[]{:S(2)}) collective-permute-start(bf16[2,304,256]{2,1,0:T(8,128)(2,1)S(1)} %get-tuple-element.32), channel_id=1, source_target_pairs={{0,15},{1,2},{2,1},{3,4},{4,3},{5,6},{6,5},{7,8},{8,7},{9,10},{10,... | collective-permute-start | bytes 933896 | tf_op jit(solution)/shard_map/ppermute | solution.py:363
  9.3 0.0 copy-start
  9.3 1.3 %copy-done = bf16[3,3,300,256]{3,2,1,0:T(8,128)(2,1)S(1)} copy-done((bf16[3,3,300,256]{3,2,1,0:T(8,128)(2,1)S(1)}, bf16[3,3,300,256]{3,2,1,0:T(8,128)(2,1)}, u32[]{:S(2)}) %copy-start) | copy-done | bytes 1382424
  10.7 2.0 %inside_a.1 = (bf16[4,256,256]{2,1,0:T(8,128)(2,1)S(1)}, f32[8,256]{1,0:T(8,128)S(1)}, bf16[256,768]{1,0:T(8,128)(2,1)S(1)}) custom-call(bf16[8,256,384]{2,1,0:T(8,128)(2,1)S(1)} %get-tuple-element.25.cols_ref, bf16[3,3,300,256]{3,2,1,0:T(8,128)(2,1)S(1)} %copy-done, f32[2,256]{1,0:T(2,128)S(1)} %get-tuple-element.26.bias_ref), custom_call_target="tpu_custom_call" | custom-call | tf_op jit(solution)/shard_map/inside_a/pallas_call | solution.py:377
  12.7 0.0 collective-permute-done.got_ref.inner_ref
  12.7 0.1 collective-permute-start.1
  12.8 0.0 copy-start.2
  12.8 2.1 %inside_b.1 = (bf16[2,256,256]{2,1,0:T(8,128)(2,1)S(1)}, f32[8,256]{1,0:T(8,128)S(1)}, f32[4,256,256]{2,1,0:T(8,128)S(1)}) custom-call(bf16[8,256,384]{2,1,0:T(8,128)(2,1)S(1)} %get-tuple-element.25.cols_ref, bf16[3,3,300,256]{3,2,1,0:T(8,128)(2,1)S(1)} %copy-done, f32[2,256]{1,0:T(2,128)S(1)} %get-tuple-element.26.bias_ref, ...), custom_call_target="tpu_custom_call" | custom-call | tf_op jit(solution)/shard_map/inside_b/pallas_call | solution.py:391
  14.9 1.7 %collective-permute-done.1.got_ref = bf16[2,16,384]{2,1,0:T(8,128)(2,1)S(1)} collective-permute-done((bf16[2,16,384]{2,1,0:T(8,128)(2,1)S(1)}, bf16[2,16,384]{2,1,0:T(8,128)(2,1)S(1)}, u32[]{:S(2)}, u32[]{:S(2)}) %collective-permute-start.1) | collective-permute-done | bytes 24608 | tf_op jit(solution)/shard_map/ppermute | solution.py:417
  16.6 0.5 %collective-permute-start.2 = (bf16[4,16,384]{2,1,0:T(8,128)(2,1)S(1)}, bf16[4,16,384]{2,1,0:T(8,128)(2,1)S(1)}, u32[]{:S(2)}, u32[]{:S(2)}) collective-permute-start(bf16[4,16,384]{2,1,0:T(8,128)(2,1)S(1)} %join.5.after_ref.mine_ref), channel_id=1, source_target_pairs={{0,4},{1,5},{2,6},{3,7},{4,0},{5,1},{6,2},{7,3},{8,12},{9,13},{10,... | collective-permute-start | bytes 147464 | tf_op jit(solution)/shard_map/ppermute | solution.py:417
  17.1 0.0 copy-done.2
  17.1 2.2 %inside_c.1.after_ref.outp_ref = f32[2,2048,128]{2,1,0:T(8,128)S(1)} custom-call(bf16[4,256,256]{2,1,0:T(8,128)(2,1)S(1)} %get-tuple-element.30.hid_a, bf16[2,256,256]{2,1,0:T(8,128)(2,1)S(1)} %get-tuple-element.31.hid_b, bf16[8,256,384]{2,1,0:T(8,128)(2,1)S(1)} %get-tuple-element.25.cols_ref, bf16[3,3,256,256]{3,2,1,0:T(8,128)(2,1)S(1)} %copy-done.2, ...), custom_call_target="tpu_custom_call" | custom-call | tf_op jit(solution)/shard_map/inside_c/pallas_call | solution.py:405
  19.4 0.0 copy-start.1
  19.4 1.3 %collective-permute-done.2.got_ref = bf16[4,16,384]{2,1,0:T(8,128)(2,1)S(1)} collective-permute-done((bf16[4,16,384]{2,1,0:T(8,128)(2,1)S(1)}, bf16[4,16,384]{2,1,0:T(8,128)(2,1)S(1)}, u32[]{:S(2)}, u32[]{:S(2)}) %collective-permute-start.2) | collective-permute-done | bytes 49184 | tf_op jit(solution)/shard_map/ppermute | solution.py:417
  20.7 1.6 %collective-permute-start.3 = (bf16[8,16,384]{2,1,0:T(8,128)(2,1)S(1)}, bf16[8,16,384]{2,1,0:T(8,128)(2,1)S(1)}, u32[]{:S(2)}, u32[]{:S(2)}) collective-permute-start(bf16[8,16,384]{2,1,0:T(8,128)(2,1)S(1)} %join.6.after_ref.mine_ref), channel_id=1, source_target_pairs={{0,8},{1,9},{2,10},{3,11},{4,12},{5,13},{6,14},{7,15},{8,0},{9,1},... | collective-permute-start | bytes 294920 | tf_op jit(solution)/shard_map/ppermute | solution.py:417
  22.4 0.0 collective-permute-done.4.outer_ref
  22.4 0.0 copy-done.1
  22.4 3.7 %border.1 = (bf16[256,8,256]{2,1,0:T(8,128)(2,1)}, f32[16,256]{1,0:T(8,128)S(1)}, f32[16,256]{1,0:T(8,128)S(1)}, f32[16,256]{1,0:T(8,128)S(1)}, f32[24,384]{1,0:T(8,128)S(1)}) custom-call(s32[1]{0:T(128)} %bitcast.me_ref, bf16[8,256,384]{2,1,0:T(8,128)(2,1)S(1)} %get-tuple-element.25.cols_ref, bf16[1,16,384]{2,1,0:T(8,128)(2,1)S(1)} %get-tuple-element.23.mine_ref.top_ref, ...), custom_call_target="tpu_custom_call" | custom-call | tf_op jit(solution)/shard_map/border/pallas_call | solution.py:435
  26.0 1.3 %collective-permute-done.3.got_ref = bf16[8,16,384]{2,1,0:T(8,128)(2,1)S(1)} collective-permute-done((bf16[8,16,384]{2,1,0:T(8,128)(2,1)S(1)}, bf16[8,16,384]{2,1,0:T(8,128)(2,1)S(1)}, u32[]{:S(2)}, u32[]{:S(2)}) %collective-permute-start.3) | collective-permute-done | bytes 98336 | tf_op jit(solution)/shard_map/ppermute | solution.py:417
  27.3 1.9 %fold.1 = bf16[256,8,256]{2,1,0:T(8,128)(2,1)} custom-call(s32[16]{0:T(128)S(1)} %get-tuple-element.22.at_ref, bf16[16,16,384]{2,1,0:T(8,128)(2,1)S(1)} %join.7.tops_ref, f32[16,256]{1,0:T(8,128)S(1)} %get-tuple-element.35.slab_ref, f32[16,256]{1,0:T(8,128)S(1)} %get-tuple-element.36.sea_ref, ...), custom_call_target="tpu_custom_call", output_to_operand_aliasing={{}: (10, {})} | custom-call | tf_op jit(solution)/shard_map/fold/pallas_call | solution.py:457
  (4 shorter events, 0.0 us)
Async XLA Ops:
  3.1 9.6 %collective-permute-start = (bf16[2,320,256]{2,1,0:T(8,128)(2,1)S(1)}, bf16[2,320,256]{2,1,0:T(8,128)(2,1)S(1)}, u32[]{:S(2)}, u32[]{:S(2)}) collective-permute-start(bf16[2,320,256]{2,1,0:T(8,128)(2,1)S(1)} %get-tuple-element.24), channel_id=1, source_target_pairs={{0,1},{1,0},{2,3},{3,2},{4,5},{5,4},{6,7},{7,6},{8,9},{9,8},{10,11... | collective-permute-start | bytes 983048 | tf_op jit(solution)/shard_map/ppermute | solution.py:364
  3.7 18.7 %collective-permute-start.4 = (bf16[2,304,256]{2,1,0:T(8,128)(2,1)S(1)}, bf16[2,304,256]{2,1,0:T(8,128)(2,1)S(1)}, u32[]{:S(2)}, u32[]{:S(2)}) collective-permute-start(bf16[2,304,256]{2,1,0:T(8,128)(2,1)S(1)} %get-tuple-element.32), channel_id=1, source_target_pairs={{0,15},{1,2},{2,1},{3,4},{4,3},{5,6},{6,5},{7,8},{8,7},{9,10},{10,... | collective-permute-start | bytes 933896 | tf_op jit(solution)/shard_map/ppermute | solution.py:363
  9.3 1.3 %copy-start = (bf16[3,3,300,256]{3,2,1,0:T(8,128)(2,1)S(1)}, bf16[3,3,300,256]{3,2,1,0:T(8,128)(2,1)}, u32[]{:S(2)}) copy-start(bf16[3,3,300,256]{3,2,1,0:T(8,128)(2,1)} %w1_ref.7) | copy-start | bytes 4147204
  12.7 3.9 %collective-permute-start.1 = (bf16[2,16,384]{2,1,0:T(8,128)(2,1)S(1)}, bf16[2,16,384]{2,1,0:T(8,128)(2,1)S(1)}, u32[]{:S(2)}, u32[]{:S(2)}) collective-permute-start(bf16[2,16,384]{2,1,0:T(8,128)(2,1)S(1)} %join.4.after_ref.mine_ref), channel_id=1, source_target_pairs={{0,2},{1,3},{2,0},{3,1},{4,6},{5,7},{6,4},{7,5},{8,10},{9,11},{10,... | collective-permute-start | bytes 73736 | tf_op jit(solution)/shard_map/ppermute | solution.py:417
  12.8 4.3 %copy-start.2 = (bf16[3,3,256,256]{3,2,1,0:T(8,128)(2,1)S(1)}, bf16[3,3,256,256]{3,2,1,0:T(8,128)(2,1)}, u32[]{:S(2)}) copy-start(bf16[3,3,256,256]{3,2,1,0:T(8,128)(2,1)} %w2_ref.5) | copy-start | bytes 3538948
  16.6 4.1 %collective-permute-start.2 = (bf16[4,16,384]{2,1,0:T(8,128)(2,1)S(1)}, bf16[4,16,384]{2,1,0:T(8,128)(2,1)S(1)}, u32[]{:S(2)}, u32[]{:S(2)}) collective-permute-start(bf16[4,16,384]{2,1,0:T(8,128)(2,1)S(1)} %join.5.after_ref.mine_ref), channel_id=1, source_target_pairs={{0,4},{1,5},{2,6},{3,7},{4,0},{5,1},{6,2},{7,3},{8,12},{9,13},{10,... | collective-permute-start | bytes 147464 | tf_op jit(solution)/shard_map/ppermute | solution.py:417
  19.4 3.0 %copy-start.1 = (bf16[3,3,300,256]{3,2,1,0:T(8,128)(2,1)S(1)}, bf16[3,3,300,256]{3,2,1,0:T(8,128)(2,1)}, u32[]{:S(2)}) copy-start(bf16[3,3,300,256]{3,2,1,0:T(8,128)(2,1)} %w1_ref.7) | copy-start | bytes 4147204
  20.7 6.6 %collective-permute-start.3 = (bf16[8,16,384]{2,1,0:T(8,128)(2,1)S(1)}, bf16[8,16,384]{2,1,0:T(8,128)(2,1)S(1)}, u32[]{:S(2)}, u32[]{:S(2)}) collective-permute-start(bf16[8,16,384]{2,1,0:T(8,128)(2,1)S(1)} %join.6.after_ref.mine_ref), channel_id=1, source_target_pairs={{0,8},{1,9},{2,10},{3,11},{4,12},{5,13},{6,14},{7,15},{8,0},{9,1},... | collective-permute-start | bytes 294920 | tf_op jit(solution)/shard_map/ppermute | solution.py:417

commit v3 on v2

--- a/solution.py
+++ b/solution.py
@@ -16,7 +16,7 @@
     return 0.5 * value * (1.0 + jnp.tanh(0.7978845608 * (value + 0.044715 * value * value * value)))
 
 
-def turned(block, chans):
+def turned(block):
     rows = block.shape[-1]
     tail = block[MAIN : MAIN + SLOT]
     tail = jnp.concatenate([tail, jnp.zeros((SLOT - tail.shape[0], rows), BF)], axis=0)
@@ -28,7 +28,8 @@
 
 
 def prepare(
-    me_ref, fold_hbm, x_hbm, mask_hbm, b1_hbm, b2_hbm, outer_ref, inner_ref, cols_ref, top_ref, bias_ref, at_ref,
+    me_ref, fold_hbm, x_hbm, mask_hbm, b1_hbm, b2_hbm, w1_hbm, w2_hbm,
+    outer_ref, inner_ref, cols_ref, top_ref, bias_ref, at_ref, w1_ref, w2_ref,
     x_ref, mask_ref, fold_ref, field, sem,
 ):
     chans, width, rows = x_ref.shape
@@ -38,6 +39,7 @@
     pairs = [(mask_hbm, mask_ref)]
     pairs += [(x_hbm.at[lo:hi], x_ref.at[lo:hi]) for lo, hi in zip(cuts, cuts[1:])]
     pairs += [(b1_hbm, bias_ref.at[0:1]), (b2_hbm, bias_ref.at[1:2]), (fold_hbm, fold_ref)]
+    pairs += [(w1_hbm, w1_ref), (w2_hbm, w2_ref)]
     copies = [pltpu.make_async_copy(src, dst, sem.at[i]) for i, (src, dst) in enumerate(pairs)]
     for copy in copies:
         copy.start()
@@ -64,7 +66,7 @@
         inner_ref[c, :held] = jnp.where(odd, low, high)
     last = []
     for c in range(width):
-        out = turned(column(c), chans)
+        out = turned(column(c))
         cols_ref[c] = out.astype(BF)
         last.append(out[rows - 2 :])
     top = jnp.concatenate([v[i : i + 1] for i in range(2) for v in last], axis=0).astype(BF)
@@ -75,22 +77,43 @@
     for copy in copies[1 + PIECES :]:
         copy.wait()
     total = fold_ref.shape[0]
+    n = total // width
+    start = lax.rem(fold_ref[0] - (width + 1) + total, total) // width
     for j in range(16):
         src = fold_ref[lax.rem(me * width + (j - 2) + total, total)]
-        at_ref[j] = lax.bitwise_xor(src // width, me) * (2 * width) + lax.rem(src, width)
+        block = lax.rem(src // width - start + me + 2 * n, n)
+        at_ref[j] = lax.rem(block, 3) * (2 * width) + lax.rem(src, width)
+    peer = lax.bitwise_xor(me, n // 2)
+    for j in range(3):
+        theirs = lax.bitwise_xor(lax.rem(start - peer + j + n, n), me)
+        mine = lax.bitwise_xor(lax.rem(start - me + j + n, n), me)
+        at_ref[16 + j] = lax.rem(theirs, n // 2)
+        at_ref[19 + j] = lax.rem(mine, n // 2)
+        at_ref[22 + j] = mine // (n // 2)
 
 
 def top_rows(block):
     return jnp.concatenate([block[0], block[1][:, : WIDE - MAIN]], axis=1)
 
 
-def join(mine_ref, got_ref, after_ref, out_ref):
+def join_first(mine_ref, got_ref, after_ref, sent_ref, out_ref, pass_ref):
+    out_ref[0] = mine_ref[0]
+    out_ref[1] = top_rows(got_ref[:, got_ref.shape[1] - mine_ref.shape[1] :])
+
+
+def join(mine_ref, got_ref, out_ref):
     count = mine_ref.shape[0]
     out_ref[:count] = mine_ref[...]
-    if got_ref.shape == mine_ref.shape:
-        out_ref[count:] = got_ref[...]
-    else:
-        out_ref[count] = top_rows(got_ref[:, got_ref.shape[1] - mine_ref.shape[1] :])
+    out_ref[count:] = got_ref[...]
+
+
+def choose(at_ref, mine_ref, got_ref, after_ref, send_ref, keep_ref, blocks):
+    count = mine_ref.shape[0]
+    blocks[:count] = mine_ref[...]
+    blocks[count:] = got_ref[...]
+    for j in range(3):
+        send_ref[j] = blocks[at_ref[16 + j]]
+        keep_ref[j] = blocks[at_ref[19 + j]]
 
 
 def mm(a, b):
@@ -220,8 +243,8 @@
     held = outer_ref.shape[1]
     odd = lax.rem(me_ref[0], 2) == 1
     for c in range(2):
-        hx[c] = turned(jnp.where(odd, inner_ref[c, :held], outer_ref[c]), chans).astype(BF)
-        hx[2 + c] = turned(jnp.where(odd, outer_ref[c], inner_ref[c, :held]), chans).astype(BF)
+        hx[c] = turned(jnp.where(odd, inner_ref[c, :held], outer_ref[c])).astype(BF)
+        hx[2 + c] = turned(jnp.where(odd, outer_ref[c], inner_ref[c, :held])).astype(BF)
 
     def column(j):
         return hx[j] if j < 2 else cols_ref[j - 2] if j < 2 + width else hx[j - width]
@@ -270,13 +293,15 @@
 
 
 def fold(
-    at_ref, tops_ref, slab_ref, sea_ref, line_ref, own_ref, wt, w1_ref, bias_ref, w2_ref, old_hbm,
+    at_ref, keep_ref, got_ref, slab_ref, sea_ref, line_ref, own_ref, wt, w1_ref, bias_ref, w2_ref, old_hbm,
     out_hbm, gf, m0, m1, r2, gs, hg, hz, outb, sem,
 ):
     chans, hidden = w1_ref.shape[2:]
     rows, width, _ = out_hbm.shape
     bias1 = bias_ref[0:1]
-    gf[...] = tops_ref[...].astype(F32).reshape(gf.shape)
+    for j in range(3):
+        block = jnp.where(at_ref[22 + j] == 0, keep_ref[j], got_ref[j])
+        gf[j * 2 * width : (j + 1) * 2 * width] = block.astype(F32)
     for ref in (m0, m1, r2, gs):
         ref[...] = jnp.zeros_like(ref)
     lane = lax.broadcasted_iota(jnp.int32, (1, WIDE), 1)
@@ -319,7 +344,7 @@
     hidden = w_first.shape[-1]
     n = lax.axis_size("lon")
     me = lax.axis_index("lon")
-    assert n & (n - 1) == 0 and MAIN <= chans < MAIN + SLOT and chans // 2 <= MAIN and width == 8 and rows == MAIN
+    assert n >= 8 and n & (n - 1) == 0 and MAIN <= chans < MAIN + SLOT and chans // 2 <= MAIN and width == 8 and rows == MAIN
     held = -(-(chans + 1) // 16) * 16
     smem = pl.BlockSpec(memory_space=pltpu.SMEM)
     vmem = pl.BlockSpec(memory_space=pltpu.VMEM)
@@ -335,7 +360,7 @@
     def far(value):
         return pltpu.with_memory_space_constraint(value, pltpu.MemorySpace.HBM)
 
-    sent, inner, cols, top, bias, at = pl.pallas_call(
+    sent, inner, cols, top, bias, at, w_first, w_second = pl.pallas_call(
         prepare,
         out_shape=(
             shape((2, held, rows), BF),
@@ -343,35 +368,26 @@
             shape((width, rows, WIDE), BF),
             shape((1, 2 * width, WIDE), BF),
             shape((2, hidden), F32),
-            shape((16,), jnp.int32),
+            shape((32,), jnp.int32),
+            shape(w_first.shape, BF),
+            shape(w_second.shape, BF),
         ),
-        in_specs=[smem] + [hbm] * 5,
-        out_specs=(vmem,) * 5 + (smem,),
+        in_specs=[smem] + [hbm] * 7,
+        out_specs=(vmem,) * 5 + (smem, vmem, vmem),
         scratch_shapes=[
             scratch((chans, width, rows), BF),
             scratch((width, rows), jnp.int32),
             pltpu.SMEM(fold_map.shape, jnp.int32),
             scratch((rows // LANES, held * width, LANES), F32),
-            dma((PIECES + 4,)),
+            dma((PIECES + 6,)),
         ],
         compiler_params=limit(14),
         name="prepare",
     )(
         place, far(fold_map), far(state.transpose(2, 1, 0)), far(ocean_mask.T),
-        far(b_first[None]), far(b_second[None]),
+        far(b_first[None]), far(b_second[None]), far(w_first), far(w_second),
     )
-    outer = lax.ppermute(sent, "lon", [(i, (i + 1 if i % 2 else i - 1) % n) for i in range(n)])
     inner = lax.ppermute(inner, "lon", [(i, i ^ 1) for i in range(n)])
-
-    def joined(mine, got, after):
-        return pl.pallas_call(
-            join,
-            out_shape=shape((2 * mine.shape[0],) + mine.shape[1:], BF),
-            in_specs=[vmem] * 3,
-            out_specs=vmem,
-            compiler_params=limit(4),
-            name="join",
-        )(mine, got, after)
 
     before = 4
     hid_a, last_a, wt = pl.pallas_call(
@@ -411,27 +427,45 @@
             name="inside_c",
         )(hid_a, hid_b, cols, w_second, bias, after)
 
-    tops = joined(top, inner, last_a)
-    step, stage, after = 2, 0, tops
-    while step < n:
+    pair = shape((2, 2 * width, WIDE), BF)
+    tops, sent = pl.pallas_call(
+        join_first,
+        out_shape=(pair, shape(sent.shape, BF)),
+        in_specs=[vmem] * 4,
+        out_specs=(vmem,) * 2,
+        input_output_aliases={3: 1},
+        compiler_params=limit(4),
+        name="join_first",
+    )(top, inner, last_a, sent)
+    step = 2
+    while step < n // 2:
         got = lax.ppermute(tops, "lon", [(i, i ^ step) for i in range(n)])
-        if stage == 0:
+        if step == 2:
+            outer = lax.ppermute(sent, "lon", [(i, (i + 1 if i % 2 else i - 1) % n) for i in range(n)])
+        if step == n // 4:
             hid_b, last_b, part = stage_b(tops)
-            after = last_b
-        elif stage == 1:
-            outp = stage_c(hid_b, tops)
-            after = outp
-        else:
-            after = tops
-        if stage < 2:
-            tops = joined(tops, got, after)
-        else:
-            late, final = tops, got
-            tops = None
-        step, stage = 2 * step, stage + 1
-        if tops is None:
-            if step < n:
-                tops = joined(late, final, late)
+            outp = stage_c(hid_b, last_b)
+            break
+        tops = pl.pallas_call(
+            join,
+            out_shape=shape((2 * tops.shape[0],) + tops.shape[1:], BF),
+            in_specs=[vmem] * 2,
+            out_specs=vmem,
+            compiler_params=limit(4),
+            name="join",
+        )(tops, got)
+        step *= 2
+    three = shape((3,) + tops.shape[1:], BF)
+    give, keep = pl.pallas_call(
+        choose,
+        out_shape=(three, three),
+        in_specs=[smem] + [vmem] * 3,
+        out_specs=(vmem,) * 2,
+        scratch_shapes=[scratch((2 * tops.shape[0],) + tops.shape[1:], BF)],
+        compiler_params=limit(4),
+        name="choose",
+    )(at, tops, got, outp)
+    got = lax.ppermute(give, "lon", [(i, i ^ (n // 2)) for i in range(n)])
     out, slab, sea, line, own = pl.pallas_call(
         border,
         out_shape=(
@@ -452,21 +486,20 @@
         ],
         compiler_params=limit(16),
         name="border",
-    )(place, cols, top, outer, inner, part, last_a, last_b, outp, wt, w_first, bias, w_second, late)
-    tops = joined(late, final, line)
+    )(place, cols, top, outer, inner, part, last_a, last_b, outp, wt, w_first, bias, w_second, give)
     return pl.pallas_call(
         fold,
         out_shape=shape((rows, width, hidden), BF),
-        in_specs=[smem] + [vmem] * 9 + [hbm],
+        in_specs=[smem] + [vmem] * 10 + [hbm],
         out_specs=hbm,
-        scratch_shapes=[scratch((n * 2 * width, WIDE), F32)]
+        scratch_shapes=[scratch((6 * width, WIDE), F32)]
         + [scratch((24, WIDE), F32)] * 4
         + [scratch((24, hidden), F32)] * 2
         + [scratch((2, width, hidden), BF), dma],
-        input_output_aliases={10: 0},
+        input_output_aliases={11: 0},
         compiler_params=limit(10),
         name="fold",
-    )(at, tops, slab, sea, line, own, wt, w_first, bias, w_second, out)
+    )(at, keep, got, slab, sea, line, own, wt, w_first, bias, w_second, out)
 
 
 def solution(mesh):

time: 29.4 us -> 32.7 us (1.11)
  starting transfers between devices: 8.45 us -> 11.1 us
  local copies, waits for them, and re-layouts: 1.36 us -> 0 us
  waiting for transfers between devices: 4.28 us -> 5.61 us
  Pallas kernels: 15 us -> 15.7 us
    ppermute x0 -> x1, starting transfers between devices: none -> 2.65 us  [local(): got = lax.ppermute(give, 'lon', [(i, i ^ n // 2) for i in range(n)])]
    unnamed x6 -> x0, local copies, waits for them, and re-layouts: 1.36 us -> none
    ppermute x3 -> x2, waiting for transfers between devices: 4.27 us -> 5.6 us  [local(): got = lax.ppermute(tops, 'lon', [(i, i ^ step) for i in range(n)])]
    pallas_call x4 -> x3, Pallas kernels: 0.04 us -> 0.57 us  [the longest x1 0.56 us: local(): pl.pallas_call(choose, out_shape=(three, three), in_specs=[smem] + [vmem]...]
    ppermute x3 -> x2, starting transfers between devices: 2.24 us -> 2.19 us  [local(): got = lax.ppermute(tops, 'lon', [(i, i ^ step) for i in range(n)])]
  transfers between devices with their start and end apart: 5 -> 5, of which waited for: 3 -> 1; matrix products, arithmetic and copies ran while one was open for 0% -> 0% of each run, Pallas kernels for 34% -> 32%
where the time goes in v3:
time: 32.7 us; the launch traced here: 32.5 us
  Pallas kernels  15.7 us (48%)
  starting transfers between devices  11.1 us (34%)
  waiting for transfers between devices  5.61 us (17%)
    ppermute x1, starting transfers between devices, local(): lax.ppermute(sent, 'lon', [(i, (i + 1 if i % 2 else i - 1) % n) for i in...  5.72 us
    ppermute x2, waiting for transfers between devices, local(): got = lax.ppermute(tops, 'lon', [(i, i ^ step) for i in range(n)])  5.6 us
    pallas_call x1, Pallas kernels, local(): pl.pallas_call(border, out_shape=(shape((rows, width, hidden), BF), shape...  3.72 us
    pallas_call x1, Pallas kernels, local(): pl.pallas_call(prepare, out_shape=(shape((2, held, rows), BF), shape((2,...  3.24 us
    ppermute x1, starting transfers between devices, local(): got = lax.ppermute(give, 'lon', [(i, i ^ n // 2) for i in range(n)])  2.65 us
    pallas_call x1, Pallas kernels, stage_c(): pl.pallas_call(functools.partial(inside_c, chans), out_shape=shape((hidde...  2.19 us
    ppermute x2, starting transfers between devices, local(): got = lax.ppermute(tops, 'lon', [(i, i ^ step) for i in range(n)])  2.19 us
    pallas_call x1, Pallas kernels, stage_b(): pl.pallas_call(functools.partial(inside_b, before), out_shape=(shape((wid...  2.09 us
  transfers between devices with their start and end apart: 5, of which 1 were waited for; matrix products, arithmetic and copies ran while one was open for 0% of the time, Pallas kernels for 32%

profile of v3, /device:TPU:0, one launch (start us, length us, event | category | flops | bytes accessed | tf_op | source)
XLA Modules:
  0.0 32.5 jit_solution(3400467800270545779)
XLA Ops:
  0.0 3.2 %prepare.1 = (bf16[2,304,256]{2,1,0:T(8,128)(2,1)S(1)}, bf16[2,320,256]{2,1,0:T(8,128)(2,1)S(1)}, bf16[8,256,384]{2,1,0:T(8,128)(2,1)S(1)}, bf16[1,16,384]{2,1,0...) custom-call(s32[1]{0:T(128)} %bitcast.me_ref, ...), custom_call_target="tpu_custom_call" | custom-call | tf_op jit(solution)/shard_map/prepare/pallas_call | solution.py:363
  3.3 0.6 %collective-permute-start = (bf16[2,320,256]{2,1,0:T(8,128)(2,1)S(1)}, bf16[2,320,256]{2,1,0:T(8,128)(2,1)S(1)}, u32[]{:S(2)}, u32[]{:S(2)}) collective-permute-start(bf16[2,320,256]{2,1,0:T(8,128)(2,1)S(1)} %get-tuple-element.30), channel_id=1, source_target_pairs={{0,1},{1,0},{2,3},{3,2},{4,5},{5,4},{6,7},{7,6},{8,9},{9,8},{10,11... | collective-permute-start | bytes 983048 | tf_op jit(solution)/shard_map/ppermute | solution.py:390
  3.8 2.0 %inside_a.1 = (bf16[4,256,256]{2,1,0:T(8,128)(2,1)S(1)}, f32[8,256]{1,0:T(8,128)S(1)}, bf16[256,768]{1,0:T(8,128)(2,1)S(1)}) custom-call(bf16[8,256,384]{2,1,0:T(8,128)(2,1)S(1)} %get-tuple-element.31.cols_ref, bf16[3,3,300,256]{3,2,1,0:T(8,128)(2,1)S(1)} %get-tuple-element.32.w1_ref, f32[2,256]{1,0:T(2,128)S(1)} %get-tuple-element.33.bias_ref), custom_call_target="tpu_custom_call" | custom-call | tf_op jit(solution)/shard_map/inside_a/pallas_call | solution.py:393
  5.8 0.0 collective-permute-done.got_ref.inner_ref
  5.8 5.7 %collective-permute-start.4 = (bf16[2,304,256]{2,1,0:T(8,128)(2,1)S(1)}, bf16[2,304,256]{2,1,0:T(8,128)(2,1)S(1)}, u32[]{:S(2)}, u32[]{:S(2)}) collective-permute-start(bf16[2,304,256]{2,1,0:T(8,128)(2,1)S(1)} %get-tuple-element.44), channel_id=1, source_target_pairs={{0,15},{1,2},{2,1},{3,4},{4,3},{5,6},{6,5},{7,8},{8,7},{9,10},{10,... | collective-permute-start | bytes 933896 | tf_op jit(solution)/shard_map/ppermute | solution.py:444
  11.5 0.0 collective-permute-start.1
  11.5 5.6 %collective-permute-done.1.got_ref = bf16[2,16,384]{2,1,0:T(8,128)(2,1)S(1)} collective-permute-done((bf16[2,16,384]{2,1,0:T(8,128)(2,1)S(1)}, bf16[2,16,384]{2,1,0:T(8,128)(2,1)S(1)}, u32[]{:S(2)}, u32[]{:S(2)}) %collective-permute-start.1) | collective-permute-done | bytes 24608 | tf_op jit(solution)/shard_map/ppermute | solution.py:442
  17.1 2.2 %collective-permute-start.2 = (bf16[4,16,384]{2,1,0:T(8,128)(2,1)S(1)}, bf16[4,16,384]{2,1,0:T(8,128)(2,1)S(1)}, u32[]{:S(2)}, u32[]{:S(2)}) collective-permute-start(bf16[4,16,384]{2,1,0:T(8,128)(2,1)S(1)} %join.1.after_ref.mine_ref), channel_id=1, source_target_pairs={{0,4},{1,5},{2,6},{3,7},{4,0},{5,1},{6,2},{7,3},{8,12},{9,13},{10,... | collective-permute-start | bytes 147464 | tf_op jit(solution)/shard_map/ppermute | solution.py:442
  19.3 2.1 %inside_b.1 = (bf16[2,256,256]{2,1,0:T(8,128)(2,1)S(1)}, f32[8,256]{1,0:T(8,128)S(1)}, f32[4,256,256]{2,1,0:T(8,128)S(1)}) custom-call(bf16[8,256,384]{2,1,0:T(8,128)(2,1)S(1)} %get-tuple-element.31.cols_ref, bf16[3,3,300,256]{3,2,1,0:T(8,128)(2,1)S(1)} %get-tuple-element.32.w1_ref, f32[2,256]{1,0:T(2,128)S(1)} %get-tuple-element.33.bias_ref, ...), custom_call_target="tpu_custom_call" | custom-call | tf_op jit(solution)/shard_map/inside_b/pallas_call | solution.py:407
  21.4 2.2 %inside_c.1.after_ref.outp_ref = f32[2,2048,128]{2,1,0:T(8,128)S(1)} custom-call(bf16[4,256,256]{2,1,0:T(8,128)(2,1)S(1)} %get-tuple-element.37.hid_a, bf16[2,256,256]{2,1,0:T(8,128)(2,1)S(1)} %get-tuple-element.39.hid_b, bf16[8,256,384]{2,1,0:T(8,128)(2,1)S(1)} %get-tuple-element.31.cols_ref, bf16[3,3,256,256]{3,2,1,0:T(8,128)(2,1)S(1)} %get-tuple-element.40.w2_ref, ...), custom_call_target="tpu_custom_call" | custom-call | tf_op jit(solution)/shard_map/inside_c/pallas_call | solution.py:421
  23.6 0.0 collective-permute-done.2.got_ref
  23.6 0.6 %choose.1 = (bf16[3,16,384]{2,1,0:T(8,128)(2,1)S(1)}, bf16[3,16,384]{2,1,0:T(8,128)(2,1)S(1)}) custom-call(s32[32]{0:T(128)S(1)} %get-tuple-element.28.at_ref, bf16[4,16,384]{2,1,0:T(8,128)(2,1)S(1)} %join.1.after_ref.mine_ref, bf16[4,16,384]{2,1,0:T(8,128)(2,1)S(1)} %collective-permute-done.2.got_ref, f32[2,2048,128]{2,1,0:T(8,128)S(1)} %inside_c.1.after_ref.outp_ref), custom_call_target="tpu_custom_call" | custom-call | tf_op jit(solution)/shard_map/choose/pallas_call | solution.py:459
  24.2 2.6 %collective-permute-start.3 = (bf16[3,16,384]{2,1,0:T(8,128)(2,1)S(1)}, bf16[3,16,384]{2,1,0:T(8,128)(2,1)S(1)}, u32[]{:S(2)}, u32[]{:S(2)}) collective-permute-start(bf16[3,16,384]{2,1,0:T(8,128)(2,1)S(1)} %get-tuple-element.43.after_ref), channel_id=1, source_target_pairs={{0,8},{1,9},{2,10},{3,11},{4,12},{5,13},{6,14},{7,15},{8,0},{9,1},... | collective-permute-start | bytes 110600 | tf_op jit(solution)/shard_map/ppermute | solution.py:468
  26.8 0.0 collective-permute-done.4.outer_ref
  26.8 3.7 %border.1 = (bf16[256,8,256]{2,1,0:T(8,128)(2,1)}, f32[16,256]{1,0:T(8,128)S(1)}, f32[16,256]{1,0:T(8,128)S(1)}, f32[16,256]{1,0:T(8,128)S(1)}, f32[24,384]{1,0:T(8,128)S(1)}) custom-call(s32[1]{0:T(128)} %bitcast.me_ref, bf16[8,256,384]{2,1,0:T(8,128)(2,1)S(1)} %get-tuple-element.31.cols_ref, bf16[1,16,384]{2,1,0:T(8,128)(2,1)S(1)} %get-tuple-element.29.mine_ref.top_ref, ...), custom_call_target="tpu_custom_call" | custom-call | tf_op jit(solution)/shard_map/border/pallas_call | solution.py:469
  30.6 0.0 collective-permute-done.3.got_ref
  30.6 1.9 %fold.1 = bf16[256,8,256]{2,1,0:T(8,128)(2,1)} custom-call(s32[32]{0:T(128)S(1)} %get-tuple-element.28.at_ref, bf16[3,16,384]{2,1,0:T(8,128)(2,1)S(1)} %get-tuple-element.42.keep_ref, bf16[3,16,384]{2,1,0:T(8,128)(2,1)S(1)} %collective-permute-done.3.got_ref, f32[16,256]{1,0:T(8,128)S(1)} %get-tuple-element.46.slab_ref, ...), custom_call_target="tpu_custom_call", output_to_operand_aliasing={{}: (11, {})} | custom-call | tf_op jit(solution)/shard_map/fold/pallas_call | solution.py:490
  (2 shorter events, 0.0 us)
Async XLA Ops:
  3.3 2.5 %collective-permute-start = (bf16[2,320,256]{2,1,0:T(8,128)(2,1)S(1)}, bf16[2,320,256]{2,1,0:T(8,128)(2,1)S(1)}, u32[]{:S(2)}, u32[]{:S(2)}) collective-permute-start(bf16[2,320,256]{2,1,0:T(8,128)(2,1)S(1)} %get-tuple-element.30), channel_id=1, source_target_pairs={{0,1},{1,0},{2,3},{3,2},{4,5},{5,4},{6,7},{7,6},{8,9},{9,8},{10,11... | collective-permute-start | bytes 983048 | tf_op jit(solution)/shard_map/ppermute | solution.py:390
  5.8 21.0 %collective-permute-start.4 = (bf16[2,304,256]{2,1,0:T(8,128)(2,1)S(1)}, bf16[2,304,256]{2,1,0:T(8,128)(2,1)S(1)}, u32[]{:S(2)}, u32[]{:S(2)}) collective-permute-start(bf16[2,304,256]{2,1,0:T(8,128)(2,1)S(1)} %get-tuple-element.44), channel_id=1, source_target_pairs={{0,15},{1,2},{2,1},{3,4},{4,3},{5,6},{6,5},{7,8},{8,7},{9,10},{10,... | collective-permute-start | bytes 933896 | tf_op jit(solution)/shard_map/ppermute | solution.py:444
  11.5 5.6 %collective-permute-start.1 = (bf16[2,16,384]{2,1,0:T(8,128)(2,1)S(1)}, bf16[2,16,384]{2,1,0:T(8,128)(2,1)S(1)}, u32[]{:S(2)}, u32[]{:S(2)}) collective-permute-start(bf16[2,16,384]{2,1,0:T(8,128)(2,1)S(1)} %get-tuple-element.36.mine_ref), channel_id=1, source_target_pairs={{0,2},{1,3},{2,0},{3,1},{4,6},{5,7},{6,4},{7,5},{8,10},{9,11},{10,... | collective-permute-start | bytes 73736 | tf_op jit(solution)/shard_map/ppermute | solution.py:442
  17.1 6.5 %collective-permute-start.2 = (bf16[4,16,384]{2,1,0:T(8,128)(2,1)S(1)}, bf16[4,16,384]{2,1,0:T(8,128)(2,1)S(1)}, u32[]{:S(2)}, u32[]{:S(2)}) collective-permute-start(bf16[4,16,384]{2,1,0:T(8,128)(2,1)S(1)} %join.1.after_ref.mine_ref), channel_id=1, source_target_pairs={{0,4},{1,5},{2,6},{3,7},{4,0},{5,1},{6,2},{7,3},{8,12},{9,13},{10,... | collective-permute-start | bytes 147464 | tf_op jit(solution)/shard_map/ppermute | solution.py:442
  24.2 6.4 %collective-permute-start.3 = (bf16[3,16,384]{2,1,0:T(8,128)(2,1)S(1)}, bf16[3,16,384]{2,1,0:T(8,128)(2,1)S(1)}, u32[]{:S(2)}, u32[]{:S(2)}) collective-permute-start(bf16[3,16,384]{2,1,0:T(8,128)(2,1)S(1)} %get-tuple-element.43.after_ref), channel_id=1, source_target_pairs={{0,8},{1,9},{2,10},{3,11},{4,12},{5,13},{6,14},{7,15},{8,0},{9,1},... | collective-permute-start | bytes 110600 | tf_op jit(solution)/shard_map/ppermute | solution.py:468

commit v4 on v3

--- a/solution.py
+++ b/solution.py
@@ -9,11 +9,18 @@
 
 BF, F32 = jnp.bfloat16, jnp.float32
 LANES, MAIN, SLOT, PIECES = 128, 256, 64, 4
+GROUP = 2
 WIDE = MAIN + 2 * SLOT
 
 
 def gelu(value):
-    return 0.5 * value * (1.0 + jnp.tanh(0.7978845608 * (value + 0.044715 * value * value * value)))
+    return half_gelu(value, 0.5)
+
+
+def half_gelu(value, half):
+    inner = value * (0.7978845608 + (0.7978845608 * 0.044715) * (value * value))
+    scaled = value * half
+    return scaled + scaled * jnp.tanh(inner)
 
 
 def turned(block):
@@ -28,13 +35,13 @@
 
 
 def prepare(
-    me_ref, fold_hbm, x_hbm, mask_hbm, b1_hbm, b2_hbm, w1_hbm, w2_hbm,
-    outer_ref, inner_ref, cols_ref, top_ref, bias_ref, at_ref, w1_ref, w2_ref,
+    fold_hbm, x_hbm, mask_hbm, b1_hbm, b2_hbm, w1_hbm, w2_hbm,
+    outer_ref, inner_ref, cols_ref, top_ref, bias_ref, pick_ref, w1_ref, w2_ref,
     x_ref, mask_ref, fold_ref, field, sem,
 ):
     chans, width, rows = x_ref.shape
     held = outer_ref.shape[1]
-    me = me_ref[0]
+    me = lax.axis_index("lon")
     cuts = [chans * i // PIECES for i in range(PIECES + 1)]
     pairs = [(mask_hbm, mask_ref)]
     pairs += [(x_hbm.at[lo:hi], x_ref.at[lo:hi]) for lo, hi in zip(cuts, cuts[1:])]
@@ -78,18 +85,16 @@
         copy.wait()
     total = fold_ref.shape[0]
     n = total // width
-    start = lax.rem(fold_ref[0] - (width + 1) + total, total) // width
-    for j in range(16):
-        src = fold_ref[lax.rem(me * width + (j - 2) + total, total)]
-        block = lax.rem(src // width - start + me + 2 * n, n)
-        at_ref[j] = lax.rem(block, 3) * (2 * width) + lax.rem(src, width)
-    peer = lax.bitwise_xor(me, n // 2)
-    for j in range(3):
-        theirs = lax.bitwise_xor(lax.rem(start - peer + j + n, n), me)
-        mine = lax.bitwise_xor(lax.rem(start - me + j + n, n), me)
-        at_ref[16 + j] = lax.rem(theirs, n // 2)
-        at_ref[19 + j] = lax.rem(mine, n // 2)
-        at_ref[22 + j] = mine // (n // 2)
+    index = lax.broadcasted_iota(jnp.int32, pick_ref.shape, 0)
+    j, line = index & 15, lax.shift_right_logical(index, 4) & 1
+    dev = jnp.where(index < 32, lax.bitwise_xor(me, n // 2), me)
+    col = fold_ref[0] - width * dev + 2 - j
+    col = jnp.where(col < 0, col + total, col)
+    col = jnp.where(col < 0, col + total, col)
+    col = jnp.where(col >= total, col - total, col)
+    block = lax.bitwise_xor(lax.shift_right_logical(col, width.bit_length() - 1), me)
+    spot = block * (2 * width) + line * width + (col & (width - 1))
+    pick_ref[...] = jnp.where((block < n // 2) & (j < width + 4), spot, -1)
 
 
 def top_rows(block):
@@ -101,19 +106,19 @@
     out_ref[1] = top_rows(got_ref[:, got_ref.shape[1] - mine_ref.shape[1] :])
 
 
-def join(mine_ref, got_ref, out_ref):
+def join(mine_ref, got_ref, after_ref, out_ref):
     count = mine_ref.shape[0]
     out_ref[:count] = mine_ref[...]
     out_ref[count:] = got_ref[...]
 
 
-def choose(at_ref, mine_ref, got_ref, after_ref, send_ref, keep_ref, blocks):
-    count = mine_ref.shape[0]
-    blocks[:count] = mine_ref[...]
-    blocks[count:] = got_ref[...]
-    for j in range(3):
-        send_ref[j] = blocks[at_ref[16 + j]]
-        keep_ref[j] = blocks[at_ref[19 + j]]
+def choose(pick_ref, mine_ref, got_ref, after_ref, give_ref, keep_ref):
+    count, lines, wide = mine_ref.shape
+    blocks = jnp.concatenate([ref[...].reshape(count * lines, wide) for ref in (mine_ref, got_ref)], axis=0)
+    lane = lax.broadcasted_iota(jnp.int32, (pick_ref.shape[0], blocks.shape[0]), 1)
+    out = mm((pick_ref[:, :1] == lane).astype(F32).astype(BF), blocks).astype(BF)
+    give_ref[...] = out[:32]
+    keep_ref[...] = out[32:]
 
 
 def mm(a, b):
@@ -172,12 +177,17 @@
     )
 
 
+def last_out(value):
+    row = lax.broadcasted_iota(jnp.int32, (8, value.shape[1]), 0)
+    return jnp.concatenate([value[:-8], jnp.where(row == 7, 0.0, value[-8:])], axis=0)
+
+
 def summed(p):
     rows, hidden = p.shape[0], p.shape[1] // 3
-    row = lax.broadcasted_iota(jnp.int32, (rows, hidden), 0)
-    south = jnp.where(row == 0, 0.0, pltpu.roll(p[:, :hidden], 1, 0))
-    north = jnp.where(row == rows - 1, 0.0, pltpu.roll(p[:, 2 * hidden :], rows - 1, 0))
-    return p[:, hidden : 2 * hidden] + south + north
+    row = lax.broadcasted_iota(jnp.int32, (8, hidden), 0)
+    south = pltpu.roll(p[:, :hidden], 1, 0)
+    south = jnp.concatenate([jnp.where(row == 0, 0.0, south[:8]), south[8:]], axis=0)
+    return p[:, hidden : 2 * hidden] + south + last_out(pltpu.roll(p[:, 2 * hidden :], rows - 1, 0))
 
 
 def edges(width):
@@ -188,60 +198,71 @@
     return cols_ref[j - 2] if 2 <= j < 2 + cols_ref.shape[0] else None
 
 
-def hidden_columns(cols_ref, w1_ref, bias_ref, wt, hid_ref, last_ref, first):
-    chans, hidden = w1_ref.shape[2:]
+def hidden_columns(cols_ref, w1_ref, bias_ref, wt, hid_ref, last_ref, first, part_ref, more):
+    chans, _ = w1_ref.shape[2:]
     rows = cols_ref.shape[1]
-    row = lax.broadcasted_iota(jnp.int32, (rows, hidden), 0)
     last_ref[...] = jnp.zeros_like(last_ref)
-    for i in range(hid_ref.shape[0]):
-        columns = [own_column(cols_ref, first + i + dx) for dx in range(3)]
-        value = summed(mm(first_taps(columns), first_weights(w1_ref, wt, columns)))
-        last_ref[i : i + 1, :] = value[rows - 1 :]
-        value = gelu(value + bias_ref[0:1]) * mask_of(columns[1], chans)
-        hid_ref[i] = jnp.where(row == rows - 1, 0.0, value).astype(BF)
-
-
-def inside_a(cols_ref, w1_ref, bias_ref, hid_ref, last_ref, wt_ref):
+    for i in range(0, hid_ref.shape[0], GROUP):
+        sets = [[own_column(cols_ref, first + i + g + dx) for dx in range(3)] for g in range(GROUP)]
+        lhs = jnp.concatenate([first_taps(columns) for columns in sets], axis=0)
+        out = mm(lhs, first_weights(w1_ref, wt, sets[0]))
+        for g in range(GROUP):
+            value = summed(out[g * rows : (g + 1) * rows])
+            last_ref[i + g : i + g + 1, :] = value[rows - 1 :]
+            value = half_gelu(value + bias_ref[0:1], 0.5 * mask_of(sets[g][1], chans))
+            hid_ref[i + g] = last_out(value).astype(BF)
+    for i, h in enumerate(more):
+        columns = [own_column(cols_ref, h + dx) for dx in range(3)]
+        part_ref[i] = summed(mm(first_taps(columns), first_weights(w1_ref, wt, columns)))
+
+
+def inside_a(cols_ref, w1_ref, bias_ref, hid_ref, last_ref, wt_ref, part_ref):
     tail_weights(w1_ref, wt_ref)
-    hidden_columns(cols_ref, w1_ref, bias_ref, wt_ref, hid_ref, last_ref, 2)
+    width = cols_ref.shape[0]
+    hidden_columns(cols_ref, w1_ref, bias_ref, wt_ref, hid_ref, last_ref, 2, part_ref, edges(width)[:1])
 
 
 def inside_b(before, cols_ref, w1_ref, bias_ref, wt_ref, after_ref, hid_ref, last_ref, part_ref):
-    hidden_columns(cols_ref, w1_ref, bias_ref, wt_ref, hid_ref, last_ref, 2 + before)
-    for i, h in enumerate(edges(cols_ref.shape[0])):
-        columns = [own_column(cols_ref, h + dx) for dx in range(3)]
-        part_ref[i] = summed(mm(first_taps(columns), first_weights(w1_ref, wt_ref, columns)))
+    width = cols_ref.shape[0]
+    hidden_columns(cols_ref, w1_ref, bias_ref, wt_ref, hid_ref, last_ref, 2 + before, part_ref, edges(width)[1:])
 
 
 def inside_c(chans, hid_a, hid_b, cols_ref, w2_ref, bias_ref, after_ref, out_ref):
     width, rows, _ = cols_ref.shape
     hidden = w2_ref.shape[3]
     before = hid_a.shape[0]
-    for o in range(width):
-        columns = []
-        for h in range(o, o + 3):
-            inside = 2 <= h < width
-            columns.append((hid_a[h - 2] if h - 2 < before else hid_b[h - 2 - before]) if inside else None)
-        have = [c for c in columns if c is not None]
-        if have:
-            value = summed(mm(jnp.concatenate(have, axis=1), second_weights(w2_ref, columns)))
-        else:
-            value = jnp.zeros((rows, hidden), F32)
-        value = value + bias_ref[1:2]
-        if len(have) == 3:
-            value = value * mask_of(cols_ref[o], chans)
+
+    def hid(h):
+        if not 2 <= h < width:
+            return None
+        return hid_a[h - 2] if h - 2 < before else hid_b[h - 2 - before]
+
+    def put(o, value):
         for i in range(hidden // LANES):
             out_ref[i, pl.ds(o, rows, stride=width), :] = value[:, i * LANES : (i + 1) * LANES]
 
+    def lhs(columns):
+        return jnp.concatenate([c for c in columns if c is not None], axis=1)
+
+    for o in range(2, width - 2, GROUP):
+        sets = [[hid(o + g + dx) for dx in range(3)] for g in range(GROUP)]
+        out = mm(jnp.concatenate([lhs(c) for c in sets], axis=0), second_weights(w2_ref, sets[0]))
+        for g in range(GROUP):
+            value = summed(out[g * rows : (g + 1) * rows]) + bias_ref[1:2]
+            put(o + g, value * mask_of(cols_ref[o + g], chans))
+    for o in (0, 1, width - 2, width - 1):
+        columns = [hid(o + dx) for dx in range(3)]
+        put(o, summed(mm(lhs(columns), second_weights(w2_ref, columns))) + bias_ref[1:2])
+
 
 def border(
-    me_ref, cols_ref, top_ref, outer_ref, inner_ref, part_ref, last_a, last_b, outp_ref, wt, w1_ref, bias_ref, w2_ref,
+    cols_ref, top_ref, outer_ref, inner_ref, part_a, part_b, last_a, last_b, outp_ref, wt, w1_ref, bias_ref, w2_ref,
     after_ref, out_hbm, slab_ref, sea_ref, line_ref, own_ref, hx, hid, outf, outb, sem,
 ):
     chans, hidden = w1_ref.shape[2:]
     width, rows, _ = cols_ref.shape
     held = outer_ref.shape[1]
-    odd = lax.rem(me_ref[0], 2) == 1
+    odd = lax.rem(lax.axis_index("lon"), 2) == 1
     for c in range(2):
         hx[c] = turned(jnp.where(odd, inner_ref[c, :held], outer_ref[c])).astype(BF)
         hx[2 + c] = turned(jnp.where(odd, outer_ref[c], inner_ref[c, :held])).astype(BF)
@@ -253,16 +274,15 @@
     for j in range(width + 4):
         own_ref[j : j + 1, :] = column(j)[rows - 16 :].astype(F32)[15:16]
     bias1 = bias_ref[0:1]
-    row = lax.broadcasted_iota(jnp.int32, (rows, hidden), 0)
     line_ref[...] = jnp.zeros_like(line_ref)
     line_ref[2:6] = last_a[:4]
     line_ref[6:width] = last_b[: width - 6]
     for i, h in enumerate(edges(width)):
         columns = [column(h + dx) if not 2 <= h + dx < 2 + width else None for dx in range(3)]
-        value = part_ref[i] + summed(mm(first_taps(columns), first_weights(w1_ref, wt, columns)))
+        value = (part_a[0] if i == 0 else part_b[i - 1]) + summed(mm(first_taps(columns), first_weights(w1_ref, wt, columns)))
         line_ref[h : h + 1, :] = value[rows - 1 :]
-        value = gelu(value + bias1) * mask_of(column(h + 1), chans)
-        hid[i] = jnp.where(row == rows - 1, 0.0, value).astype(BF)
+        value = half_gelu(value + bias1, 0.5 * mask_of(column(h + 1), chans))
+        hid[i] = last_out(value).astype(BF)
     for o in (0, 1, width - 2, width - 1):
         columns = [hid[edges(width).index(o + dx)] if o + dx in edges(width) else None for dx in range(3)]
         have = [c for c in columns if c is not None]
@@ -293,25 +313,18 @@
 
 
 def fold(
-    at_ref, keep_ref, got_ref, slab_ref, sea_ref, line_ref, own_ref, wt, w1_ref, bias_ref, w2_ref, old_hbm,
-    out_hbm, gf, m0, m1, r2, gs, hg, hz, outb, sem,
+    keep_ref, got_ref, slab_ref, sea_ref, line_ref, own_ref, wt, w1_ref, bias_ref, w2_ref, old_hbm,
+    out_hbm, m0, m1, r2, gs, hg, hz, outb, sem,
 ):
     chans, hidden = w1_ref.shape[2:]
     rows, width, _ = out_hbm.shape
     bias1 = bias_ref[0:1]
-    for j in range(3):
-        block = jnp.where(at_ref[22 + j] == 0, keep_ref[j], got_ref[j])
-        gf[j * 2 * width : (j + 1) * 2 * width] = block.astype(F32)
-    for ref in (m0, m1, r2, gs):
-        ref[...] = jnp.zeros_like(ref)
     lane = lax.broadcasted_iota(jnp.int32, (1, WIDE), 1)
     sign = jnp.where(lane < chans // 2, -1.0, 1.0).astype(F32)
-    for j in range(width + 4):
-        at = at_ref[j]
-        m0[j : j + 1, :] = gf[pl.ds(at, 1), :]
-        north = gf[pl.ds(at + width, 1), :]
-        m1[j : j + 1, :] = north
-        gs[j : j + 1, :] = north * sign
+    both = keep_ref[...].astype(F32) + got_ref[...].astype(F32)
+    for ref, value in ((m0, both[:16]), (m1, both[16:]), (gs, both[16:] * sign)):
+        ref[:16] = value
+        ref[16:] = jnp.zeros_like(ref[16:])
     r2[...] = own_ref[...] * sign
 
     def taps(ref, offsets):
@@ -343,16 +356,13 @@
     rows, width, chans = state.shape
     hidden = w_first.shape[-1]
     n = lax.axis_size("lon")
-    me = lax.axis_index("lon")
     assert n >= 8 and n & (n - 1) == 0 and MAIN <= chans < MAIN + SLOT and chans // 2 <= MAIN and width == 8 and rows == MAIN
     held = -(-(chans + 1) // 16) * 16
-    smem = pl.BlockSpec(memory_space=pltpu.SMEM)
     vmem = pl.BlockSpec(memory_space=pltpu.VMEM)
     hbm = pl.BlockSpec(memory_space=pltpu.MemorySpace.HBM)
     shape = jax.ShapeDtypeStruct
     scratch = pltpu.VMEM
     dma = pltpu.SemaphoreType.DMA
-    place = jnp.full((1,), me, jnp.int32)
 
     def limit(mib):
         return pltpu.CompilerParams(vmem_limit_bytes=mib << 20)
@@ -360,7 +370,7 @@
     def far(value):
         return pltpu.with_memory_space_constraint(value, pltpu.MemorySpace.HBM)
 
-    sent, inner, cols, top, bias, at, w_first, w_second = pl.pallas_call(
+    sent, inner, cols, top, bias, pick, w_first, w_second = pl.pallas_call(
         prepare,
         out_shape=(
             shape((2, held, rows), BF),
@@ -368,12 +378,12 @@
             shape((width, rows, WIDE), BF),
             shape((1, 2 * width, WIDE), BF),
             shape((2, hidden), F32),
-            shape((32,), jnp.int32),
+            shape((64, LANES), jnp.int32),
             shape(w_first.shape, BF),
             shape(w_second.shape, BF),
         ),
-        in_specs=[smem] + [hbm] * 7,
-        out_specs=(vmem,) * 5 + (smem, vmem, vmem),
+        in_specs=[hbm] * 7,
+        out_specs=(vmem,) * 8,
         scratch_shapes=[
             scratch((chans, width, rows), BF),
             scratch((width, rows), jnp.int32),
@@ -384,21 +394,22 @@
         compiler_params=limit(14),
         name="prepare",
     )(
-        place, far(fold_map), far(state.transpose(2, 1, 0)), far(ocean_mask.T),
+        far(fold_map), far(state.transpose(2, 1, 0)), far(ocean_mask.T),
         far(b_first[None]), far(b_second[None]), far(w_first), far(w_second),
     )
     inner = lax.ppermute(inner, "lon", [(i, i ^ 1) for i in range(n)])
 
     before = 4
-    hid_a, last_a, wt = pl.pallas_call(
+    hid_a, last_a, wt, part_a = pl.pallas_call(
         inside_a,
         out_shape=(
             shape((before, rows, hidden), BF),
             shape((8, hidden), F32),
             shape((4 * SLOT, 3 * hidden), BF),
+            shape((1, rows, hidden), F32),
         ),
         in_specs=[vmem] * 3,
-        out_specs=(vmem,) * 3,
+        out_specs=(vmem,) * 4,
         compiler_params=limit(12),
         name="inside_a",
     )(cols, w_first, bias)
@@ -409,7 +420,7 @@
             out_shape=(
                 shape((width - 2 - before, rows, hidden), BF),
                 shape((8, hidden), F32),
-                shape((4, rows, hidden), F32),
+                shape((3, rows, hidden), F32),
             ),
             in_specs=[vmem] * 5,
             out_specs=(vmem,) * 3,
@@ -442,29 +453,28 @@
         got = lax.ppermute(tops, "lon", [(i, i ^ step) for i in range(n)])
         if step == 2:
             outer = lax.ppermute(sent, "lon", [(i, (i + 1 if i % 2 else i - 1) % n) for i in range(n)])
+            hid_b, last_b, part_b = stage_b(tops)
         if step == n // 4:
-            hid_b, last_b, part = stage_b(tops)
-            outp = stage_c(hid_b, last_b)
+            outp = stage_c(hid_b, tops)
             break
         tops = pl.pallas_call(
             join,
             out_shape=shape((2 * tops.shape[0],) + tops.shape[1:], BF),
-            in_specs=[vmem] * 2,
+            in_specs=[vmem] * 3,
             out_specs=vmem,
             compiler_params=limit(4),
             name="join",
-        )(tops, got)
+        )(tops, got, last_b)
         step *= 2
-    three = shape((3,) + tops.shape[1:], BF)
+    lines = shape((32, WIDE), BF)
     give, keep = pl.pallas_call(
         choose,
-        out_shape=(three, three),
-        in_specs=[smem] + [vmem] * 3,
+        out_shape=(lines, lines),
+        in_specs=[vmem] * 4,
         out_specs=(vmem,) * 2,
-        scratch_shapes=[scratch((2 * tops.shape[0],) + tops.shape[1:], BF)],
         compiler_params=limit(4),
         name="choose",
-    )(at, tops, got, outp)
+    )(pick, tops, got, outp)
     got = lax.ppermute(give, "lon", [(i, i ^ (n // 2)) for i in range(n)])
     out, slab, sea, line, own = pl.pallas_call(
         border,
@@ -475,7 +485,7 @@
             shape((16, hidden), F32),
             shape((24, WIDE), F32),
         ),
-        in_specs=[smem] + [vmem] * 13,
+        in_specs=[vmem] * 14,
         out_specs=(hbm,) + (vmem,) * 4,
         scratch_shapes=[
             scratch((4, rows, WIDE), BF),
@@ -486,20 +496,19 @@
         ],
         compiler_params=limit(16),
         name="border",
-    )(place, cols, top, outer, inner, part, last_a, last_b, outp, wt, w_first, bias, w_second, give)
+    )(cols, top, outer, inner, part_a, part_b, last_a, last_b, outp, wt, w_first, bias, w_second, give)
     return pl.pallas_call(
         fold,
         out_shape=shape((rows, width, hidden), BF),
-        in_specs=[smem] + [vmem] * 10 + [hbm],
+        in_specs=[vmem] * 10 + [hbm],
         out_specs=hbm,
-        scratch_shapes=[scratch((6 * width, WIDE), F32)]
-        + [scratch((24, WIDE), F32)] * 4
+        scratch_shapes=[scratch((24, WIDE), F32)] * 4
         + [scratch((24, hidden), F32)] * 2
         + [scratch((2, width, hidden), BF), dma],
-        input_output_aliases={11: 0},
+        input_output_aliases={10: 0},
         compiler_params=limit(10),
         name="fold",
-    )(at, keep, got, slab, sea, line, own, wt, w_first, bias, w_second, out)
+    )(keep, got, slab, sea, line, own, wt, w_first, bias, w_second, out)
 
 
 def solution(mesh):

time: 32.7 us -> 29.3 us (0.90)
  waiting for transfers between devices: 5.61 us -> 3.67 us
  Pallas kernels: 15.7 us -> 14 us
    ppermute x2, waiting for transfers between devices: 5.6 us -> 3.66 us  [local(): got = lax.ppermute(tops, 'lon', [(i, i ^ step) for i in range(n)])]
    pallas_call x1, Pallas kernels: 3.24 us -> 2.47 us  [local(): pl.pallas_call(prepare, out_shape=(shape((2, held, rows), BF), shape((2,...]
    pallas_call x1, Pallas kernels: 1.89 us -> 1.33 us  [local(): pl.pallas_call(fold, out_shape=shape((rows, width, hidden), BF), in_specs...]
    pallas_call x1, Pallas kernels: 0.56 us -> 0.2 us  [local(): pl.pallas_call(choose, out_shape=(lines, lines), in_specs=[vmem] * 4, out...]
  transfers between devices with their start and end apart: 5 -> 5, of which waited for: 1 -> 1; matrix products, arithmetic and copies ran while one was open for 0% -> 0% of each run, Pallas kernels for 32% -> 35%
where the time goes in v4:
time: 29.3 us; the launch traced here: 29.1 us
  Pallas kernels  14 us (48%)
  starting transfers between devices  11.4 us (39%)
  waiting for transfers between devices  3.67 us (13%)
    ppermute x1, starting transfers between devices, local(): lax.ppermute(sent, 'lon', [(i, (i + 1 if i % 2 else i - 1) % n) for i in...  5.72 us
    pallas_call x1, Pallas kernels, local(): pl.pallas_call(border, out_shape=(shape((rows, width, hidden), BF), shape...  3.67 us
    ppermute x2, waiting for transfers between devices, local(): got = lax.ppermute(tops, 'lon', [(i, i ^ step) for i in range(n)])  3.66 us
    ppermute x1, starting transfers between devices, local(): got = lax.ppermute(give, 'lon', [(i, i ^ n // 2) for i in range(n)])  2.91 us
    pallas_call x1, Pallas kernels, local(): pl.pallas_call(prepare, out_shape=(shape((2, held, rows), BF), shape((2,...  2.47 us
    pallas_call x1, Pallas kernels, stage_c(): pl.pallas_call(functools.partial(inside_c, chans), out_shape=shape((hidde...  2.23 us
    pallas_call x1, Pallas kernels, local(): pl.pallas_call(inside_a, out_shape=(shape((before, rows, hidden), BF), sh...  2.18 us
    ppermute x2, starting transfers between devices, local(): got = lax.ppermute(tops, 'lon', [(i, i ^ step) for i in range(n)])  2.18 us
  transfers between devices with their start and end apart: 5, of which 1 were waited for; matrix products, arithmetic and copies ran while one was open for 0% of the time, Pallas kernels for 35%

profile of v4, /device:TPU:0, one launch (start us, length us, event | category | flops | bytes accessed | tf_op | source)
XLA Modules:
  0.0 29.1 jit_solution(13858668569718012081)
XLA Ops:
  0.0 2.5 %prepare.1 = (bf16[2,304,256]{2,1,0:T(8,128)(2,1)S(1)}, bf16[2,320,256]{2,1,0:T(8,128)(2,1)S(1)}, bf16[8,256,384]{2,1,0:T(8,128)(2,1)S(1)}, bf16[1,16,384]{2,1,0...) custom-call(s32[128]{0:T(128)} %fold_hbm.1, ...), custom_call_target="tpu_custom_call" | custom-call | tf_op jit(solution)/shard_map/prepare/pallas_call | solution.py:373
  2.5 0.6 %collective-permute-start = (bf16[2,320,256]{2,1,0:T(8,128)(2,1)S(1)}, bf16[2,320,256]{2,1,0:T(8,128)(2,1)S(1)}, u32[]{:S(2)}, u32[]{:S(2)}) collective-permute-start(bf16[2,320,256]{2,1,0:T(8,128)(2,1)S(1)} %get-tuple-element.31), channel_id=1, source_target_pairs={{0,1},{1,0},{2,3},{3,2},{4,5},{5,4},{6,7},{7,6},{8,9},{9,8},{10,11... | collective-permute-start | bytes 983048 | tf_op jit(solution)/shard_map/ppermute | solution.py:400
  3.0 2.2 %inside_a.1 = (bf16[4,256,256]{2,1,0:T(8,128)(2,1)S(1)}, f32[8,256]{1,0:T(8,128)S(1)}, bf16[256,768]{1,0:T(8,128)(2,1)S(1)}, f32[1,256,256]{2,1,0:T(8,128)S(1)}) custom-call(bf16[8,256,384]{2,1,0:T(8,128)(2,1)S(1)} %get-tuple-element.32.cols_ref, bf16[3,3,300,256]{3,2,1,0:T(8,128)(2,1)S(1)} %get-tuple-element.33.w1_ref, f32[2,256]{1,0:T(2,128)S(1)} %get-tuple-element.34.bias_ref), custom_call_target="tpu_custom_call" | custom-call | tf_op jit(solution)/shard_map/inside_a/pallas_call | solution.py:403
  5.2 0.0 collective-permute-done.got_ref.inner_ref
  5.2 5.7 %collective-permute-start.4 = (bf16[2,304,256]{2,1,0:T(8,128)(2,1)S(1)}, bf16[2,304,256]{2,1,0:T(8,128)(2,1)S(1)}, u32[]{:S(2)}, u32[]{:S(2)}) collective-permute-start(bf16[2,304,256]{2,1,0:T(8,128)(2,1)S(1)} %get-tuple-element.45), channel_id=1, source_target_pairs={{0,15},{1,2},{2,1},{3,4},{4,3},{5,6},{6,5},{7,8},{8,7},{9,10},{10,... | collective-permute-start | bytes 933896 | tf_op jit(solution)/shard_map/ppermute | solution.py:455
  11.0 0.0 collective-permute-start.1
  11.0 1.9 %inside_b.1 = (bf16[2,256,256]{2,1,0:T(8,128)(2,1)S(1)}, f32[8,256]{1,0:T(8,128)S(1)}, f32[3,256,256]{2,1,0:T(8,128)S(1)}) custom-call(bf16[8,256,384]{2,1,0:T(8,128)(2,1)S(1)} %get-tuple-element.32.cols_ref, bf16[3,3,300,256]{3,2,1,0:T(8,128)(2,1)S(1)} %get-tuple-element.33.w1_ref, f32[2,256]{1,0:T(2,128)S(1)} %get-tuple-element.34.bias_ref, ...), custom_call_target="tpu_custom_call" | custom-call | tf_op jit(solution)/shard_map/inside_b/pallas_call | solution.py:418
  12.9 3.7 %collective-permute-done.1.got_ref = bf16[2,16,384]{2,1,0:T(8,128)(2,1)S(1)} collective-permute-done((bf16[2,16,384]{2,1,0:T(8,128)(2,1)S(1)}, bf16[2,16,384]{2,1,0:T(8,128)(2,1)S(1)}, u32[]{:S(2)}, u32[]{:S(2)}) %collective-permute-start.1) | collective-permute-done | bytes 24608 | tf_op jit(solution)/shard_map/ppermute | solution.py:453
  16.6 2.2 %collective-permute-start.2 = (bf16[4,16,384]{2,1,0:T(8,128)(2,1)S(1)}, bf16[4,16,384]{2,1,0:T(8,128)(2,1)S(1)}, u32[]{:S(2)}, u32[]{:S(2)}) collective-permute-start(bf16[4,16,384]{2,1,0:T(8,128)(2,1)S(1)} %join.1.after_ref.mine_ref), channel_id=1, source_target_pairs={{0,4},{1,5},{2,6},{3,7},{4,0},{5,1},{6,2},{7,3},{8,12},{9,13},{10,... | collective-permute-start | bytes 147464 | tf_op jit(solution)/shard_map/ppermute | solution.py:453
  18.8 2.2 %inside_c.1.after_ref.outp_ref = f32[2,2048,128]{2,1,0:T(8,128)S(1)} custom-call(bf16[4,256,256]{2,1,0:T(8,128)(2,1)S(1)} %get-tuple-element.40.hid_a, bf16[2,256,256]{2,1,0:T(8,128)(2,1)S(1)} %get-tuple-element.41.hid_b, bf16[8,256,384]{2,1,0:T(8,128)(2,1)S(1)} %get-tuple-element.32.cols_ref, bf16[3,3,256,256]{3,2,1,0:T(8,128)(2,1)S(1)} %get-tuple-element.42.w2_ref, ...), custom_call_target="tpu_custom_call" | custom-call | tf_op jit(solution)/shard_map/inside_c/pallas_call | solution.py:432
  21.0 0.0 collective-permute-done.2.got_ref
  21.0 0.2 choose.1
  21.2 2.9 %collective-permute-start.3 = (bf16[32,384]{1,0:T(8,128)(2,1)S(1)}, bf16[32,384]{1,0:T(8,128)(2,1)S(1)}, u32[]{:S(2)}, u32[]{:S(2)}) collective-permute-start(bf16[32,384]{1,0:T(8,128)(2,1)S(1)} %get-tuple-element.44.after_ref), channel_id=1, source_target_pairs={{0,8},{1,9},{2,10},{3,11},{4,12},{5,13},{6,14},{7,15},{8,0},{9,1},... | collective-permute-start | bytes 73736 | tf_op jit(solution)/shard_map/ppermute | solution.py:478
  24.1 0.0 collective-permute-done.4.outer_ref
  24.1 3.7 %border.1 = (bf16[256,8,256]{2,1,0:T(8,128)(2,1)}, f32[16,256]{1,0:T(8,128)S(1)}, f32[16,256]{1,0:T(8,128)S(1)}, f32[16,256]{1,0:T(8,128)S(1)}, f32[24,384]{1,0:T(8,128)S(1)}) custom-call(bf16[8,256,384]{2,1,0:T(8,128)(2,1)S(1)} %get-tuple-element.32.cols_ref, bf16[1,16,384]{2,1,0:T(8,128)(2,1)S(1)} %get-tuple-element.30.mine_ref.top_ref, ...), custom_call_target="tpu_custom_call" | custom-call | tf_op jit(solution)/shard_map/border/pallas_call | solution.py:479
  27.8 0.0 collective-permute-done.3.got_ref
  27.8 1.3 %fold.1 = bf16[256,8,256]{2,1,0:T(8,128)(2,1)} custom-call(bf16[32,384]{1,0:T(8,128)(2,1)S(1)} %get-tuple-element.43.keep_ref, bf16[32,384]{1,0:T(8,128)(2,1)S(1)} %collective-permute-done.3.got_ref, f32[16,256]{1,0:T(8,128)S(1)} %get-tuple-element.48.slab_ref, f32[16,256]{1,0:T(8,128)S(1)} %get-tuple-element.49.sea_ref, ...), custom_call_target="tpu_custom_call", output_to_operand_aliasing={{}: (10, {})} | custom-call | tf_op jit(solution)/shard_map/fold/pallas_call | solution.py:500
  (2 shorter events, 0.0 us)
Async XLA Ops:
  2.5 2.8 %collective-permute-start = (bf16[2,320,256]{2,1,0:T(8,128)(2,1)S(1)}, bf16[2,320,256]{2,1,0:T(8,128)(2,1)S(1)}, u32[]{:S(2)}, u32[]{:S(2)}) collective-permute-start(bf16[2,320,256]{2,1,0:T(8,128)(2,1)S(1)} %get-tuple-element.31), channel_id=1, source_target_pairs={{0,1},{1,0},{2,3},{3,2},{4,5},{5,4},{6,7},{7,6},{8,9},{9,8},{10,11... | collective-permute-start | bytes 983048 | tf_op jit(solution)/shard_map/ppermute | solution.py:400
  5.2 18.9 %collective-permute-start.4 = (bf16[2,304,256]{2,1,0:T(8,128)(2,1)S(1)}, bf16[2,304,256]{2,1,0:T(8,128)(2,1)S(1)}, u32[]{:S(2)}, u32[]{:S(2)}) collective-permute-start(bf16[2,304,256]{2,1,0:T(8,128)(2,1)S(1)} %get-tuple-element.45), channel_id=1, source_target_pairs={{0,15},{1,2},{2,1},{3,4},{4,3},{5,6},{6,5},{7,8},{8,7},{9,10},{10,... | collective-permute-start | bytes 933896 | tf_op jit(solution)/shard_map/ppermute | solution.py:455
  11.0 5.6 %collective-permute-start.1 = (bf16[2,16,384]{2,1,0:T(8,128)(2,1)S(1)}, bf16[2,16,384]{2,1,0:T(8,128)(2,1)S(1)}, u32[]{:S(2)}, u32[]{:S(2)}) collective-permute-start(bf16[2,16,384]{2,1,0:T(8,128)(2,1)S(1)} %get-tuple-element.37.after_ref.mine_ref), channel_id=1, source_target_pairs={{0,2},{1,3},{2,0},{3,1},{4,6},{5,7},{6,4},{7,5},{8,10},{9,11},{10,... | collective-permute-start | bytes 73736 | tf_op jit(solution)/shard_map/ppermute | solution.py:453
  16.6 4.4 %collective-permute-start.2 = (bf16[4,16,384]{2,1,0:T(8,128)(2,1)S(1)}, bf16[4,16,384]{2,1,0:T(8,128)(2,1)S(1)}, u32[]{:S(2)}, u32[]{:S(2)}) collective-permute-start(bf16[4,16,384]{2,1,0:T(8,128)(2,1)S(1)} %join.1.after_ref.mine_ref), channel_id=1, source_target_pairs={{0,4},{1,5},{2,6},{3,7},{4,0},{5,1},{6,2},{7,3},{8,12},{9,13},{10,... | collective-permute-start | bytes 147464 | tf_op jit(solution)/shard_map/ppermute | solution.py:453
  21.2 6.6 %collective-permute-start.3 = (bf16[32,384]{1,0:T(8,128)(2,1)S(1)}, bf16[32,384]{1,0:T(8,128)(2,1)S(1)}, u32[]{:S(2)}, u32[]{:S(2)}) collective-permute-start(bf16[32,384]{1,0:T(8,128)(2,1)S(1)} %get-tuple-element.44.after_ref), channel_id=1, source_target_pairs={{0,8},{1,9},{2,10},{3,11},{4,12},{5,13},{6,14},{7,15},{8,0},{9,1},... | collective-permute-start | bytes 73736 | tf_op jit(solution)/shard_map/ppermute | solution.py:478

commit v5 on v4

--- a/solution.py
+++ b/solution.py
@@ -40,7 +40,7 @@
     x_ref, mask_ref, fold_ref, field, sem,
 ):
     chans, width, rows = x_ref.shape
-    held = outer_ref.shape[1]
+    held = field.shape[1] // width
     me = lax.axis_index("lon")
     cuts = [chans * i // PIECES for i in range(PIECES + 1)]
     pairs = [(mask_hbm, mask_ref)]
@@ -67,20 +67,24 @@
         parts = [field[i, pl.ds(c, held, stride=width), :] for i in range(rows // LANES)]
         return jnp.concatenate(parts, axis=1).astype(BF)
 
-    for c in range(2):
-        low, high = column(c), column(width - 2 + c)
-        outer_ref[c] = jnp.where(odd, high, low)
-        inner_ref[c, :held] = jnp.where(odd, low, high)
     last = []
     for c in range(width):
         out = turned(column(c))
         cols_ref[c] = out.astype(BF)
         last.append(out[rows - 2 :])
+    lanes = lax.broadcasted_iota(jnp.int32, (rows, LANES), 1)
+
+    def message(c):
+        first, second = cols_ref[c], cols_ref[c + 1]
+        rest = jnp.where(lanes < SLOT, first[:, MAIN:][:, :LANES], second[:, MAIN:][:, :LANES])
+        return jnp.concatenate([first[:, :MAIN], second[:, :MAIN], rest], axis=1)
+
+    low, high = message(0), message(width - 2)
+    outer_ref[...] = jnp.where(odd, high, low)
+    inner_ref[:rows] = jnp.where(odd, low, high)
     top = jnp.concatenate([v[i : i + 1] for i in range(2) for v in last], axis=0).astype(BF)
     top_ref[0] = top
-    inner_ref[0, held:] = top[:, :rows]
-    pad = jnp.zeros((2 * width, 2 * rows - WIDE), BF)
-    inner_ref[1, held:] = jnp.concatenate([top[:, rows:], pad], axis=1)
+    inner_ref[rows:] = jnp.concatenate([top, jnp.zeros((2 * width, inner_ref.shape[1] - WIDE), BF)], axis=1)
     for copy in copies[1 + PIECES :]:
         copy.wait()
     total = fold_ref.shape[0]
@@ -97,16 +101,12 @@
     pick_ref[...] = jnp.where((block < n // 2) & (j < width + 4), spot, -1)
 
 
-def top_rows(block):
-    return jnp.concatenate([block[0], block[1][:, : WIDE - MAIN]], axis=1)
-
-
 def join_first(mine_ref, got_ref, after_ref, sent_ref, out_ref, pass_ref):
     out_ref[0] = mine_ref[0]
-    out_ref[1] = top_rows(got_ref[:, got_ref.shape[1] - mine_ref.shape[1] :])
-
-
-def join(mine_ref, got_ref, after_ref, out_ref):
+    out_ref[1] = got_ref[got_ref.shape[0] - mine_ref.shape[1] :, :WIDE]
+
+
+def join(mine_ref, got_ref, out_ref):
     count = mine_ref.shape[0]
     out_ref[:count] = mine_ref[...]
     out_ref[count:] = got_ref[...]
@@ -136,8 +136,9 @@
             rest = jnp.concatenate(
                 [w1_ref[dy, dx, MAIN:, :], jnp.zeros((SLOT - chans + MAIN, hidden), BF)], axis=0
             )
-            wt[dx * SLOT : (dx + 1) * SLOT, dy * hidden : (dy + 1) * hidden] = rest
-    wt[3 * SLOT :, :] = jnp.zeros((SLOT, 3 * hidden), BF)
+            wt[(dx + 1) * SLOT : (dx + 2) * SLOT, dy * hidden : (dy + 1) * hidden] = rest
+    for at in (0, 4 * SLOT):
+        wt[at : at + SLOT, :] = jnp.zeros((SLOT, 3 * hidden), BF)
 
 
 def first_taps(columns):
@@ -160,9 +161,9 @@
         at = slice(dy * hidden, (dy + 1) * hidden)
         parts = [w1_ref[dy, dx, :MAIN, :] for dx in range(3) if columns[dx] is not None]
         if columns[0] is not None or columns[1] is not None:
-            parts.append(wt[: 2 * SLOT, at])
+            parts.append(wt[SLOT : 3 * SLOT, at])
         if columns[2] is not None:
-            parts.append(wt[2 * SLOT :, at])
+            parts.append(wt[3 * SLOT :, at])
         out.append(jnp.concatenate(parts, axis=0))
     return jnp.concatenate(out, axis=1)
 
@@ -227,7 +228,7 @@
     hidden_columns(cols_ref, w1_ref, bias_ref, wt_ref, hid_ref, last_ref, 2 + before, part_ref, edges(width)[1:])
 
 
-def inside_c(chans, hid_a, hid_b, cols_ref, w2_ref, bias_ref, after_ref, out_ref):
+def second_columns(chans, todo, hid_a, hid_b, cols_ref, w2_ref, bias_ref, out_ref):
     width, rows, _ = cols_ref.shape
     hidden = w2_ref.shape[3]
     before = hid_a.shape[0]
@@ -244,88 +245,117 @@
     def lhs(columns):
         return jnp.concatenate([c for c in columns if c is not None], axis=1)
 
-    for o in range(2, width - 2, GROUP):
-        sets = [[hid(o + g + dx) for dx in range(3)] for g in range(GROUP)]
+    for group in todo:
+        sets = [[hid(o + dx) for dx in range(3)] for o in group]
         out = mm(jnp.concatenate([lhs(c) for c in sets], axis=0), second_weights(w2_ref, sets[0]))
-        for g in range(GROUP):
+        for g, o in enumerate(group):
             value = summed(out[g * rows : (g + 1) * rows]) + bias_ref[1:2]
-            put(o + g, value * mask_of(cols_ref[o + g], chans))
-    for o in (0, 1, width - 2, width - 1):
-        columns = [hid(o + dx) for dx in range(3)]
-        put(o, summed(mm(lhs(columns), second_weights(w2_ref, columns))) + bias_ref[1:2])
+            if 2 <= o < width - 2:
+                value = value * mask_of(cols_ref[o], chans)
+            put(o, value)
+
+
+def inside_c(chans, hid_a, hid_b, cols_ref, w2_ref, bias_ref, after_ref, out_ref):
+    width = cols_ref.shape[0]
+    todo = ((2, 3), (4, 5), (0,), (1,), (width - 2,), (width - 1,))
+    second_columns(chans, todo, hid_a, hid_b, cols_ref, w2_ref, bias_ref, out_ref)
 
 
 def border(
-    cols_ref, top_ref, outer_ref, inner_ref, part_a, part_b, last_a, last_b, outp_ref, wt, w1_ref, bias_ref, w2_ref,
-    after_ref, out_hbm, slab_ref, sea_ref, line_ref, own_ref, hx, hid, outf, outb, sem,
+    cols_ref, outer_ref, inner_ref, part_a, part_b, last_a, last_b, outp_ref, wt, w1_ref, bias_ref, w2_ref, after_ref,
+    outf, line, own, hx, hid,
 ):
     chans, hidden = w1_ref.shape[2:]
     width, rows, _ = cols_ref.shape
-    held = outer_ref.shape[1]
+    rest = 2 * MAIN
     odd = lax.rem(lax.axis_index("lon"), 2) == 1
-    for c in range(2):
-        hx[c] = turned(jnp.where(odd, inner_ref[c, :held], outer_ref[c])).astype(BF)
-        hx[2 + c] = turned(jnp.where(odd, outer_ref[c], inner_ref[c, :held])).astype(BF)
-
-    def column(j):
-        return hx[j] if j < 2 else cols_ref[j - 2] if j < 2 + width else hx[j - width]
-
-    own_ref[...] = jnp.zeros_like(own_ref)
-    for j in range(width + 4):
-        own_ref[j : j + 1, :] = column(j)[rows - 16 :].astype(F32)[15:16]
     bias1 = bias_ref[0:1]
-    line_ref[...] = jnp.zeros_like(line_ref)
-    line_ref[2:6] = last_a[:4]
-    line_ref[6:width] = last_b[: width - 6]
-    for i, h in enumerate(edges(width)):
-        columns = [column(h + dx) if not 2 <= h + dx < 2 + width else None for dx in range(3)]
-        value = (part_a[0] if i == 0 else part_b[i - 1]) + summed(mm(first_taps(columns), first_weights(w1_ref, wt, columns)))
-        line_ref[h : h + 1, :] = value[rows - 1 :]
-        value = half_gelu(value + bias1, 0.5 * mask_of(column(h + 1), chans))
-        hid[i] = last_out(value).astype(BF)
+    outer, inner = outer_ref[...], inner_ref[:rows]
+    hx[0] = jnp.where(odd, inner, outer)
+    hx[1] = jnp.where(odd, outer, inner)
+
+    at = edges(width)
+    taken = (
+        (0, slice(0, rest), (0, 1), 1),
+        (0, slice(MAIN, rest), (0,), 0),
+        (1, slice(0, MAIN), (2,), 3),
+        (1, slice(0, rest), (1, 2), 2),
+    )
+    line[...] = jnp.zeros_like(line)
+    line[2 : 2 + 4] = last_a[:4]
+    line[6:width] = last_b[: width - 6]
+    for i, (side, main, dxs, slot) in enumerate(taken):
+        lhs = jnp.concatenate([hx[side, :, main], hx[side, :, rest:]], axis=1)
+        rhs = []
+        for dy in range(3):
+            block = wt[slot * SLOT : (slot + 2) * SLOT, dy * hidden : (dy + 1) * hidden]
+            rhs.append(jnp.concatenate([w1_ref[dy, dx, :MAIN, :] for dx in dxs] + [block], axis=0))
+        value = (part_a[0] if i == 0 else part_b[i - 1]) + summed(mm(lhs, jnp.concatenate(rhs, axis=1)))
+        line[at[i] : at[i] + 1, :] = value[rows - 1 :]
+        sea = chans - MAIN
+        if i == 0:
+            mask = hx[0, :, rest:].astype(F32)[:, SLOT + sea : SLOT + sea + 1]
+        elif i == 3:
+            mask = hx[1, :, rest:].astype(F32)[:, sea : sea + 1]
+        else:
+            mask = mask_of(cols_ref[at[i] - 1], chans)
+        hid[i] = last_out(half_gelu(value + bias1, 0.5 * mask)).astype(BF)
+
     for o in (0, 1, width - 2, width - 1):
-        columns = [hid[edges(width).index(o + dx)] if o + dx in edges(width) else None for dx in range(3)]
+        columns = [hid[at.index(o + dx)] if o + dx in at else None for dx in range(3)]
         have = [c for c in columns if c is not None]
         value = summed(mm(jnp.concatenate(have, axis=1), second_weights(w2_ref, columns)))
         mask = mask_of(cols_ref[o], chans)
         for i in range(hidden // LANES):
-            at = (i, pl.ds(o, rows, stride=width), slice(None))
-            outf[at] = (outp_ref[at] + value[:, i * LANES : (i + 1) * LANES]) * mask
-    step = rows // PIECES
-    place = lax.rem(lax.broadcasted_iota(jnp.int32, (step * width, LANES), 0), width)
-    edge = (place < 2) | (place >= width - 2)
-    copies = []
-    for p in range(PIECES):
-        at = slice(p * step * width, (p + 1) * step * width)
-        for i in range(hidden // LANES):
-            lanes = slice(i * LANES, (i + 1) * LANES)
-            value = jnp.where(edge, outf[i, at], outp_ref[i, at])
-            outb[p * step : (p + 1) * step, :, lanes] = value.reshape(step, width, LANES).astype(BF)
-            if p == PIECES - 1:
-                slab_ref[:, lanes] = value[(step - 2) * width :]
-        here = slice(p * step, (p + 1) * step)
-        copies.append(pltpu.make_async_copy(outb.at[here], out_hbm.at[here], sem.at[p]))
-        copies[-1].start()
-    sea = mask_of(top_ref[0], chans)
-    sea_ref[...] = jnp.broadcast_to(sea, sea_ref.shape)
-    for copy in copies:
-        copy.wait()
-
-
-def fold(
-    keep_ref, got_ref, slab_ref, sea_ref, line_ref, own_ref, wt, w1_ref, bias_ref, w2_ref, old_hbm,
+            to = (i, pl.ds(o, rows, stride=width), slice(None))
+            outf[to] = (outp_ref[to] + value[:, i * LANES : (i + 1) * LANES]) * mask
+    own[...] = jnp.zeros_like(own)
+    for j in range(width):
+        own[2 + j : 3 + j, :] = cols_ref[j, rows - 16 :].astype(F32)[15:16]
+    half = lax.broadcasted_iota(jnp.int32, (8, LANES), 1) < SLOT
+    for side, first in ((0, 0), (1, 2 + width)):
+        end = hx[side, rows - 16 :].astype(F32)[8:16]
+        tail = end[:, rest:]
+        turn = pltpu.roll(tail, SLOT, 1)
+        for c, both_halves in enumerate((jnp.where(half, tail, turn), jnp.where(half, turn, tail))):
+            full = jnp.concatenate([end[:, c * MAIN : (c + 1) * MAIN], both_halves], axis=1)
+            own[first + c : first + c + 1, :] = full[7:8]
+
+
+def finish(
+    keep_ref, got_ref, top_ref, outp_ref, outf, line, own, wt, w1_ref, bias_ref, w2_ref,
     out_hbm, m0, m1, r2, gs, hg, hz, outb, sem,
 ):
     chans, hidden = w1_ref.shape[2:]
     rows, width, _ = out_hbm.shape
     bias1 = bias_ref[0:1]
+    step = rows // PIECES
+    place = lax.rem(lax.broadcasted_iota(jnp.int32, (step * width, LANES), 0), width)
+    edge = (place < 2) | (place >= width - 2)
+    copies = []
+
+    def assemble(p, more):
+        here = slice(p * step, (p + 1) * step)
+        lines = slice(p * step * width, (p + 1) * step * width)
+        for i in range(hidden // LANES):
+            lanes = slice(i * LANES, (i + 1) * LANES)
+            value = jnp.where(edge, outf[i, lines], outp_ref[i, lines])
+            if more is not None:
+                end = (step - 2) * width
+                value = jnp.concatenate([value[:end], value[end:] + more[:, lanes]], axis=0)
+            outb[here, :, lanes] = value.reshape(step, width, LANES).astype(BF)
+        copies.append(pltpu.make_async_copy(outb.at[here], out_hbm.at[here], sem.at[p]))
+        copies[-1].start()
+
+    for p in range(PIECES - 1):
+        assemble(p, None)
     lane = lax.broadcasted_iota(jnp.int32, (1, WIDE), 1)
     sign = jnp.where(lane < chans // 2, -1.0, 1.0).astype(F32)
     both = keep_ref[...].astype(F32) + got_ref[...].astype(F32)
     for ref, value in ((m0, both[:16]), (m1, both[16:]), (gs, both[16:] * sign)):
         ref[:16] = value
         ref[16:] = jnp.zeros_like(ref[16:])
-    r2[...] = own_ref[...] * sign
+    r2[...] = own[...] * sign
 
     def taps(ref, offsets):
         return first_taps([ref[o : o + 16, :].astype(BF) for o in offsets])
@@ -337,19 +367,19 @@
     pre = mixed[16:]
     pre += mm(taps(m0, (2, 1, 0)), first_weights(w1_ref, wt, every, (0,)))
     pre += mm(taps(m1, (2, 1, 0)), first_weights(w1_ref, wt, every, (1,)))
-    hg[...] = jnp.zeros_like(hg)
-    hg[:16, :] = gelu(pre + bias1) * m1[1:17, chans : chans + 1]
-    hz[...] = jnp.zeros_like(hz)
-    hz[:16, :] = gelu(line_ref[...] + mixed[:16] + bias1) * own_ref[1:17, chans : chans + 1]
+    hg[16:] = jnp.zeros_like(hg[16:])
+    hg[:16] = gelu(pre + bias1) * m1[1:17, chans : chans + 1]
+    hz[16:] = jnp.zeros_like(hz[16:])
+    hz[:16] = gelu(line[...] + mixed[:16] + bias1) * own[1:17, chans : chans + 1]
     wide = [jnp.concatenate([ref[o : o + 16, :].astype(BF) for o in range(3)], axis=1) for ref in (hz, hg)]
     more = mm(jnp.concatenate(wide, axis=0), second_weights(w2_ref, every, (1, 2)))
     below = more[:width, hidden:]
     level = more[:width, :hidden] + more[16 : 16 + width, hidden:]
-    value = slab_ref[...] + jnp.concatenate([below, level], axis=0) * sea_ref[...]
-    outb[...] = value.reshape(2, width, hidden).astype(BF)
-    copy = pltpu.make_async_copy(outb, out_hbm.at[rows - 2 : rows], sem)
-    copy.start()
-    copy.wait()
+    fixed = jnp.concatenate([below, level], axis=0) * mask_of(top_ref[0], chans)
+
+    assemble(PIECES - 1, fixed)
+    for copy in copies:
+        copy.wait()
 
 
 def local(state, ocean_mask, fold_map, w_first, b_first, w_second, b_second):
@@ -373,8 +403,8 @@
     sent, inner, cols, top, bias, pick, w_first, w_second = pl.pallas_call(
         prepare,
         out_shape=(
-            shape((2, held, rows), BF),
-            shape((2, held + 2 * width, rows), BF),
+            shape((rows, 2 * MAIN + LANES), BF),
+            shape((rows + 2 * width, 2 * MAIN + LANES), BF),
             shape((width, rows, WIDE), BF),
             shape((1, 2 * width, WIDE), BF),
             shape((2, hidden), F32),
@@ -405,7 +435,7 @@
         out_shape=(
             shape((before, rows, hidden), BF),
             shape((8, hidden), F32),
-            shape((4 * SLOT, 3 * hidden), BF),
+            shape((5 * SLOT, 3 * hidden), BF),
             shape((1, rows, hidden), F32),
         ),
         in_specs=[vmem] * 3,
@@ -428,10 +458,12 @@
             name="inside_b",
         )(cols, w_first, bias, wt, after)
 
+    field = shape((hidden // LANES, rows * width, LANES), F32)
+
     def stage_c(hid_b, after):
         return pl.pallas_call(
             functools.partial(inside_c, chans),
-            out_shape=shape((hidden // LANES, rows * width, LANES), F32),
+            out_shape=field,
             in_specs=[vmem] * 6,
             out_specs=vmem,
             compiler_params=limit(12),
@@ -453,18 +485,18 @@
         got = lax.ppermute(tops, "lon", [(i, i ^ step) for i in range(n)])
         if step == 2:
             outer = lax.ppermute(sent, "lon", [(i, (i + 1 if i % 2 else i - 1) % n) for i in range(n)])
+        if step == n // 4:
             hid_b, last_b, part_b = stage_b(tops)
-        if step == n // 4:
             outp = stage_c(hid_b, tops)
             break
         tops = pl.pallas_call(
             join,
             out_shape=shape((2 * tops.shape[0],) + tops.shape[1:], BF),
-            in_specs=[vmem] * 3,
+            in_specs=[vmem] * 2,
             out_specs=vmem,
             compiler_params=limit(4),
             name="join",
-        )(tops, got, last_b)
+        )(tops, got)
         step *= 2
     lines = shape((32, WIDE), BF)
     give, keep = pl.pallas_call(
@@ -476,39 +508,26 @@
         name="choose",
     )(pick, tops, got, outp)
     got = lax.ppermute(give, "lon", [(i, i ^ (n // 2)) for i in range(n)])
-    out, slab, sea, line, own = pl.pallas_call(
+    outf, line, own = pl.pallas_call(
         border,
-        out_shape=(
-            shape((rows, width, hidden), BF),
-            shape((2 * width, hidden), F32),
-            shape((2 * width, hidden), F32),
-            shape((16, hidden), F32),
-            shape((24, WIDE), F32),
-        ),
-        in_specs=[vmem] * 14,
-        out_specs=(hbm,) + (vmem,) * 4,
-        scratch_shapes=[
-            scratch((4, rows, WIDE), BF),
-            scratch((4, rows, hidden), BF),
-            scratch((hidden // LANES, rows * width, LANES), F32),
-            scratch((rows, width, hidden), BF),
-            dma((PIECES,)),
-        ],
-        compiler_params=limit(16),
+        out_shape=(field, shape((16, hidden), F32), shape((24, WIDE), F32)),
+        in_specs=[vmem] * 13,
+        out_specs=(vmem,) * 3,
+        scratch_shapes=[scratch((2, rows, 2 * MAIN + LANES), BF), scratch((4, rows, hidden), BF)],
+        compiler_params=limit(14),
         name="border",
-    )(cols, top, outer, inner, part_a, part_b, last_a, last_b, outp, wt, w_first, bias, w_second, give)
+    )(cols, outer, inner, part_a, part_b, last_a, last_b, outp, wt, w_first, bias, w_second, give)
     return pl.pallas_call(
-        fold,
+        finish,
         out_shape=shape((rows, width, hidden), BF),
-        in_specs=[vmem] * 10 + [hbm],
+        in_specs=[vmem] * 11,
         out_specs=hbm,
         scratch_shapes=[scratch((24, WIDE), F32)] * 4
         + [scratch((24, hidden), F32)] * 2
-        + [scratch((2, width, hidden), BF), dma],
-        input_output_aliases={10: 0},
-        compiler_params=limit(10),
-        name="fold",
-    )(keep, got, slab, sea, line, own, wt, w_first, bias, w_second, out)
+        + [scratch((rows, width, hidden), BF), dma((PIECES,))],
+        compiler_params=limit(14),
+        name="finish",
+    )(keep, got, top, outp, outf, line, own, wt, w_first, bias, w_second)
 
 
 def solution(mesh):

time: 29.3 us -> 30.2 us (1.031)
  waiting for transfers between devices: 3.67 us -> 5.97 us
  Pallas kernels: 14 us -> 12.8 us
    ppermute x2, waiting for transfers between devices: 3.66 us -> 5.96 us  [local(): got = lax.ppermute(tops, 'lon', [(i, i ^ step) for i in range(n)])]
    pallas_call x4, Pallas kernels: 9.7 us -> 8.54 us  [the longest x1 2.26 us: stage_c(): pl.pallas_call(functools.partial(inside_c, chans), out_shape=field, in_sp...]
  transfers between devices with their start and end apart: 5 -> 5, of which waited for: 1 -> 1; matrix products, arithmetic and copies ran while one was open for 0% -> 0% of each run, Pallas kernels for 35% -> 29%
where the time goes in v5:
time: 30.2 us; the launch traced here: 30 us
  Pallas kernels  12.8 us (42%)
  starting transfers between devices  11.1 us (37%)
  waiting for transfers between devices  5.97 us (20%)
    ppermute x2, waiting for transfers between devices, local(): got = lax.ppermute(tops, 'lon', [(i, i ^ step) for i in range(n)])  5.96 us
    ppermute x1, starting transfers between devices, local(): lax.ppermute(sent, 'lon', [(i, (i + 1 if i % 2 else i - 1) % n) for i in...  5.72 us
    ppermute x1, starting transfers between devices, local(): got = lax.ppermute(give, 'lon', [(i, i ^ n // 2) for i in range(n)])  2.65 us
    pallas_call x1, Pallas kernels, stage_c(): pl.pallas_call(functools.partial(inside_c, chans), out_shape=field, in_sp...  2.26 us
    pallas_call x1, Pallas kernels, local(): pl.pallas_call(prepare, out_shape=(shape((rows, 2 * MAIN + LANES), BF), s...  2.25 us
    pallas_call x1, Pallas kernels, local(): pl.pallas_call(border, out_shape=(field, shape((16, hidden), F32), shape(...  2.25 us
    ppermute x2, starting transfers between devices, local(): got = lax.ppermute(tops, 'lon', [(i, i ^ step) for i in range(n)])  2.18 us
    pallas_call x1, Pallas kernels, local(): pl.pallas_call(inside_a, out_shape=(shape((before, rows, hidden), BF), sh...  2.17 us
  transfers between devices with their start and end apart: 5, of which 1 were waited for; matrix products, arithmetic and copies ran while one was open for 0% of the time, Pallas kernels for 29%

profile of v5, /device:TPU:0, one launch (start us, length us, event | category | flops | bytes accessed | tf_op | source)
XLA Modules:
  0.0 30.0 jit_solution(4396202872816091059)
XLA Ops:
  0.0 2.3 %prepare.1 = (bf16[256,640]{1,0:T(8,128)(2,1)S(1)}, bf16[272,640]{1,0:T(8,128)(2,1)S(1)}, bf16[8,256,384]{2,1,0:T(8,128)(2,1)S(1)}, bf16[1,16,384]{2,1,0:T(8,128...) custom-call(s32[128]{0:T(128)} %fold_hbm.1, ...), custom_call_target="tpu_custom_call" | custom-call | tf_op jit(solution)/shard_map/prepare/pallas_call | solution.py:403
  2.3 0.6 %collective-permute-start = (bf16[272,640]{1,0:T(8,128)(2,1)S(1)}, bf16[272,640]{1,0:T(8,128)(2,1)S(1)}, u32[]{:S(2)}, u32[]{:S(2)}) collective-permute-start(bf16[272,640]{1,0:T(8,128)(2,1)S(1)} %get-tuple-element.29), channel_id=1, source_target_pairs={{0,1},{1,0},{2,3},{3,2},{4,5},{5,4},{6,7},{7,6},{8,9},{9,8},{10,11... | collective-permute-start | bytes 1044488 | tf_op jit(solution)/shard_map/ppermute | solution.py:430
  2.8 2.2 %inside_a.1 = (bf16[4,256,256]{2,1,0:T(8,128)(2,1)S(1)}, f32[8,256]{1,0:T(8,128)S(1)}, bf16[320,768]{1,0:T(8,128)(2,1)S(1)}, f32[1,256,256]{2,1,0:T(8,128)S(1)}) custom-call(bf16[8,256,384]{2,1,0:T(8,128)(2,1)S(1)} %get-tuple-element.30.cols_ref, bf16[3,3,300,256]{3,2,1,0:T(8,128)(2,1)S(1)} %get-tuple-element.31.w1_ref, f32[2,256]{1,0:T(2,128)S(1)} %get-tuple-element.32.bias_ref), custom_call_target="tpu_custom_call" | custom-call | tf_op jit(solution)/shard_map/inside_a/pallas_call | solution.py:433
  5.0 0.0 collective-permute-done.got_ref.inner_ref
  5.0 5.7 %collective-permute-start.4 = (bf16[256,640]{1,0:T(8,128)(2,1)S(1)}, bf16[256,640]{1,0:T(8,128)(2,1)S(1)}, u32[]{:S(2)}, u32[]{:S(2)}) collective-permute-start(bf16[256,640]{1,0:T(8,128)(2,1)S(1)} %get-tuple-element.42), channel_id=1, source_target_pairs={{0,15},{1,2},{2,1},{3,4},{4,3},{5,6},{6,5},{7,8},{8,7},{9,10},{10,... | collective-permute-start | bytes 983048 | tf_op jit(solution)/shard_map/ppermute | solution.py:487
  10.7 0.0 collective-permute-start.1
  10.7 6.0 %collective-permute-done.1.got_ref = bf16[2,16,384]{2,1,0:T(8,128)(2,1)S(1)} collective-permute-done((bf16[2,16,384]{2,1,0:T(8,128)(2,1)S(1)}, bf16[2,16,384]{2,1,0:T(8,128)(2,1)S(1)}, u32[]{:S(2)}, u32[]{:S(2)}) %collective-permute-start.1) | collective-permute-done | bytes 24608 | tf_op jit(solution)/shard_map/ppermute | solution.py:485
  16.7 2.2 %collective-permute-start.2 = (bf16[4,16,384]{2,1,0:T(8,128)(2,1)S(1)}, bf16[4,16,384]{2,1,0:T(8,128)(2,1)S(1)}, u32[]{:S(2)}, u32[]{:S(2)}) collective-permute-start(bf16[4,16,384]{2,1,0:T(8,128)(2,1)S(1)} %join.1.after_ref.mine_ref), channel_id=1, source_target_pairs={{0,4},{1,5},{2,6},{3,7},{4,0},{5,1},{6,2},{7,3},{8,12},{9,13},{10,... | collective-permute-start | bytes 147464 | tf_op jit(solution)/shard_map/ppermute | solution.py:485
  18.9 1.9 %inside_b.1 = (bf16[2,256,256]{2,1,0:T(8,128)(2,1)S(1)}, f32[8,256]{1,0:T(8,128)S(1)}, f32[3,256,256]{2,1,0:T(8,128)S(1)}) custom-call(bf16[8,256,384]{2,1,0:T(8,128)(2,1)S(1)} %get-tuple-element.30.cols_ref, bf16[3,3,300,256]{3,2,1,0:T(8,128)(2,1)S(1)} %get-tuple-element.31.w1_ref, f32[2,256]{1,0:T(2,128)S(1)} %get-tuple-element.32.bias_ref, ...), custom_call_target="tpu_custom_call" | custom-call | tf_op jit(solution)/shard_map/inside_b/pallas_call | solution.py:448
  20.8 2.3 %inside_c.1.after_ref.outp_ref = f32[2,2048,128]{2,1,0:T(8,128)S(1)} custom-call(bf16[4,256,256]{2,1,0:T(8,128)(2,1)S(1)} %get-tuple-element.36.hid_a, bf16[2,256,256]{2,1,0:T(8,128)(2,1)S(1)} %get-tuple-element.38.hid_b, bf16[8,256,384]{2,1,0:T(8,128)(2,1)S(1)} %get-tuple-element.30.cols_ref, bf16[3,3,256,256]{3,2,1,0:T(8,128)(2,1)S(1)} %get-tuple-element.39.w2_ref, ...), custom_call_target="tpu_custom_call" | custom-call | tf_op jit(solution)/shard_map/inside_c/pallas_call | solution.py:464
  23.1 0.0 collective-permute-done.2.got_ref
  23.1 0.2 choose.1
  23.3 2.7 %collective-permute-start.3 = (bf16[32,384]{1,0:T(8,128)(2,1)S(1)}, bf16[32,384]{1,0:T(8,128)(2,1)S(1)}, u32[]{:S(2)}, u32[]{:S(2)}) collective-permute-start(bf16[32,384]{1,0:T(8,128)(2,1)S(1)} %get-tuple-element.41.after_ref), channel_id=1, source_target_pairs={{0,8},{1,9},{2,10},{3,11},{4,12},{5,13},{6,14},{7,15},{8,0},{9,1},... | collective-permute-start | bytes 73736 | tf_op jit(solution)/shard_map/ppermute | solution.py:510
  25.9 0.0 collective-permute-done.4.outer_ref
  25.9 2.2 %border.1 = (f32[2,2048,128]{2,1,0:T(8,128)S(1)}, f32[16,256]{1,0:T(8,128)S(1)}, f32[24,384]{1,0:T(8,128)S(1)}) custom-call(bf16[8,256,384]{2,1,0:T(8,128)(2,1)S(1)} %get-tuple-element.30.cols_ref, bf16[256,640]{1,0:T(8,128)(2,1)S(1)} %collective-permute-done.4.outer_ref, bf16[272,640]{1,0:T(8,128)(2,1)S(1)} %collective-permute-done.got_ref.inner_ref, ...), custom_call_target="tpu_custom_call" | custom-call | tf_op jit(solution)/shard_map/border/pallas_call | solution.py:511
  28.2 0.0 collective-permute-done.3.got_ref
  28.2 1.8 %finish.1 = bf16[256,8,256]{2,1,0:T(8,128)(2,1)} custom-call(bf16[32,384]{1,0:T(8,128)(2,1)S(1)} %get-tuple-element.40.keep_ref, bf16[32,384]{1,0:T(8,128)(2,1)S(1)} %collective-permute-done.3.got_ref, bf16[1,16,384]{2,1,0:T(8,128)(2,1)S(1)} %get-tuple-element.28.mine_ref.top_ref, f32[2,2048,128]{2,1,0:T(8,128)S(1)} %inside_c.1.after_ref.outp_ref, ...), custom_call_target="tpu_custom_call" | custom-call | tf_op jit(solution)/shard_map/finish/pallas_call | solution.py:520
  (2 shorter events, 0.0 us)
Async XLA Ops:
  2.3 2.7 %collective-permute-start = (bf16[272,640]{1,0:T(8,128)(2,1)S(1)}, bf16[272,640]{1,0:T(8,128)(2,1)S(1)}, u32[]{:S(2)}, u32[]{:S(2)}) collective-permute-start(bf16[272,640]{1,0:T(8,128)(2,1)S(1)} %get-tuple-element.29), channel_id=1, source_target_pairs={{0,1},{1,0},{2,3},{3,2},{4,5},{5,4},{6,7},{7,6},{8,9},{9,8},{10,11... | collective-permute-start | bytes 1044488 | tf_op jit(solution)/shard_map/ppermute | solution.py:430
  5.0 20.9 %collective-permute-start.4 = (bf16[256,640]{1,0:T(8,128)(2,1)S(1)}, bf16[256,640]{1,0:T(8,128)(2,1)S(1)}, u32[]{:S(2)}, u32[]{:S(2)}) collective-permute-start(bf16[256,640]{1,0:T(8,128)(2,1)S(1)} %get-tuple-element.42), channel_id=1, source_target_pairs={{0,15},{1,2},{2,1},{3,4},{4,3},{5,6},{6,5},{7,8},{8,7},{9,10},{10,... | collective-permute-start | bytes 983048 | tf_op jit(solution)/shard_map/ppermute | solution.py:487
  10.7 6.0 %collective-permute-start.1 = (bf16[2,16,384]{2,1,0:T(8,128)(2,1)S(1)}, bf16[2,16,384]{2,1,0:T(8,128)(2,1)S(1)}, u32[]{:S(2)}, u32[]{:S(2)}) collective-permute-start(bf16[2,16,384]{2,1,0:T(8,128)(2,1)S(1)} %get-tuple-element.35.mine_ref), channel_id=1, source_target_pairs={{0,2},{1,3},{2,0},{3,1},{4,6},{5,7},{6,4},{7,5},{8,10},{9,11},{10,... | collective-permute-start | bytes 73736 | tf_op jit(solution)/shard_map/ppermute | solution.py:485
  16.7 6.4 %collective-permute-start.2 = (bf16[4,16,384]{2,1,0:T(8,128)(2,1)S(1)}, bf16[4,16,384]{2,1,0:T(8,128)(2,1)S(1)}, u32[]{:S(2)}, u32[]{:S(2)}) collective-permute-start(bf16[4,16,384]{2,1,0:T(8,128)(2,1)S(1)} %join.1.after_ref.mine_ref), channel_id=1, source_target_pairs={{0,4},{1,5},{2,6},{3,7},{4,0},{5,1},{6,2},{7,3},{8,12},{9,13},{10,... | collective-permute-start | bytes 147464 | tf_op jit(solution)/shard_map/ppermute | solution.py:485
  23.3 4.9 %collective-permute-start.3 = (bf16[32,384]{1,0:T(8,128)(2,1)S(1)}, bf16[32,384]{1,0:T(8,128)(2,1)S(1)}, u32[]{:S(2)}, u32[]{:S(2)}) collective-permute-start(bf16[32,384]{1,0:T(8,128)(2,1)S(1)} %get-tuple-element.41.after_ref), channel_id=1, source_target_pairs={{0,8},{1,9},{2,10},{3,11},{4,12},{5,13},{6,14},{7,15},{8,0},{9,1},... | collective-permute-start | bytes 73736 | tf_op jit(solution)/shard_map/ppermute | solution.py:510

commit v6 on v5

--- a/solution.py
+++ b/solution.py
@@ -8,8 +8,8 @@
 from jax.sharding import PartitionSpec as P
 
 BF, F32 = jnp.bfloat16, jnp.float32
-LANES, MAIN, SLOT, PIECES = 128, 256, 64, 4
-GROUP = 2
+LANES, MAIN, SLOT, PIECES, CUTS = 128, 256, 64, 4, 4
+GROUP, BEFORE = 2, 3
 WIDE = MAIN + 2 * SLOT
 
 
@@ -35,43 +35,41 @@
 
 
 def prepare(
-    fold_hbm, x_hbm, mask_hbm, b1_hbm, b2_hbm, w1_hbm, w2_hbm,
-    outer_ref, inner_ref, cols_ref, top_ref, bias_ref, pick_ref, w1_ref, w2_ref,
+    fold_hbm, x_hbm, mask_hbm, b1_hbm, b2_hbm, w1_hbm,
+    outer_ref, inner_ref, cols_ref, top_ref, bias_ref, pick_ref, w1_ref,
     x_ref, mask_ref, fold_ref, field, sem,
 ):
     chans, width, rows = x_ref.shape
     held = field.shape[1] // width
     me = lax.axis_index("lon")
-    cuts = [chans * i // PIECES for i in range(PIECES + 1)]
+    halves = [slice(i * LANES, (i + 1) * LANES) for i in range(rows // LANES)]
+    parts = CUTS // len(halves)
+    cuts = [chans * i // parts for i in range(parts + 1)]
+    spans = [(i, at, lo, hi) for i, at in enumerate(halves) for lo, hi in zip(cuts, cuts[1:])]
     pairs = [(mask_hbm, mask_ref)]
-    pairs += [(x_hbm.at[lo:hi], x_ref.at[lo:hi]) for lo, hi in zip(cuts, cuts[1:])]
+    pairs += [(x_hbm.at[lo:hi, :, at], x_ref.at[lo:hi, :, at]) for _, at, lo, hi in spans]
     pairs += [(b1_hbm, bias_ref.at[0:1]), (b2_hbm, bias_ref.at[1:2]), (fold_hbm, fold_ref)]
-    pairs += [(w1_hbm, w1_ref), (w2_hbm, w2_ref)]
+    pairs += [(w1_hbm, w1_ref)]
     copies = [pltpu.make_async_copy(src, dst, sem.at[i]) for i, (src, dst) in enumerate(pairs)]
     for copy in copies:
         copy.start()
     odd = lax.rem(me, 2) == 1
     copies[0].wait()
     mask = mask_ref[...].astype(F32)
-    halves = [slice(i * LANES, (i + 1) * LANES) for i in range(rows // LANES)]
-    for i, at in enumerate(halves):
+    last = []
+    for (i, at, lo, hi), copy in zip(spans, copies[1:]):
+        copy.wait()
+        block = x_ref[lo:hi, :, at].astype(F32) * mask[None, :, at]
+        field[i, lo * width : hi * width, :] = block.reshape((hi - lo) * width, LANES)
+        if hi < chans:
+            continue
         field[i, chans * width : (chans + 1) * width, :] = mask[:, at]
         field[i, (chans + 1) * width :, :] = jnp.zeros(((held - chans - 1) * width, LANES), F32)
-    for lo, hi, copy in zip(cuts, cuts[1:], copies[1:]):
-        copy.wait()
-        for i, at in enumerate(halves):
-            block = x_ref[lo:hi, :, at].astype(F32) * mask[None, :, at]
-            field[i, lo * width : hi * width, :] = block.reshape((hi - lo) * width, LANES)
-
-    def column(c):
-        parts = [field[i, pl.ds(c, held, stride=width), :] for i in range(rows // LANES)]
-        return jnp.concatenate(parts, axis=1).astype(BF)
-
-    last = []
-    for c in range(width):
-        out = turned(column(c))
-        cols_ref[c] = out.astype(BF)
-        last.append(out[rows - 2 :])
+        for c in range(width):
+            out = turned(field[i, pl.ds(c, held, stride=width), :].astype(BF))
+            cols_ref[c, at] = out.astype(BF)
+            if at.stop == rows:
+                last.append(out[LANES - 2 :])
     lanes = lax.broadcasted_iota(jnp.int32, (rows, LANES), 1)
 
     def message(c):
@@ -85,7 +83,7 @@
     top = jnp.concatenate([v[i : i + 1] for i in range(2) for v in last], axis=0).astype(BF)
     top_ref[0] = top
     inner_ref[rows:] = jnp.concatenate([top, jnp.zeros((2 * width, inner_ref.shape[1] - WIDE), BF)], axis=1)
-    for copy in copies[1 + PIECES :]:
+    for copy in copies[1 + CUTS :]:
         copy.wait()
     total = fold_ref.shape[0]
     n = total // width
@@ -204,10 +202,11 @@
     rows = cols_ref.shape[1]
     last_ref[...] = jnp.zeros_like(last_ref)
     for i in range(0, hid_ref.shape[0], GROUP):
-        sets = [[own_column(cols_ref, first + i + g + dx) for dx in range(3)] for g in range(GROUP)]
+        group = range(min(GROUP, hid_ref.shape[0] - i))
+        sets = [[own_column(cols_ref, first + i + g + dx) for dx in range(3)] for g in group]
         lhs = jnp.concatenate([first_taps(columns) for columns in sets], axis=0)
         out = mm(lhs, first_weights(w1_ref, wt, sets[0]))
-        for g in range(GROUP):
+        for g in group:
             value = summed(out[g * rows : (g + 1) * rows])
             last_ref[i + g : i + g + 1, :] = value[rows - 1 :]
             value = half_gelu(value + bias_ref[0:1], 0.5 * mask_of(sets[g][1], chans))
@@ -217,15 +216,17 @@
         part_ref[i] = summed(mm(first_taps(columns), first_weights(w1_ref, wt, columns)))
 
 
-def inside_a(cols_ref, w1_ref, bias_ref, hid_ref, last_ref, wt_ref, part_ref):
+def inside_a(cols_ref, w1_ref, bias_ref, w2_hbm, hid_ref, last_ref, wt_ref, w2_ref, sem):
+    copy = pltpu.make_async_copy(w2_hbm, w2_ref, sem)
+    copy.start()
     tail_weights(w1_ref, wt_ref)
-    width = cols_ref.shape[0]
-    hidden_columns(cols_ref, w1_ref, bias_ref, wt_ref, hid_ref, last_ref, 2, part_ref, edges(width)[:1])
+    hidden_columns(cols_ref, w1_ref, bias_ref, wt_ref, hid_ref, last_ref, 2, None, ())
+    copy.wait()
 
 
 def inside_b(before, cols_ref, w1_ref, bias_ref, wt_ref, after_ref, hid_ref, last_ref, part_ref):
     width = cols_ref.shape[0]
-    hidden_columns(cols_ref, w1_ref, bias_ref, wt_ref, hid_ref, last_ref, 2 + before, part_ref, edges(width)[1:])
+    hidden_columns(cols_ref, w1_ref, bias_ref, wt_ref, hid_ref, last_ref, 2 + before, part_ref, edges(width))
 
 
 def second_columns(chans, todo, hid_a, hid_b, cols_ref, w2_ref, bias_ref, out_ref):
@@ -262,7 +263,7 @@
 
 
 def border(
-    cols_ref, outer_ref, inner_ref, part_a, part_b, last_a, last_b, outp_ref, wt, w1_ref, bias_ref, w2_ref, after_ref,
+    cols_ref, outer_ref, inner_ref, part_ref, last_a, last_b, outp_ref, wt, w1_ref, bias_ref, w2_ref, after_ref,
     outf, line, own, hx, hid,
 ):
     chans, hidden = w1_ref.shape[2:]
@@ -282,15 +283,15 @@
         (1, slice(0, rest), (1, 2), 2),
     )
     line[...] = jnp.zeros_like(line)
-    line[2 : 2 + 4] = last_a[:4]
-    line[6:width] = last_b[: width - 6]
+    line[2 : 2 + BEFORE] = last_a[:BEFORE]
+    line[2 + BEFORE : width] = last_b[: width - 2 - BEFORE]
     for i, (side, main, dxs, slot) in enumerate(taken):
         lhs = jnp.concatenate([hx[side, :, main], hx[side, :, rest:]], axis=1)
         rhs = []
         for dy in range(3):
             block = wt[slot * SLOT : (slot + 2) * SLOT, dy * hidden : (dy + 1) * hidden]
             rhs.append(jnp.concatenate([w1_ref[dy, dx, :MAIN, :] for dx in dxs] + [block], axis=0))
-        value = (part_a[0] if i == 0 else part_b[i - 1]) + summed(mm(lhs, jnp.concatenate(rhs, axis=1)))
+        value = part_ref[i] + summed(mm(lhs, jnp.concatenate(rhs, axis=1)))
         line[at[i] : at[i] + 1, :] = value[rows - 1 :]
         sea = chans - MAIN
         if i == 0:
@@ -329,25 +330,25 @@
     chans, hidden = w1_ref.shape[2:]
     rows, width, _ = out_hbm.shape
     bias1 = bias_ref[0:1]
-    step = rows // PIECES
-    place = lax.rem(lax.broadcasted_iota(jnp.int32, (step * width, LANES), 0), width)
-    edge = (place < 2) | (place >= width - 2)
+    ends = [rows * p // PIECES for p in range(PIECES)] + [rows - 8, rows]
     copies = []
 
     def assemble(p, more):
-        here = slice(p * step, (p + 1) * step)
-        lines = slice(p * step * width, (p + 1) * step * width)
+        lo, hi = ends[p], ends[p + 1]
+        here, lines = slice(lo, hi), slice(lo * width, hi * width)
+        place = lax.rem(lax.broadcasted_iota(jnp.int32, ((hi - lo) * width, LANES), 0), width)
+        edge = (place < 2) | (place >= width - 2)
         for i in range(hidden // LANES):
             lanes = slice(i * LANES, (i + 1) * LANES)
             value = jnp.where(edge, outf[i, lines], outp_ref[i, lines])
             if more is not None:
-                end = (step - 2) * width
+                end = (hi - lo - 2) * width
                 value = jnp.concatenate([value[:end], value[end:] + more[:, lanes]], axis=0)
-            outb[here, :, lanes] = value.reshape(step, width, LANES).astype(BF)
+            outb[here, :, lanes] = value.reshape(hi - lo, width, LANES).astype(BF)
         copies.append(pltpu.make_async_copy(outb.at[here], out_hbm.at[here], sem.at[p]))
         copies[-1].start()
 
-    for p in range(PIECES - 1):
+    for p in range(PIECES):
         assemble(p, None)
     lane = lax.broadcasted_iota(jnp.int32, (1, WIDE), 1)
     sign = jnp.where(lane < chans // 2, -1.0, 1.0).astype(F32)
@@ -377,7 +378,7 @@
     level = more[:width, :hidden] + more[16 : 16 + width, hidden:]
     fixed = jnp.concatenate([below, level], axis=0) * mask_of(top_ref[0], chans)
 
-    assemble(PIECES - 1, fixed)
+    assemble(PIECES, fixed)
     for copy in copies:
         copy.wait()
 
@@ -400,7 +401,7 @@
     def far(value):
         return pltpu.with_memory_space_constraint(value, pltpu.MemorySpace.HBM)
 
-    sent, inner, cols, top, bias, pick, w_first, w_second = pl.pallas_call(
+    sent, inner, cols, top, bias, pick, w_first = pl.pallas_call(
         prepare,
         out_shape=(
             shape((rows, 2 * MAIN + LANES), BF),
@@ -410,39 +411,39 @@
             shape((2, hidden), F32),
             shape((64, LANES), jnp.int32),
             shape(w_first.shape, BF),
-            shape(w_second.shape, BF),
         ),
-        in_specs=[hbm] * 7,
-        out_specs=(vmem,) * 8,
+        in_specs=[hbm] * 6,
+        out_specs=(vmem,) * 7,
         scratch_shapes=[
             scratch((chans, width, rows), BF),
             scratch((width, rows), jnp.int32),
             pltpu.SMEM(fold_map.shape, jnp.int32),
             scratch((rows // LANES, held * width, LANES), F32),
-            dma((PIECES + 6,)),
+            dma((CUTS + 5,)),
         ],
         compiler_params=limit(14),
         name="prepare",
     )(
         far(fold_map), far(state.transpose(2, 1, 0)), far(ocean_mask.T),
-        far(b_first[None]), far(b_second[None]), far(w_first), far(w_second),
+        far(b_first[None]), far(b_second[None]), far(w_first),
     )
     inner = lax.ppermute(inner, "lon", [(i, i ^ 1) for i in range(n)])
 
-    before = 4
-    hid_a, last_a, wt, part_a = pl.pallas_call(
+    before = BEFORE
+    hid_a, last_a, wt, w_second = pl.pallas_call(
         inside_a,
         out_shape=(
             shape((before, rows, hidden), BF),
             shape((8, hidden), F32),
             shape((5 * SLOT, 3 * hidden), BF),
-            shape((1, rows, hidden), F32),
+            shape(w_second.shape, BF),
         ),
-        in_specs=[vmem] * 3,
+        in_specs=[vmem] * 3 + [hbm],
         out_specs=(vmem,) * 4,
+        scratch_shapes=[dma],
         compiler_params=limit(12),
         name="inside_a",
-    )(cols, w_first, bias)
+    )(cols, w_first, bias, far(w_second))
 
     def stage_b(after):
         return pl.pallas_call(
@@ -450,7 +451,7 @@
             out_shape=(
                 shape((width - 2 - before, rows, hidden), BF),
                 shape((8, hidden), F32),
-                shape((3, rows, hidden), F32),
+                shape((4, rows, hidden), F32),
             ),
             in_specs=[vmem] * 5,
             out_specs=(vmem,) * 3,
@@ -511,12 +512,12 @@
     outf, line, own = pl.pallas_call(
         border,
         out_shape=(field, shape((16, hidden), F32), shape((24, WIDE), F32)),
-        in_specs=[vmem] * 13,
+        in_specs=[vmem] * 12,
         out_specs=(vmem,) * 3,
         scratch_shapes=[scratch((2, rows, 2 * MAIN + LANES), BF), scratch((4, rows, hidden), BF)],
         compiler_params=limit(14),
         name="border",
-    )(cols, outer, inner, part_a, part_b, last_a, last_b, outp, wt, w_first, bias, w_second, give)
+    )(cols, outer, inner, part_b, last_a, last_b, outp, wt, w_first, bias, w_second, give)
     return pl.pallas_call(
         finish,
         out_shape=shape((rows, width, hidden), BF),
@@ -524,7 +525,7 @@
         out_specs=hbm,
         scratch_shapes=[scratch((24, WIDE), F32)] * 4
         + [scratch((24, hidden), F32)] * 2
-        + [scratch((rows, width, hidden), BF), dma((PIECES,))],
+        + [scratch((rows, width, hidden), BF), dma((PIECES + 1,))],
         compiler_params=limit(14),
         name="finish",
     )(keep, got, top, outp, outf, line, own, wt, w_first, bias, w_second)

time: 30.2 us -> 30.2 us (level)
    pallas_call x1, Pallas kernels: 1.91 us -> 2.55 us  [stage_b(): pl.pallas_call(functools.partial(inside_b, before), out_shape=(shape((wid...]
    pallas_call x1, Pallas kernels: 2.17 us -> 1.56 us  [local(): pl.pallas_call(inside_a, out_shape=(shape((before, rows, hidden), BF), sh...]
where the time goes in v6:
time: 30.2 us; the launch traced here: 30 us
  Pallas kernels  12.8 us (42%)
  starting transfers between devices  11.1 us (37%)
  waiting for transfers between devices  5.97 us (20%)
    ppermute x2, waiting for transfers between devices, local(): got = lax.ppermute(tops, 'lon', [(i, i ^ step) for i in range(n)])  5.96 us
    ppermute x1, starting transfers between devices, local(): lax.ppermute(sent, 'lon', [(i, (i + 1 if i % 2 else i - 1) % n) for i in...  5.72 us
    ppermute x1, starting transfers between devices, local(): got = lax.ppermute(give, 'lon', [(i, i ^ n // 2) for i in range(n)])  2.66 us
    pallas_call x1, Pallas kernels, stage_b(): pl.pallas_call(functools.partial(inside_b, before), out_shape=(shape((wid...  2.55 us
    pallas_call x1, Pallas kernels, local(): pl.pallas_call(prepare, out_shape=(shape((rows, 2 * MAIN + LANES), BF), s...  2.29 us
    pallas_call x1, Pallas kernels, local(): pl.pallas_call(border, out_shape=(field, shape((16, hidden), F32), shape(...  2.27 us
    pallas_call x1, Pallas kernels, stage_c(): pl.pallas_call(functools.partial(inside_c, chans), out_shape=field, in_sp...  2.22 us
    ppermute x2, starting transfers between devices, local(): got = lax.ppermute(tops, 'lon', [(i, i ^ step) for i in range(n)])  2.17 us
  transfers between devices with their start and end apart: 5, of which 1 were waited for; matrix products, arithmetic and copies ran while one was open for 0% of the time, Pallas kernels for 29%

profile of v6, /device:TPU:0, one launch (start us, length us, event | category | flops | bytes accessed | tf_op | source)
XLA Modules:
  0.0 30.0 jit_solution(2529676335508160670)
XLA Ops:
  0.0 2.3 %prepare.1 = (bf16[256,640]{1,0:T(8,128)(2,1)S(1)}, bf16[272,640]{1,0:T(8,128)(2,1)S(1)}, bf16[8,256,384]{2,1,0:T(8,128)(2,1)S(1)}, bf16[1,16,384]{2,1,0:T(8,128...) custom-call(s32[128]{0:T(128)} %fold_hbm.1, ...), custom_call_target="tpu_custom_call" | custom-call | tf_op jit(solution)/shard_map/prepare/pallas_call | solution.py:404
  2.3 0.6 %collective-permute-start = (bf16[272,640]{1,0:T(8,128)(2,1)S(1)}, bf16[272,640]{1,0:T(8,128)(2,1)S(1)}, u32[]{:S(2)}, u32[]{:S(2)}) collective-permute-start(bf16[272,640]{1,0:T(8,128)(2,1)S(1)} %get-tuple-element.28), channel_id=1, source_target_pairs={{0,1},{1,0},{2,3},{3,2},{4,5},{5,4},{6,7},{7,6},{8,9},{9,8},{10,11... | collective-permute-start | bytes 1044488 | tf_op jit(solution)/shard_map/ppermute | solution.py:430
  2.9 1.6 %inside_a.1 = (bf16[3,256,256]{2,1,0:T(8,128)(2,1)S(1)}, f32[8,256]{1,0:T(8,128)S(1)}, bf16[320,768]{1,0:T(8,128)(2,1)S(1)}, bf16[3,3,256,256]{3,2,1,0:T(8,128)(2,1)S(1)}) custom-call(bf16[8,256,384]{2,1,0:T(8,128)(2,1)S(1)} %get-tuple-element.29.cols_ref, bf16[3,3,300,256]{3,2,1,0:T(8,128)(2,1)S(1)} %get-tuple-element.30.w1_ref, ...), custom_call_target="tpu_custom_call" | custom-call | tf_op jit(solution)/shard_map/inside_a/pallas_call | solution.py:433
  4.4 0.0 collective-permute-done.got_ref.inner_ref
  4.5 5.7 %collective-permute-start.4 = (bf16[256,640]{1,0:T(8,128)(2,1)S(1)}, bf16[256,640]{1,0:T(8,128)(2,1)S(1)}, u32[]{:S(2)}, u32[]{:S(2)}) collective-permute-start(bf16[256,640]{1,0:T(8,128)(2,1)S(1)} %get-tuple-element.41), channel_id=1, source_target_pairs={{0,15},{1,2},{2,1},{3,4},{4,3},{5,6},{6,5},{7,8},{8,7},{9,10},{10,... | collective-permute-start | bytes 983048 | tf_op jit(solution)/shard_map/ppermute | solution.py:488
  10.2 0.0 collective-permute-start.1
  10.2 6.0 %collective-permute-done.1.got_ref = bf16[2,16,384]{2,1,0:T(8,128)(2,1)S(1)} collective-permute-done((bf16[2,16,384]{2,1,0:T(8,128)(2,1)S(1)}, bf16[2,16,384]{2,1,0:T(8,128)(2,1)S(1)}, u32[]{:S(2)}, u32[]{:S(2)}) %collective-permute-start.1) | collective-permute-done | bytes 24608 | tf_op jit(solution)/shard_map/ppermute | solution.py:486
  16.1 2.2 %collective-permute-start.2 = (bf16[4,16,384]{2,1,0:T(8,128)(2,1)S(1)}, bf16[4,16,384]{2,1,0:T(8,128)(2,1)S(1)}, u32[]{:S(2)}, u32[]{:S(2)}) collective-permute-start(bf16[4,16,384]{2,1,0:T(8,128)(2,1)S(1)} %join.1.after_ref.mine_ref), channel_id=1, source_target_pairs={{0,4},{1,5},{2,6},{3,7},{4,0},{5,1},{6,2},{7,3},{8,12},{9,13},{10,... | collective-permute-start | bytes 147464 | tf_op jit(solution)/shard_map/ppermute | solution.py:486
  18.3 2.6 %inside_b.1 = (bf16[3,256,256]{2,1,0:T(8,128)(2,1)S(1)}, f32[8,256]{1,0:T(8,128)S(1)}, f32[4,256,256]{2,1,0:T(8,128)S(1)}) custom-call(bf16[8,256,384]{2,1,0:T(8,128)(2,1)S(1)} %get-tuple-element.29.cols_ref, bf16[3,3,300,256]{3,2,1,0:T(8,128)(2,1)S(1)} %get-tuple-element.30.w1_ref, f32[2,256]{1,0:T(2,128)S(1)} %get-tuple-element.31.bias_ref, ...), custom_call_target="tpu_custom_call" | custom-call | tf_op jit(solution)/shard_map/inside_b/pallas_call | solution.py:449
  20.9 2.2 %inside_c.1.after_ref.outp_ref = f32[2,2048,128]{2,1,0:T(8,128)S(1)} custom-call(bf16[3,256,256]{2,1,0:T(8,128)(2,1)S(1)} %get-tuple-element.35.hid_a, bf16[3,256,256]{2,1,0:T(8,128)(2,1)S(1)} %get-tuple-element.37.hid_b, bf16[8,256,384]{2,1,0:T(8,128)(2,1)S(1)} %get-tuple-element.29.cols_ref, bf16[3,3,256,256]{3,2,1,0:T(8,128)(2,1)S(1)} %get-tuple-element.38.w2_ref, ...), custom_call_target="tpu_custom_call" | custom-call | tf_op jit(solution)/shard_map/inside_c/pallas_call | solution.py:465
  23.1 0.0 collective-permute-done.2.got_ref
  23.1 0.2 choose.1
  23.3 2.7 %collective-permute-start.3 = (bf16[32,384]{1,0:T(8,128)(2,1)S(1)}, bf16[32,384]{1,0:T(8,128)(2,1)S(1)}, u32[]{:S(2)}, u32[]{:S(2)}) collective-permute-start(bf16[32,384]{1,0:T(8,128)(2,1)S(1)} %get-tuple-element.40.after_ref), channel_id=1, source_target_pairs={{0,8},{1,9},{2,10},{3,11},{4,12},{5,13},{6,14},{7,15},{8,0},{9,1},... | collective-permute-start | bytes 73736 | tf_op jit(solution)/shard_map/ppermute | solution.py:511
  26.0 0.0 collective-permute-done.4.outer_ref
  26.0 2.3 %border.1 = (f32[2,2048,128]{2,1,0:T(8,128)S(1)}, f32[16,256]{1,0:T(8,128)S(1)}, f32[24,384]{1,0:T(8,128)S(1)}) custom-call(bf16[8,256,384]{2,1,0:T(8,128)(2,1)S(1)} %get-tuple-element.29.cols_ref, bf16[256,640]{1,0:T(8,128)(2,1)S(1)} %collective-permute-done.4.outer_ref, bf16[272,640]{1,0:T(8,128)(2,1)S(1)} %collective-permute-done.got_ref.inner_ref, ...), custom_call_target="tpu_custom_call" | custom-call | tf_op jit(solution)/shard_map/border/pallas_call | solution.py:512
  28.3 0.0 collective-permute-done.3.got_ref
  28.3 1.7 %finish.1 = bf16[256,8,256]{2,1,0:T(8,128)(2,1)} custom-call(bf16[32,384]{1,0:T(8,128)(2,1)S(1)} %get-tuple-element.39.keep_ref, bf16[32,384]{1,0:T(8,128)(2,1)S(1)} %collective-permute-done.3.got_ref, bf16[1,16,384]{2,1,0:T(8,128)(2,1)S(1)} %get-tuple-element.27.mine_ref.top_ref, f32[2,2048,128]{2,1,0:T(8,128)S(1)} %inside_c.1.after_ref.outp_ref, ...), custom_call_target="tpu_custom_call" | custom-call | tf_op jit(solution)/shard_map/finish/pallas_call | solution.py:521
  (2 shorter events, 0.0 us)
Async XLA Ops:
  2.3 2.1 %collective-permute-start = (bf16[272,640]{1,0:T(8,128)(2,1)S(1)}, bf16[272,640]{1,0:T(8,128)(2,1)S(1)}, u32[]{:S(2)}, u32[]{:S(2)}) collective-permute-start(bf16[272,640]{1,0:T(8,128)(2,1)S(1)} %get-tuple-element.28), channel_id=1, source_target_pairs={{0,1},{1,0},{2,3},{3,2},{4,5},{5,4},{6,7},{7,6},{8,9},{9,8},{10,11... | collective-permute-start | bytes 1044488 | tf_op jit(solution)/shard_map/ppermute | solution.py:430
  4.5 21.5 %collective-permute-start.4 = (bf16[256,640]{1,0:T(8,128)(2,1)S(1)}, bf16[256,640]{1,0:T(8,128)(2,1)S(1)}, u32[]{:S(2)}, u32[]{:S(2)}) collective-permute-start(bf16[256,640]{1,0:T(8,128)(2,1)S(1)} %get-tuple-element.41), channel_id=1, source_target_pairs={{0,15},{1,2},{2,1},{3,4},{4,3},{5,6},{6,5},{7,8},{8,7},{9,10},{10,... | collective-permute-start | bytes 983048 | tf_op jit(solution)/shard_map/ppermute | solution.py:488
  10.2 6.0 %collective-permute-start.1 = (bf16[2,16,384]{2,1,0:T(8,128)(2,1)S(1)}, bf16[2,16,384]{2,1,0:T(8,128)(2,1)S(1)}, u32[]{:S(2)}, u32[]{:S(2)}) collective-permute-start(bf16[2,16,384]{2,1,0:T(8,128)(2,1)S(1)} %get-tuple-element.34.mine_ref), channel_id=1, source_target_pairs={{0,2},{1,3},{2,0},{3,1},{4,6},{5,7},{6,4},{7,5},{8,10},{9,11},{10,... | collective-permute-start | bytes 73736 | tf_op jit(solution)/shard_map/ppermute | solution.py:486
  16.1 7.0 %collective-permute-start.2 = (bf16[4,16,384]{2,1,0:T(8,128)(2,1)S(1)}, bf16[4,16,384]{2,1,0:T(8,128)(2,1)S(1)}, u32[]{:S(2)}, u32[]{:S(2)}) collective-permute-start(bf16[4,16,384]{2,1,0:T(8,128)(2,1)S(1)} %join.1.after_ref.mine_ref), channel_id=1, source_target_pairs={{0,4},{1,5},{2,6},{3,7},{4,0},{5,1},{6,2},{7,3},{8,12},{9,13},{10,... | collective-permute-start | bytes 147464 | tf_op jit(solution)/shard_map/ppermute | solution.py:486
  23.3 4.9 %collective-permute-start.3 = (bf16[32,384]{1,0:T(8,128)(2,1)S(1)}, bf16[32,384]{1,0:T(8,128)(2,1)S(1)}, u32[]{:S(2)}, u32[]{:S(2)}) collective-permute-start(bf16[32,384]{1,0:T(8,128)(2,1)S(1)} %get-tuple-element.40.after_ref), channel_id=1, source_target_pairs={{0,8},{1,9},{2,10},{3,11},{4,12},{5,13},{6,14},{7,15},{8,0},{9,1},... | collective-permute-start | bytes 73736 | tf_op jit(solution)/shard_map/ppermute | solution.py:511

commit v7 on v6

--- a/solution.py
+++ b/solution.py
@@ -54,37 +54,7 @@
     for copy in copies:
         copy.start()
     odd = lax.rem(me, 2) == 1
-    copies[0].wait()
-    mask = mask_ref[...].astype(F32)
-    last = []
-    for (i, at, lo, hi), copy in zip(spans, copies[1:]):
-        copy.wait()
-        block = x_ref[lo:hi, :, at].astype(F32) * mask[None, :, at]
-        field[i, lo * width : hi * width, :] = block.reshape((hi - lo) * width, LANES)
-        if hi < chans:
-            continue
-        field[i, chans * width : (chans + 1) * width, :] = mask[:, at]
-        field[i, (chans + 1) * width :, :] = jnp.zeros(((held - chans - 1) * width, LANES), F32)
-        for c in range(width):
-            out = turned(field[i, pl.ds(c, held, stride=width), :].astype(BF))
-            cols_ref[c, at] = out.astype(BF)
-            if at.stop == rows:
-                last.append(out[LANES - 2 :])
-    lanes = lax.broadcasted_iota(jnp.int32, (rows, LANES), 1)
-
-    def message(c):
-        first, second = cols_ref[c], cols_ref[c + 1]
-        rest = jnp.where(lanes < SLOT, first[:, MAIN:][:, :LANES], second[:, MAIN:][:, :LANES])
-        return jnp.concatenate([first[:, :MAIN], second[:, :MAIN], rest], axis=1)
-
-    low, high = message(0), message(width - 2)
-    outer_ref[...] = jnp.where(odd, high, low)
-    inner_ref[:rows] = jnp.where(odd, low, high)
-    top = jnp.concatenate([v[i : i + 1] for i in range(2) for v in last], axis=0).astype(BF)
-    top_ref[0] = top
-    inner_ref[rows:] = jnp.concatenate([top, jnp.zeros((2 * width, inner_ref.shape[1] - WIDE), BF)], axis=1)
-    for copy in copies[1 + CUTS :]:
-        copy.wait()
+    copies[3 + CUTS].wait()
     total = fold_ref.shape[0]
     n = total // width
     index = lax.broadcasted_iota(jnp.int32, pick_ref.shape, 0)
@@ -97,6 +67,39 @@
     block = lax.bitwise_xor(lax.shift_right_logical(col, width.bit_length() - 1), me)
     spot = block * (2 * width) + line * width + (col & (width - 1))
     pick_ref[...] = jnp.where((block < n // 2) & (j < width + 4), spot, -1)
+    copies[0].wait()
+    mask = mask_ref[...].astype(F32)
+    last = []
+    for (i, at, lo, hi), copy in zip(spans, copies[1:]):
+        copy.wait()
+        block = x_ref[lo:hi, :, at].astype(F32) * mask[None, :, at]
+        field[i, lo * width : hi * width, :] = block.reshape((hi - lo) * width, LANES)
+        if hi < chans:
+            continue
+        field[i, chans * width : (chans + 1) * width, :] = mask[:, at]
+        field[i, (chans + 1) * width :, :] = jnp.zeros(((held - chans - 1) * width, LANES), F32)
+    for i, at in enumerate(halves):
+        for c in range(width):
+            out = turned(field[i, pl.ds(c, held, stride=width), :].astype(BF))
+            cols_ref[c, at] = out.astype(BF)
+            if at.stop == rows:
+                last.append(out[LANES - 2 :])
+    lanes = lax.broadcasted_iota(jnp.int32, (rows, LANES), 1)
+
+    def message(c):
+        first, second = cols_ref[c], cols_ref[c + 1]
+        rest = jnp.where(lanes < SLOT, first[:, MAIN:][:, :LANES], second[:, MAIN:][:, :LANES])
+        return jnp.concatenate([first[:, :MAIN], second[:, :MAIN], rest], axis=1)
+
+    low, high = message(0), message(width - 2)
+    outer_ref[...] = jnp.where(odd, high, low)
+    inner_ref[:rows] = jnp.where(odd, low, high)
+    top = jnp.concatenate([v[i : i + 1] for i in range(2) for v in last], axis=0).astype(BF)
+    top_ref[0] = top
+    inner_ref[rows:] = jnp.concatenate([top, jnp.zeros((2 * width, inner_ref.shape[1] - WIDE), BF)], axis=1)
+    for k, copy in enumerate(copies[1 + CUTS :]):
+        if k != 2:
+            copy.wait()
 
 
 def join_first(mine_ref, got_ref, after_ref, sent_ref, out_ref, pass_ref):

time: 30.2 us -> 30 us (level)
  no operation moved by 1% of the time
where the time goes in v7:
time: 30 us; the launch traced here: 29.9 us
  Pallas kernels  12.7 us (42%)
  starting transfers between devices  11.1 us (37%)
  waiting for transfers between devices  5.96 us (20%)
    ppermute x2, waiting for transfers between devices, local(): got = lax.ppermute(tops, 'lon', [(i, i ^ step) for i in range(n)])  5.95 us
    ppermute x1, starting transfers between devices, local(): lax.ppermute(sent, 'lon', [(i, (i + 1 if i % 2 else i - 1) % n) for i in...  5.72 us
    ppermute x1, starting transfers between devices, local(): got = lax.ppermute(give, 'lon', [(i, i ^ n // 2) for i in range(n)])  2.66 us
    pallas_call x1, Pallas kernels, stage_b(): pl.pallas_call(functools.partial(inside_b, before), out_shape=(shape((wid...  2.55 us
    pallas_call x1, Pallas kernels, local(): pl.pallas_call(border, out_shape=(field, shape((16, hidden), F32), shape(...  2.25 us
    pallas_call x1, Pallas kernels, stage_c(): pl.pallas_call(functools.partial(inside_c, chans), out_shape=field, in_sp...  2.22 us
    pallas_call x1, Pallas kernels, local(): pl.pallas_call(prepare, out_shape=(shape((rows, 2 * MAIN + LANES), BF), s...  2.19 us
    ppermute x2, starting transfers between devices, local(): got = lax.ppermute(tops, 'lon', [(i, i ^ step) for i in range(n)])  2.18 us
  transfers between devices with their start and end apart: 5, of which 1 were waited for; matrix products, arithmetic and copies ran while one was open for 0% of the time, Pallas kernels for 29%

profile of v7, /device:TPU:0, one launch (start us, length us, event | category | flops | bytes accessed | tf_op | source)
XLA Modules:
  0.0 29.9 jit_solution(5346415519217110175)
XLA Ops:
  0.0 2.2 %prepare.1 = (bf16[256,640]{1,0:T(8,128)(2,1)S(1)}, bf16[272,640]{1,0:T(8,128)(2,1)S(1)}, bf16[8,256,384]{2,1,0:T(8,128)(2,1)S(1)}, bf16[1,16,384]{2,1,0:T(8,128...) custom-call(s32[128]{0:T(128)} %fold_hbm.1, ...), custom_call_target="tpu_custom_call" | custom-call | tf_op jit(solution)/shard_map/prepare/pallas_call | solution.py:407
  2.2 0.6 %collective-permute-start = (bf16[272,640]{1,0:T(8,128)(2,1)S(1)}, bf16[272,640]{1,0:T(8,128)(2,1)S(1)}, u32[]{:S(2)}, u32[]{:S(2)}) collective-permute-start(bf16[272,640]{1,0:T(8,128)(2,1)S(1)} %get-tuple-element.28), channel_id=1, source_target_pairs={{0,1},{1,0},{2,3},{3,2},{4,5},{5,4},{6,7},{7,6},{8,9},{9,8},{10,11... | collective-permute-start | bytes 1044488 | tf_op jit(solution)/shard_map/ppermute | solution.py:433
  2.8 1.6 %inside_a.1 = (bf16[3,256,256]{2,1,0:T(8,128)(2,1)S(1)}, f32[8,256]{1,0:T(8,128)S(1)}, bf16[320,768]{1,0:T(8,128)(2,1)S(1)}, bf16[3,3,256,256]{3,2,1,0:T(8,128)(2,1)S(1)}) custom-call(bf16[8,256,384]{2,1,0:T(8,128)(2,1)S(1)} %get-tuple-element.29.cols_ref, bf16[3,3,300,256]{3,2,1,0:T(8,128)(2,1)S(1)} %get-tuple-element.30.w1_ref, ...), custom_call_target="tpu_custom_call" | custom-call | tf_op jit(solution)/shard_map/inside_a/pallas_call | solution.py:436
  4.3 0.0 collective-permute-done.got_ref.inner_ref
  4.4 5.7 %collective-permute-start.4 = (bf16[256,640]{1,0:T(8,128)(2,1)S(1)}, bf16[256,640]{1,0:T(8,128)(2,1)S(1)}, u32[]{:S(2)}, u32[]{:S(2)}) collective-permute-start(bf16[256,640]{1,0:T(8,128)(2,1)S(1)} %get-tuple-element.41), channel_id=1, source_target_pairs={{0,15},{1,2},{2,1},{3,4},{4,3},{5,6},{6,5},{7,8},{8,7},{9,10},{10,... | collective-permute-start | bytes 983048 | tf_op jit(solution)/shard_map/ppermute | solution.py:491
  10.1 0.0 collective-permute-start.1
  10.1 5.9 %collective-permute-done.1.got_ref = bf16[2,16,384]{2,1,0:T(8,128)(2,1)S(1)} collective-permute-done((bf16[2,16,384]{2,1,0:T(8,128)(2,1)S(1)}, bf16[2,16,384]{2,1,0:T(8,128)(2,1)S(1)}, u32[]{:S(2)}, u32[]{:S(2)}) %collective-permute-start.1) | collective-permute-done | bytes 24608 | tf_op jit(solution)/shard_map/ppermute | solution.py:489
  16.0 2.2 %collective-permute-start.2 = (bf16[4,16,384]{2,1,0:T(8,128)(2,1)S(1)}, bf16[4,16,384]{2,1,0:T(8,128)(2,1)S(1)}, u32[]{:S(2)}, u32[]{:S(2)}) collective-permute-start(bf16[4,16,384]{2,1,0:T(8,128)(2,1)S(1)} %join.1.after_ref.mine_ref), channel_id=1, source_target_pairs={{0,4},{1,5},{2,6},{3,7},{4,0},{5,1},{6,2},{7,3},{8,12},{9,13},{10,... | collective-permute-start | bytes 147464 | tf_op jit(solution)/shard_map/ppermute | solution.py:489
  18.2 2.6 %inside_b.1 = (bf16[3,256,256]{2,1,0:T(8,128)(2,1)S(1)}, f32[8,256]{1,0:T(8,128)S(1)}, f32[4,256,256]{2,1,0:T(8,128)S(1)}) custom-call(bf16[8,256,384]{2,1,0:T(8,128)(2,1)S(1)} %get-tuple-element.29.cols_ref, bf16[3,3,300,256]{3,2,1,0:T(8,128)(2,1)S(1)} %get-tuple-element.30.w1_ref, f32[2,256]{1,0:T(2,128)S(1)} %get-tuple-element.31.bias_ref, ...), custom_call_target="tpu_custom_call" | custom-call | tf_op jit(solution)/shard_map/inside_b/pallas_call | solution.py:452
  20.8 2.2 %inside_c.1.after_ref.outp_ref = f32[2,2048,128]{2,1,0:T(8,128)S(1)} custom-call(bf16[3,256,256]{2,1,0:T(8,128)(2,1)S(1)} %get-tuple-element.35.hid_a, bf16[3,256,256]{2,1,0:T(8,128)(2,1)S(1)} %get-tuple-element.37.hid_b, bf16[8,256,384]{2,1,0:T(8,128)(2,1)S(1)} %get-tuple-element.29.cols_ref, bf16[3,3,256,256]{3,2,1,0:T(8,128)(2,1)S(1)} %get-tuple-element.38.w2_ref, ...), custom_call_target="tpu_custom_call" | custom-call | tf_op jit(solution)/shard_map/inside_c/pallas_call | solution.py:468
  23.0 0.0 collective-permute-done.2.got_ref
  23.0 0.2 choose.1
  23.2 2.7 %collective-permute-start.3 = (bf16[32,384]{1,0:T(8,128)(2,1)S(1)}, bf16[32,384]{1,0:T(8,128)(2,1)S(1)}, u32[]{:S(2)}, u32[]{:S(2)}) collective-permute-start(bf16[32,384]{1,0:T(8,128)(2,1)S(1)} %get-tuple-element.40.after_ref), channel_id=1, source_target_pairs={{0,8},{1,9},{2,10},{3,11},{4,12},{5,13},{6,14},{7,15},{8,0},{9,1},... | collective-permute-start | bytes 73736 | tf_op jit(solution)/shard_map/ppermute | solution.py:514
  25.9 0.0 collective-permute-done.4.outer_ref
  25.9 2.3 %border.1 = (f32[2,2048,128]{2,1,0:T(8,128)S(1)}, f32[16,256]{1,0:T(8,128)S(1)}, f32[24,384]{1,0:T(8,128)S(1)}) custom-call(bf16[8,256,384]{2,1,0:T(8,128)(2,1)S(1)} %get-tuple-element.29.cols_ref, bf16[256,640]{1,0:T(8,128)(2,1)S(1)} %collective-permute-done.4.outer_ref, bf16[272,640]{1,0:T(8,128)(2,1)S(1)} %collective-permute-done.got_ref.inner_ref, ...), custom_call_target="tpu_custom_call" | custom-call | tf_op jit(solution)/shard_map/border/pallas_call | solution.py:515
  28.1 0.0 collective-permute-done.3.got_ref
  28.1 1.7 %finish.1 = bf16[256,8,256]{2,1,0:T(8,128)(2,1)} custom-call(bf16[32,384]{1,0:T(8,128)(2,1)S(1)} %get-tuple-element.39.keep_ref, bf16[32,384]{1,0:T(8,128)(2,1)S(1)} %collective-permute-done.3.got_ref, bf16[1,16,384]{2,1,0:T(8,128)(2,1)S(1)} %get-tuple-element.27.mine_ref.top_ref, f32[2,2048,128]{2,1,0:T(8,128)S(1)} %inside_c.1.after_ref.outp_ref, ...), custom_call_target="tpu_custom_call" | custom-call | tf_op jit(solution)/shard_map/finish/pallas_call | solution.py:524
  (2 shorter events, 0.0 us)
Async XLA Ops:
  2.2 2.1 %collective-permute-start = (bf16[272,640]{1,0:T(8,128)(2,1)S(1)}, bf16[272,640]{1,0:T(8,128)(2,1)S(1)}, u32[]{:S(2)}, u32[]{:S(2)}) collective-permute-start(bf16[272,640]{1,0:T(8,128)(2,1)S(1)} %get-tuple-element.28), channel_id=1, source_target_pairs={{0,1},{1,0},{2,3},{3,2},{4,5},{5,4},{6,7},{7,6},{8,9},{9,8},{10,11... | collective-permute-start | bytes 1044488 | tf_op jit(solution)/shard_map/ppermute | solution.py:433
  4.4 21.5 %collective-permute-start.4 = (bf16[256,640]{1,0:T(8,128)(2,1)S(1)}, bf16[256,640]{1,0:T(8,128)(2,1)S(1)}, u32[]{:S(2)}, u32[]{:S(2)}) collective-permute-start(bf16[256,640]{1,0:T(8,128)(2,1)S(1)} %get-tuple-element.41), channel_id=1, source_target_pairs={{0,15},{1,2},{2,1},{3,4},{4,3},{5,6},{6,5},{7,8},{8,7},{9,10},{10,... | collective-permute-start | bytes 983048 | tf_op jit(solution)/shard_map/ppermute | solution.py:491
  10.1 6.0 %collective-permute-start.1 = (bf16[2,16,384]{2,1,0:T(8,128)(2,1)S(1)}, bf16[2,16,384]{2,1,0:T(8,128)(2,1)S(1)}, u32[]{:S(2)}, u32[]{:S(2)}) collective-permute-start(bf16[2,16,384]{2,1,0:T(8,128)(2,1)S(1)} %get-tuple-element.34.mine_ref), channel_id=1, source_target_pairs={{0,2},{1,3},{2,0},{3,1},{4,6},{5,7},{6,4},{7,5},{8,10},{9,11},{10,... | collective-permute-start | bytes 73736 | tf_op jit(solution)/shard_map/ppermute | solution.py:489
  16.0 7.0 %collective-permute-start.2 = (bf16[4,16,384]{2,1,0:T(8,128)(2,1)S(1)}, bf16[4,16,384]{2,1,0:T(8,128)(2,1)S(1)}, u32[]{:S(2)}, u32[]{:S(2)}) collective-permute-start(bf16[4,16,384]{2,1,0:T(8,128)(2,1)S(1)} %join.1.after_ref.mine_ref), channel_id=1, source_target_pairs={{0,4},{1,5},{2,6},{3,7},{4,0},{5,1},{6,2},{7,3},{8,12},{9,13},{10,... | collective-permute-start | bytes 147464 | tf_op jit(solution)/shard_map/ppermute | solution.py:489
  23.2 4.9 %collective-permute-start.3 = (bf16[32,384]{1,0:T(8,128)(2,1)S(1)}, bf16[32,384]{1,0:T(8,128)(2,1)S(1)}, u32[]{:S(2)}, u32[]{:S(2)}) collective-permute-start(bf16[32,384]{1,0:T(8,128)(2,1)S(1)} %get-tuple-element.40.after_ref), channel_id=1, source_target_pairs={{0,8},{1,9},{2,10},{3,11},{4,12},{5,13},{6,14},{7,15},{8,0},{9,1},... | collective-permute-start | bytes 73736 | tf_op jit(solution)/shard_map/ppermute | solution.py:514

commit v8 on v7

--- a/solution.py
+++ b/solution.py
@@ -348,11 +348,18 @@
                 end = (hi - lo - 2) * width
                 value = jnp.concatenate([value[:end], value[end:] + more[:, lanes]], axis=0)
             outb[here, :, lanes] = value.reshape(hi - lo, width, LANES).astype(BF)
+
+    def send(p):
+        here = slice(ends[p], ends[p + 1])
         copies.append(pltpu.make_async_copy(outb.at[here], out_hbm.at[here], sem.at[p]))
         copies[-1].start()
 
-    for p in range(PIECES):
-        assemble(p, None)
+    assemble(0, None)
+    send(0)
+    assemble(1, None)
+    send(1)
+    assemble(2, None)
+    send(2)
     lane = lax.broadcasted_iota(jnp.int32, (1, WIDE), 1)
     sign = jnp.where(lane < chans // 2, -1.0, 1.0).astype(F32)
     both = keep_ref[...].astype(F32) + got_ref[...].astype(F32)
@@ -375,6 +382,8 @@
     hg[:16] = gelu(pre + bias1) * m1[1:17, chans : chans + 1]
     hz[16:] = jnp.zeros_like(hz[16:])
     hz[:16] = gelu(line[...] + mixed[:16] + bias1) * own[1:17, chans : chans + 1]
+    assemble(3, None)
+    send(3)
     wide = [jnp.concatenate([ref[o : o + 16, :].astype(BF) for o in range(3)], axis=1) for ref in (hz, hg)]
     more = mm(jnp.concatenate(wide, axis=0), second_weights(w2_ref, every, (1, 2)))
     below = more[:width, hidden:]
@@ -382,6 +391,7 @@
     fixed = jnp.concatenate([below, level], axis=0) * mask_of(top_ref[0], chans)
 
     assemble(PIECES, fixed)
+    send(PIECES)
     for copy in copies:
         copy.wait()
 

time: 30 us -> 30 us (level)
  no operation moved by 1% of the time
where the time goes in v8:
time: 30 us; the launch traced here: 29.9 us
  Pallas kernels  12.7 us (42%)
  starting transfers between devices  11.1 us (37%)
  waiting for transfers between devices  5.96 us (20%)
    ppermute x2, waiting for transfers between devices, local(): got = lax.ppermute(tops, 'lon', [(i, i ^ step) for i in range(n)])  5.95 us
    ppermute x1, starting transfers between devices, local(): lax.ppermute(sent, 'lon', [(i, (i + 1 if i % 2 else i - 1) % n) for i in...  5.72 us
    ppermute x1, starting transfers between devices, local(): got = lax.ppermute(give, 'lon', [(i, i ^ n // 2) for i in range(n)])  2.66 us
    pallas_call x1, Pallas kernels, stage_b(): pl.pallas_call(functools.partial(inside_b, before), out_shape=(shape((wid...  2.55 us
    pallas_call x1, Pallas kernels, local(): pl.pallas_call(border, out_shape=(field, shape((16, hidden), F32), shape(...  2.25 us
    pallas_call x1, Pallas kernels, stage_c(): pl.pallas_call(functools.partial(inside_c, chans), out_shape=field, in_sp...  2.22 us
    pallas_call x1, Pallas kernels, local(): pl.pallas_call(prepare, out_shape=(shape((rows, 2 * MAIN + LANES), BF), s...  2.19 us
    ppermute x2, starting transfers between devices, local(): got = lax.ppermute(tops, 'lon', [(i, i ^ step) for i in range(n)])  2.18 us
  transfers between devices with their start and end apart: 5, of which 1 were waited for; matrix products, arithmetic and copies ran while one was open for 0% of the time, Pallas kernels for 29%

profile of v8, /device:TPU:0, one launch (start us, length us, event | category | flops | bytes accessed | tf_op | source)
XLA Modules:
  0.0 29.9 jit_solution(5346415519217110175)
XLA Ops:
  0.0 2.2 %prepare.1 = (bf16[256,640]{1,0:T(8,128)(2,1)S(1)}, bf16[272,640]{1,0:T(8,128)(2,1)S(1)}, bf16[8,256,384]{2,1,0:T(8,128)(2,1)S(1)}, bf16[1,16,384]{2,1,0:T(8,128...) custom-call(s32[128]{0:T(128)} %fold_hbm.1, ...), custom_call_target="tpu_custom_call" | custom-call | tf_op jit(solution)/shard_map/prepare/pallas_call | solution.py:417
  2.2 0.6 %collective-permute-start = (bf16[272,640]{1,0:T(8,128)(2,1)S(1)}, bf16[272,640]{1,0:T(8,128)(2,1)S(1)}, u32[]{:S(2)}, u32[]{:S(2)}) collective-permute-start(bf16[272,640]{1,0:T(8,128)(2,1)S(1)} %get-tuple-element.28), channel_id=1, source_target_pairs={{0,1},{1,0},{2,3},{3,2},{4,5},{5,4},{6,7},{7,6},{8,9},{9,8},{10,11... | collective-permute-start | bytes 1044488 | tf_op jit(solution)/shard_map/ppermute | solution.py:443
  2.8 1.6 %inside_a.1 = (bf16[3,256,256]{2,1,0:T(8,128)(2,1)S(1)}, f32[8,256]{1,0:T(8,128)S(1)}, bf16[320,768]{1,0:T(8,128)(2,1)S(1)}, bf16[3,3,256,256]{3,2,1,0:T(8,128)(2,1)S(1)}) custom-call(bf16[8,256,384]{2,1,0:T(8,128)(2,1)S(1)} %get-tuple-element.29.cols_ref, bf16[3,3,300,256]{3,2,1,0:T(8,128)(2,1)S(1)} %get-tuple-element.30.w1_ref, ...), custom_call_target="tpu_custom_call" | custom-call | tf_op jit(solution)/shard_map/inside_a/pallas_call | solution.py:446
  4.3 0.0 collective-permute-done.got_ref.inner_ref
  4.4 5.7 %collective-permute-start.4 = (bf16[256,640]{1,0:T(8,128)(2,1)S(1)}, bf16[256,640]{1,0:T(8,128)(2,1)S(1)}, u32[]{:S(2)}, u32[]{:S(2)}) collective-permute-start(bf16[256,640]{1,0:T(8,128)(2,1)S(1)} %get-tuple-element.41), channel_id=1, source_target_pairs={{0,15},{1,2},{2,1},{3,4},{4,3},{5,6},{6,5},{7,8},{8,7},{9,10},{10,... | collective-permute-start | bytes 983048 | tf_op jit(solution)/shard_map/ppermute | solution.py:501
  10.1 0.0 collective-permute-start.1
  10.1 5.9 %collective-permute-done.1.got_ref = bf16[2,16,384]{2,1,0:T(8,128)(2,1)S(1)} collective-permute-done((bf16[2,16,384]{2,1,0:T(8,128)(2,1)S(1)}, bf16[2,16,384]{2,1,0:T(8,128)(2,1)S(1)}, u32[]{:S(2)}, u32[]{:S(2)}) %collective-permute-start.1) | collective-permute-done | bytes 24608 | tf_op jit(solution)/shard_map/ppermute | solution.py:499
  16.0 2.2 %collective-permute-start.2 = (bf16[4,16,384]{2,1,0:T(8,128)(2,1)S(1)}, bf16[4,16,384]{2,1,0:T(8,128)(2,1)S(1)}, u32[]{:S(2)}, u32[]{:S(2)}) collective-permute-start(bf16[4,16,384]{2,1,0:T(8,128)(2,1)S(1)} %join.1.after_ref.mine_ref), channel_id=1, source_target_pairs={{0,4},{1,5},{2,6},{3,7},{4,0},{5,1},{6,2},{7,3},{8,12},{9,13},{10,... | collective-permute-start | bytes 147464 | tf_op jit(solution)/shard_map/ppermute | solution.py:499
  18.2 2.6 %inside_b.1 = (bf16[3,256,256]{2,1,0:T(8,128)(2,1)S(1)}, f32[8,256]{1,0:T(8,128)S(1)}, f32[4,256,256]{2,1,0:T(8,128)S(1)}) custom-call(bf16[8,256,384]{2,1,0:T(8,128)(2,1)S(1)} %get-tuple-element.29.cols_ref, bf16[3,3,300,256]{3,2,1,0:T(8,128)(2,1)S(1)} %get-tuple-element.30.w1_ref, f32[2,256]{1,0:T(2,128)S(1)} %get-tuple-element.31.bias_ref, ...), custom_call_target="tpu_custom_call" | custom-call | tf_op jit(solution)/shard_map/inside_b/pallas_call | solution.py:462
  20.8 2.2 %inside_c.1.after_ref.outp_ref = f32[2,2048,128]{2,1,0:T(8,128)S(1)} custom-call(bf16[3,256,256]{2,1,0:T(8,128)(2,1)S(1)} %get-tuple-element.35.hid_a, bf16[3,256,256]{2,1,0:T(8,128)(2,1)S(1)} %get-tuple-element.37.hid_b, bf16[8,256,384]{2,1,0:T(8,128)(2,1)S(1)} %get-tuple-element.29.cols_ref, bf16[3,3,256,256]{3,2,1,0:T(8,128)(2,1)S(1)} %get-tuple-element.38.w2_ref, ...), custom_call_target="tpu_custom_call" | custom-call | tf_op jit(solution)/shard_map/inside_c/pallas_call | solution.py:478
  23.0 0.0 collective-permute-done.2.got_ref
  23.0 0.2 choose.1
  23.2 2.7 %collective-permute-start.3 = (bf16[32,384]{1,0:T(8,128)(2,1)S(1)}, bf16[32,384]{1,0:T(8,128)(2,1)S(1)}, u32[]{:S(2)}, u32[]{:S(2)}) collective-permute-start(bf16[32,384]{1,0:T(8,128)(2,1)S(1)} %get-tuple-element.40.after_ref), channel_id=1, source_target_pairs={{0,8},{1,9},{2,10},{3,11},{4,12},{5,13},{6,14},{7,15},{8,0},{9,1},... | collective-permute-start | bytes 73736 | tf_op jit(solution)/shard_map/ppermute | solution.py:524
  25.9 0.0 collective-permute-done.4.outer_ref
  25.9 2.3 %border.1 = (f32[2,2048,128]{2,1,0:T(8,128)S(1)}, f32[16,256]{1,0:T(8,128)S(1)}, f32[24,384]{1,0:T(8,128)S(1)}) custom-call(bf16[8,256,384]{2,1,0:T(8,128)(2,1)S(1)} %get-tuple-element.29.cols_ref, bf16[256,640]{1,0:T(8,128)(2,1)S(1)} %collective-permute-done.4.outer_ref, bf16[272,640]{1,0:T(8,128)(2,1)S(1)} %collective-permute-done.got_ref.inner_ref, ...), custom_call_target="tpu_custom_call" | custom-call | tf_op jit(solution)/shard_map/border/pallas_call | solution.py:525
  28.1 0.0 collective-permute-done.3.got_ref
  28.1 1.7 %finish.1 = bf16[256,8,256]{2,1,0:T(8,128)(2,1)} custom-call(bf16[32,384]{1,0:T(8,128)(2,1)S(1)} %get-tuple-element.39.keep_ref, bf16[32,384]{1,0:T(8,128)(2,1)S(1)} %collective-permute-done.3.got_ref, bf16[1,16,384]{2,1,0:T(8,128)(2,1)S(1)} %get-tuple-element.27.mine_ref.top_ref, f32[2,2048,128]{2,1,0:T(8,128)S(1)} %inside_c.1.after_ref.outp_ref, ...), custom_call_target="tpu_custom_call" | custom-call | tf_op jit(solution)/shard_map/finish/pallas_call | solution.py:534
  (2 shorter events, 0.0 us)
Async XLA Ops:
  2.2 2.1 %collective-permute-start = (bf16[272,640]{1,0:T(8,128)(2,1)S(1)}, bf16[272,640]{1,0:T(8,128)(2,1)S(1)}, u32[]{:S(2)}, u32[]{:S(2)}) collective-permute-start(bf16[272,640]{1,0:T(8,128)(2,1)S(1)} %get-tuple-element.28), channel_id=1, source_target_pairs={{0,1},{1,0},{2,3},{3,2},{4,5},{5,4},{6,7},{7,6},{8,9},{9,8},{10,11... | collective-permute-start | bytes 1044488 | tf_op jit(solution)/shard_map/ppermute | solution.py:443
  4.4 21.5 %collective-permute-start.4 = (bf16[256,640]{1,0:T(8,128)(2,1)S(1)}, bf16[256,640]{1,0:T(8,128)(2,1)S(1)}, u32[]{:S(2)}, u32[]{:S(2)}) collective-permute-start(bf16[256,640]{1,0:T(8,128)(2,1)S(1)} %get-tuple-element.41), channel_id=1, source_target_pairs={{0,15},{1,2},{2,1},{3,4},{4,3},{5,6},{6,5},{7,8},{8,7},{9,10},{10,... | collective-permute-start | bytes 983048 | tf_op jit(solution)/shard_map/ppermute | solution.py:501
  10.1 6.0 %collective-permute-start.1 = (bf16[2,16,384]{2,1,0:T(8,128)(2,1)S(1)}, bf16[2,16,384]{2,1,0:T(8,128)(2,1)S(1)}, u32[]{:S(2)}, u32[]{:S(2)}) collective-permute-start(bf16[2,16,384]{2,1,0:T(8,128)(2,1)S(1)} %get-tuple-element.34.mine_ref), channel_id=1, source_target_pairs={{0,2},{1,3},{2,0},{3,1},{4,6},{5,7},{6,4},{7,5},{8,10},{9,11},{10,... | collective-permute-start | bytes 73736 | tf_op jit(solution)/shard_map/ppermute | solution.py:499
  16.0 7.0 %collective-permute-start.2 = (bf16[4,16,384]{2,1,0:T(8,128)(2,1)S(1)}, bf16[4,16,384]{2,1,0:T(8,128)(2,1)S(1)}, u32[]{:S(2)}, u32[]{:S(2)}) collective-permute-start(bf16[4,16,384]{2,1,0:T(8,128)(2,1)S(1)} %join.1.after_ref.mine_ref), channel_id=1, source_target_pairs={{0,4},{1,5},{2,6},{3,7},{4,0},{5,1},{6,2},{7,3},{8,12},{9,13},{10,... | collective-permute-start | bytes 147464 | tf_op jit(solution)/shard_map/ppermute | solution.py:499
  23.2 4.9 %collective-permute-start.3 = (bf16[32,384]{1,0:T(8,128)(2,1)S(1)}, bf16[32,384]{1,0:T(8,128)(2,1)S(1)}, u32[]{:S(2)}, u32[]{:S(2)}) collective-permute-start(bf16[32,384]{1,0:T(8,128)(2,1)S(1)} %get-tuple-element.40.after_ref), channel_id=1, source_target_pairs={{0,8},{1,9},{2,10},{3,11},{4,12},{5,13},{6,14},{7,15},{8,0},{9,1},... | collective-permute-start | bytes 73736 | tf_op jit(solution)/shard_map/ppermute | solution.py:524

commit v9 on v7

--- a/solution.py
+++ b/solution.py
@@ -138,6 +138,8 @@
                 [w1_ref[dy, dx, MAIN:, :], jnp.zeros((SLOT - chans + MAIN, hidden), BF)], axis=0
             )
             wt[(dx + 1) * SLOT : (dx + 2) * SLOT, dy * hidden : (dy + 1) * hidden] = rest
+    wt[5 * SLOT : 6 * SLOT, :] = wt[2 * SLOT : 3 * SLOT, :]
+    wt[6 * SLOT :, :] = wt[SLOT : 2 * SLOT, :]
     for at in (0, 4 * SLOT):
         wt[at : at + SLOT, :] = jnp.zeros((SLOT, 3 * hidden), BF)
 
@@ -164,7 +166,7 @@
         if columns[0] is not None or columns[1] is not None:
             parts.append(wt[SLOT : 3 * SLOT, at])
         if columns[2] is not None:
-            parts.append(wt[3 * SLOT :, at])
+            parts.append(wt[3 * SLOT : 5 * SLOT, at])
         out.append(jnp.concatenate(parts, axis=0))
     return jnp.concatenate(out, axis=1)
 
@@ -216,7 +218,11 @@
             hid_ref[i + g] = last_out(value).astype(BF)
     for i, h in enumerate(more):
         columns = [own_column(cols_ref, h + dx) for dx in range(3)]
-        part_ref[i] = summed(mm(first_taps(columns), first_weights(w1_ref, wt, columns)))
+        lhs, rhs = first_taps(columns), first_weights(w1_ref, wt, columns)
+        if h == 1:
+            lhs = jnp.concatenate([lhs[:, : 2 * MAIN], lhs[:, 2 * MAIN + LANES :]], axis=1)
+            rhs = jnp.concatenate([rhs[: 2 * MAIN], rhs[2 * MAIN + LANES :]], axis=0)
+        part_ref[i] = summed(mm(lhs, rhs))
 
 
 def inside_a(cols_ref, w1_ref, bias_ref, w2_hbm, hid_ref, last_ref, wt_ref, w2_ref, sem):
@@ -281,7 +287,7 @@
     at = edges(width)
     taken = (
         (0, slice(0, rest), (0, 1), 1),
-        (0, slice(MAIN, rest), (0,), 0),
+        (0, slice(MAIN, rest), (0,), 5),
         (1, slice(0, MAIN), (2,), 3),
         (1, slice(0, rest), (1, 2), 2),
     )
@@ -289,7 +295,11 @@
     line[2 : 2 + BEFORE] = last_a[:BEFORE]
     line[2 + BEFORE : width] = last_b[: width - 2 - BEFORE]
     for i, (side, main, dxs, slot) in enumerate(taken):
-        lhs = jnp.concatenate([hx[side, :, main], hx[side, :, rest:]], axis=1)
+        tail = hx[side, :, rest:]
+        if i == 1:
+            lanes = lax.broadcasted_iota(jnp.int32, tail.shape, 1)
+            tail = jnp.where(lanes < SLOT, cols_ref[0, :, MAIN:], tail)
+        lhs = jnp.concatenate([hx[side, :, main], tail], axis=1)
         rhs = []
         for dy in range(3):
             block = wt[slot * SLOT : (slot + 2) * SLOT, dy * hidden : (dy + 1) * hidden]
@@ -438,7 +448,7 @@
         out_shape=(
             shape((before, rows, hidden), BF),
             shape((8, hidden), F32),
-            shape((5 * SLOT, 3 * hidden), BF),
+            shape((7 * SLOT, 3 * hidden), BF),
             shape(w_second.shape, BF),
         ),
         in_specs=[vmem] * 3 + [hbm],

time: 30 us -> 30 us (level)
  no operation moved by 1% of the time
where the time goes in v9:
time: 30 us; the launch traced here: 29.9 us
  Pallas kernels  12.7 us (42%)
  starting transfers between devices  11.1 us (37%)
  waiting for transfers between devices  5.96 us (20%)
    ppermute x2, waiting for transfers between devices, local(): got = lax.ppermute(tops, 'lon', [(i, i ^ step) for i in range(n)])  5.95 us
    ppermute x1, starting transfers between devices, local(): lax.ppermute(sent, 'lon', [(i, (i + 1 if i % 2 else i - 1) % n) for i in...  5.72 us
    ppermute x1, starting transfers between devices, local(): got = lax.ppermute(give, 'lon', [(i, i ^ n // 2) for i in range(n)])  2.66 us
    pallas_call x1, Pallas kernels, stage_b(): pl.pallas_call(functools.partial(inside_b, before), out_shape=(shape((wid...  2.54 us
    pallas_call x1, Pallas kernels, stage_c(): pl.pallas_call(functools.partial(inside_c, chans), out_shape=field, in_sp...  2.24 us
    pallas_call x1, Pallas kernels, local(): pl.pallas_call(border, out_shape=(field, shape((16, hidden), F32), shape(...  2.23 us
    pallas_call x1, Pallas kernels, local(): pl.pallas_call(prepare, out_shape=(shape((rows, 2 * MAIN + LANES), BF), s...  2.19 us
    ppermute x2, starting transfers between devices, local(): got = lax.ppermute(tops, 'lon', [(i, i ^ step) for i in range(n)])  2.18 us
  transfers between devices with their start and end apart: 5, of which 1 were waited for; matrix products, arithmetic and copies ran while one was open for 0% of the time, Pallas kernels for 29%

profile of v9, /device:TPU:0, one launch (start us, length us, event | category | flops | bytes accessed | tf_op | source)
XLA Modules:
  0.0 29.9 jit_solution(10276244259676273290)
XLA Ops:
  0.0 2.2 %prepare.1 = (bf16[256,640]{1,0:T(8,128)(2,1)S(1)}, bf16[272,640]{1,0:T(8,128)(2,1)S(1)}, bf16[8,256,384]{2,1,0:T(8,128)(2,1)S(1)}, bf16[1,16,384]{2,1,0:T(8,128...) custom-call(s32[128]{0:T(128)} %fold_hbm.1, ...), custom_call_target="tpu_custom_call" | custom-call | tf_op jit(solution)/shard_map/prepare/pallas_call | solution.py:417
  2.2 0.6 %collective-permute-start = (bf16[272,640]{1,0:T(8,128)(2,1)S(1)}, bf16[272,640]{1,0:T(8,128)(2,1)S(1)}, u32[]{:S(2)}, u32[]{:S(2)}) collective-permute-start(bf16[272,640]{1,0:T(8,128)(2,1)S(1)} %get-tuple-element.28), channel_id=1, source_target_pairs={{0,1},{1,0},{2,3},{3,2},{4,5},{5,4},{6,7},{7,6},{8,9},{9,8},{10,11... | collective-permute-start | bytes 1044488 | tf_op jit(solution)/shard_map/ppermute | solution.py:443
  2.8 1.6 %inside_a.1 = (bf16[3,256,256]{2,1,0:T(8,128)(2,1)S(1)}, f32[8,256]{1,0:T(8,128)S(1)}, bf16[448,768]{1,0:T(8,128)(2,1)S(1)}, bf16[3,3,256,256]{3,2,1,0:T(8,128)(2,1)S(1)}) custom-call(bf16[8,256,384]{2,1,0:T(8,128)(2,1)S(1)} %get-tuple-element.29.cols_ref, bf16[3,3,300,256]{3,2,1,0:T(8,128)(2,1)S(1)} %get-tuple-element.30.w1_ref, ...), custom_call_target="tpu_custom_call" | custom-call | tf_op jit(solution)/shard_map/inside_a/pallas_call | solution.py:446
  4.3 0.0 collective-permute-done.got_ref.inner_ref
  4.4 5.7 %collective-permute-start.4 = (bf16[256,640]{1,0:T(8,128)(2,1)S(1)}, bf16[256,640]{1,0:T(8,128)(2,1)S(1)}, u32[]{:S(2)}, u32[]{:S(2)}) collective-permute-start(bf16[256,640]{1,0:T(8,128)(2,1)S(1)} %get-tuple-element.41), channel_id=1, source_target_pairs={{0,15},{1,2},{2,1},{3,4},{4,3},{5,6},{6,5},{7,8},{8,7},{9,10},{10,... | collective-permute-start | bytes 983048 | tf_op jit(solution)/shard_map/ppermute | solution.py:501
  10.1 0.0 collective-permute-start.1
  10.1 5.9 %collective-permute-done.1.got_ref = bf16[2,16,384]{2,1,0:T(8,128)(2,1)S(1)} collective-permute-done((bf16[2,16,384]{2,1,0:T(8,128)(2,1)S(1)}, bf16[2,16,384]{2,1,0:T(8,128)(2,1)S(1)}, u32[]{:S(2)}, u32[]{:S(2)}) %collective-permute-start.1) | collective-permute-done | bytes 24608 | tf_op jit(solution)/shard_map/ppermute | solution.py:499
  16.0 2.2 %collective-permute-start.2 = (bf16[4,16,384]{2,1,0:T(8,128)(2,1)S(1)}, bf16[4,16,384]{2,1,0:T(8,128)(2,1)S(1)}, u32[]{:S(2)}, u32[]{:S(2)}) collective-permute-start(bf16[4,16,384]{2,1,0:T(8,128)(2,1)S(1)} %join.1.after_ref.mine_ref), channel_id=1, source_target_pairs={{0,4},{1,5},{2,6},{3,7},{4,0},{5,1},{6,2},{7,3},{8,12},{9,13},{10,... | collective-permute-start | bytes 147464 | tf_op jit(solution)/shard_map/ppermute | solution.py:499
  18.2 2.5 %inside_b.1 = (bf16[3,256,256]{2,1,0:T(8,128)(2,1)S(1)}, f32[8,256]{1,0:T(8,128)S(1)}, f32[4,256,256]{2,1,0:T(8,128)S(1)}) custom-call(bf16[8,256,384]{2,1,0:T(8,128)(2,1)S(1)} %get-tuple-element.29.cols_ref, bf16[3,3,300,256]{3,2,1,0:T(8,128)(2,1)S(1)} %get-tuple-element.30.w1_ref, f32[2,256]{1,0:T(2,128)S(1)} %get-tuple-element.31.bias_ref, ...), custom_call_target="tpu_custom_call" | custom-call | tf_op jit(solution)/shard_map/inside_b/pallas_call | solution.py:462
  20.8 2.2 %inside_c.1.after_ref.outp_ref = f32[2,2048,128]{2,1,0:T(8,128)S(1)} custom-call(bf16[3,256,256]{2,1,0:T(8,128)(2,1)S(1)} %get-tuple-element.35.hid_a, bf16[3,256,256]{2,1,0:T(8,128)(2,1)S(1)} %get-tuple-element.37.hid_b, bf16[8,256,384]{2,1,0:T(8,128)(2,1)S(1)} %get-tuple-element.29.cols_ref, bf16[3,3,256,256]{3,2,1,0:T(8,128)(2,1)S(1)} %get-tuple-element.38.w2_ref, ...), custom_call_target="tpu_custom_call" | custom-call | tf_op jit(solution)/shard_map/inside_c/pallas_call | solution.py:478
  23.0 0.0 collective-permute-done.2.got_ref
  23.0 0.2 choose.1
  23.2 2.7 %collective-permute-start.3 = (bf16[32,384]{1,0:T(8,128)(2,1)S(1)}, bf16[32,384]{1,0:T(8,128)(2,1)S(1)}, u32[]{:S(2)}, u32[]{:S(2)}) collective-permute-start(bf16[32,384]{1,0:T(8,128)(2,1)S(1)} %get-tuple-element.40.after_ref), channel_id=1, source_target_pairs={{0,8},{1,9},{2,10},{3,11},{4,12},{5,13},{6,14},{7,15},{8,0},{9,1},... | collective-permute-start | bytes 73736 | tf_op jit(solution)/shard_map/ppermute | solution.py:524
  25.9 0.0 collective-permute-done.4.outer_ref
  25.9 2.2 %border.1 = (f32[2,2048,128]{2,1,0:T(8,128)S(1)}, f32[16,256]{1,0:T(8,128)S(1)}, f32[24,384]{1,0:T(8,128)S(1)}) custom-call(bf16[8,256,384]{2,1,0:T(8,128)(2,1)S(1)} %get-tuple-element.29.cols_ref, bf16[256,640]{1,0:T(8,128)(2,1)S(1)} %collective-permute-done.4.outer_ref, bf16[272,640]{1,0:T(8,128)(2,1)S(1)} %collective-permute-done.got_ref.inner_ref, ...), custom_call_target="tpu_custom_call" | custom-call | tf_op jit(solution)/shard_map/border/pallas_call | solution.py:525
  28.1 0.0 collective-permute-done.3.got_ref
  28.1 1.7 %finish.1 = bf16[256,8,256]{2,1,0:T(8,128)(2,1)} custom-call(bf16[32,384]{1,0:T(8,128)(2,1)S(1)} %get-tuple-element.39.keep_ref, bf16[32,384]{1,0:T(8,128)(2,1)S(1)} %collective-permute-done.3.got_ref, bf16[1,16,384]{2,1,0:T(8,128)(2,1)S(1)} %get-tuple-element.27.mine_ref.top_ref, f32[2,2048,128]{2,1,0:T(8,128)S(1)} %inside_c.1.after_ref.outp_ref, ...), custom_call_target="tpu_custom_call" | custom-call | tf_op jit(solution)/shard_map/finish/pallas_call | solution.py:534
  (2 shorter events, 0.0 us)
Async XLA Ops:
  2.2 2.1 %collective-permute-start = (bf16[272,640]{1,0:T(8,128)(2,1)S(1)}, bf16[272,640]{1,0:T(8,128)(2,1)S(1)}, u32[]{:S(2)}, u32[]{:S(2)}) collective-permute-start(bf16[272,640]{1,0:T(8,128)(2,1)S(1)} %get-tuple-element.28), channel_id=1, source_target_pairs={{0,1},{1,0},{2,3},{3,2},{4,5},{5,4},{6,7},{7,6},{8,9},{9,8},{10,11... | collective-permute-start | bytes 1044488 | tf_op jit(solution)/shard_map/ppermute | solution.py:443
  4.4 21.5 %collective-permute-start.4 = (bf16[256,640]{1,0:T(8,128)(2,1)S(1)}, bf16[256,640]{1,0:T(8,128)(2,1)S(1)}, u32[]{:S(2)}, u32[]{:S(2)}) collective-permute-start(bf16[256,640]{1,0:T(8,128)(2,1)S(1)} %get-tuple-element.41), channel_id=1, source_target_pairs={{0,15},{1,2},{2,1},{3,4},{4,3},{5,6},{6,5},{7,8},{8,7},{9,10},{10,... | collective-permute-start | bytes 983048 | tf_op jit(solution)/shard_map/ppermute | solution.py:501
  10.1 6.0 %collective-permute-start.1 = (bf16[2,16,384]{2,1,0:T(8,128)(2,1)S(1)}, bf16[2,16,384]{2,1,0:T(8,128)(2,1)S(1)}, u32[]{:S(2)}, u32[]{:S(2)}) collective-permute-start(bf16[2,16,384]{2,1,0:T(8,128)(2,1)S(1)} %get-tuple-element.34.mine_ref), channel_id=1, source_target_pairs={{0,2},{1,3},{2,0},{3,1},{4,6},{5,7},{6,4},{7,5},{8,10},{9,11},{10,... | collective-permute-start | bytes 73736 | tf_op jit(solution)/shard_map/ppermute | solution.py:499
  16.0 7.0 %collective-permute-start.2 = (bf16[4,16,384]{2,1,0:T(8,128)(2,1)S(1)}, bf16[4,16,384]{2,1,0:T(8,128)(2,1)S(1)}, u32[]{:S(2)}, u32[]{:S(2)}) collective-permute-start(bf16[4,16,384]{2,1,0:T(8,128)(2,1)S(1)} %join.1.after_ref.mine_ref), channel_id=1, source_target_pairs={{0,4},{1,5},{2,6},{3,7},{4,0},{5,1},{6,2},{7,3},{8,12},{9,13},{10,... | collective-permute-start | bytes 147464 | tf_op jit(solution)/shard_map/ppermute | solution.py:499
  23.2 4.9 %collective-permute-start.3 = (bf16[32,384]{1,0:T(8,128)(2,1)S(1)}, bf16[32,384]{1,0:T(8,128)(2,1)S(1)}, u32[]{:S(2)}, u32[]{:S(2)}) collective-permute-start(bf16[32,384]{1,0:T(8,128)(2,1)S(1)} %get-tuple-element.40.after_ref), channel_id=1, source_target_pairs={{0,8},{1,9},{2,10},{3,11},{4,12},{5,13},{6,14},{7,15},{8,0},{9,1},... | collective-permute-start | bytes 73736 | tf_op jit(solution)/shard_map/ppermute | solution.py:524
